TPU v7x, 32 devices: a whole 2x2x4 slice. The times are simulated.
32 devices in a mesh: dp: 16 (over z, x, core), mp: 2 (over y).
Axes of the slice: x: 2, y: 2, z: 4, core: 2. Of those that a mesh axis runs over, the one named last changes fastest.
Arguments:
- hidden: bfloat16 [49152, 768], P('dp'), may hold values from -6 to 6
- doc_lengths: int32 [48, 8], P('dp'), may hold values from 1 to 512, 1024 in all within a row
- query_weight: bfloat16 [768, 384], P('dp', 'mp'), may hold values from -0.21875 to 0.21875
- key_weight: bfloat16 [768, 384], P('dp', 'mp'), may hold values from -0.21875 to 0.21875
- value_weight: bfloat16 [768, 384], P('dp', 'mp'), may hold values from -0.21875 to 0.21875
- query_bias: float32 [384], P('mp'), may hold values from -3 to 3
- value_bias: float32 [384], P('mp'), may hold values from -2 to 2
- depth_weight: bfloat16 [9, 768], P(None, 'dp'), may hold values from -2 to 2
- point_weight: bfloat16 [768, 384], P('dp', 'mp'), may hold values from -0.21875 to 0.21875
- point_bias: float32 [384], P('mp'), may hold values from -2 to 2
- kernel_weight: bfloat16 [384, 54], P('mp'), may hold values from -0.3125 to 0.3125
- kernel_bias: float32 [54], replicated, may hold values from -3 to 3
- conv_weight: bfloat16 [768, 384], P('dp', 'mp'), may hold values from -0.21875 to 0.21875
- conv_bias: float32 [384], P('mp'), may hold values from -2 to 2
- out_weight: bfloat16 [2, 384, 768], P(None, 'mp', 'dp'), may hold values from -0.625 to 0.625
- out_bias: float32 [768], replicated, may hold values from -2 to 2
- norm1_gain: float32 [768], replicated, may hold values from 0.5 to 1.5
- norm1_bias: float32 [768], replicated, may hold values from -2 to 2
- ffn_in_weight: bfloat16 [2, 384, 1536], P('mp', None, 'dp'), may hold values from -0.3125 to 0.3125
- ffn_in_bias: float32 [2, 1536], P('mp'), may hold values from -3 to 3
- ffn_out_weight: bfloat16 [2, 1536, 384], P('mp', 'dp'), may hold values from -0.15625 to 0.15625
- ffn_out_bias: float32 [768], P('mp'), may hold values from -2 to 2
- norm2_gain: float32 [768], P('mp'), may hold values from 0.5 to 1.5
- norm2_bias: float32 [768], P('mp'), may hold values from -2 to 2
- out_grad: bfloat16 [49152, 768], P('dp', 'mp'), may hold values from -6 to 6
Outputs:
- output: bfloat16 [49152, 768], P('dp', 'mp')
- input_grad: float32 [49152, 768], P('dp', 'mp')
- query_weight_grad: float32 [768, 384], P('dp', 'mp')
- key_weight_grad: float32 [768, 384], P('dp', 'mp')
- value_weight_grad: float32 [768, 384], P('dp', 'mp')
- query_bias_grad: float32 [384], P('mp')
- value_bias_grad: float32 [384], P('mp')
- depth_weight_grad: float32 [9, 768], P(None, 'dp')
- point_weight_grad: float32 [768, 384], P('dp', 'mp')
- point_bias_grad: float32 [384], P('mp')
- kernel_weight_grad: float32 [384, 54], P('mp')
- kernel_bias_grad: float32 [54], replicated
- conv_weight_grad: float32 [768, 384], P('dp', 'mp')
- conv_bias_grad: float32 [384], P('mp')
- out_weight_grad: float32 [2, 384, 768], P(None, 'mp', 'dp')
- out_bias_grad: float32 [768], replicated
- norm1_gain_grad: float32 [768], replicated
- norm1_bias_grad: float32 [768], replicated
- ffn_in_weight_grad: float32 [2, 384, 1536], P('mp', None, 'dp')
- ffn_in_bias_grad: float32 [2, 1536], P('mp')
- ffn_out_weight_grad: float32 [2, 1536, 384], P('mp', 'dp')
- ffn_out_bias_grad: float32 [768], P('mp')
- norm2_gain_grad: float32 [768], P('mp')
- norm2_bias_grad: float32 [768], P('mp')
Inputs may be any that keep to these rules, and one draw needn't show every extreme that they name: `doc_lengths`: row s lists, in order, the lengths of the 8 documents packed into sequence s; every row sums to 1024 and its longest document has exactly 512 tokens.
All inputs are finite; a program needn't handle non-finite values.
Results may differ from a plain program's by a relative error of at most 0.014.
Values may be sent and summed in bfloat16 or wider, within the bound.
A program may use at most 320 MiB of HBM per device.

v0:
```python
import jax
import jax.numpy as jnp
from jax import lax
from jax.sharding import PartitionSpec as P

HEAD_DIM = 64
KERNEL = 9


EPSILON = 1e-06
MASK_FILL = -1e30
INV_ROOT2 = 0.7071067811865476
INV_ROOT_TWO_PI = 0.3989422804014327


def matmul(left, right):
    return jnp.dot(left, right, preferred_element_type=jnp.float32)


def matmul_left(left, right):
    return lax.dot_general(
        left, right, (((0,), (0,)), ((), ())), preferred_element_type=jnp.float32
    )


def matmul_right(left, right):
    return lax.dot_general(
        left, right, (((1,), (1,)), ((), ())), preferred_element_type=jnp.float32
    )


def shifted(tensor, offset, half_width):
    filler = jnp.zeros((half_width,) + tensor.shape[1:], tensor.dtype)
    padded = jnp.concatenate([filler, tensor, filler], axis=0)
    return padded[half_width + offset : half_width + offset + tensor.shape[0]]


def same_segment(segment, offset, half_width):
    filler = jnp.full((half_width,), -1, dtype=jnp.int32)
    padded = jnp.concatenate([filler, segment, filler])
    return padded[half_width + offset : half_width + offset + segment.shape[0]] == segment


def segment_ids(lengths_row, seq_rows):
    doc_ends = jnp.cumsum(lengths_row)
    positions = jnp.arange(seq_rows, dtype=jnp.int32)
    return jnp.sum((positions[:, None] >= doc_ends[None, :]).astype(jnp.int32), axis=1)


def tap_mask_list(segment):
    half_width = KERNEL // 2
    return [
        same_segment(segment, tap_index - half_width, half_width).astype(jnp.float32)[:, None]
        for tap_index in range(KERNEL)
    ]


def gelu(tensor):
    return 0.5 * tensor * (1.0 + lax.erf(tensor * INV_ROOT2))


def gelu_slope(tensor):
    normal_cdf = 0.5 * (1.0 + lax.erf(tensor * INV_ROOT2))
    return normal_cdf + tensor * jnp.exp(-0.5 * tensor * tensor) * INV_ROOT_TWO_PI


def gather_layer(w_query, w_key, w_value, w_point, w_conv, w_depth, w_out, w_inner, w_outer):
    return (
        lax.all_gather(w_query, "dp", axis=0, tiled=True),
        lax.all_gather(w_key, "dp", axis=0, tiled=True),
        lax.all_gather(w_value, "dp", axis=0, tiled=True),
        lax.all_gather(w_point, "dp", axis=0, tiled=True),
        lax.all_gather(w_conv, "dp", axis=0, tiled=True),
        lax.all_gather(w_depth, "dp", axis=1, tiled=True),
        lax.all_gather(w_out, "dp", axis=2, tiled=True),
        lax.all_gather(w_inner, "dp", axis=2, tiled=True),
        lax.all_gather(w_outer, "dp", axis=1, tiled=True),
    )


def gather_again(w_query, w_key, w_value, w_point, w_conv, w_depth, w_out, w_inner, w_outer):
    return (
        lax.all_gather(w_query, "dp", axis=0, tiled=True),
        lax.all_gather(w_key, "dp", axis=0, tiled=True),
        lax.all_gather(w_value, "dp", axis=0, tiled=True),
        lax.all_gather(w_point, "dp", axis=0, tiled=True),
        lax.all_gather(w_conv, "dp", axis=0, tiled=True),
        lax.all_gather(w_depth, "dp", axis=1, tiled=True),
        lax.all_gather(w_out, "dp", axis=2, tiled=True),
        lax.all_gather(w_inner, "dp", axis=2, tiled=True),
        lax.all_gather(w_outer, "dp", axis=1, tiled=True),
    )


def forward_pass(rows_in, segment, full_weights, small_params):
    w_query, w_key, w_value, w_point, w_conv, w_depth, w_out, w_inner, w_outer = full_weights
    (
        b_query,
        b_value,
        b_point,
        w_kernel,
        b_kernel,
        b_conv,
        b_out,
        first_norm_gain,
        first_norm_bias,
        b_inner,
        b_outer,
        second_norm_gain,
        second_norm_bias,
    ) = small_params
    seq_rows, hidden_width = rows_in.shape
    local_width = w_query.shape[1]
    local_heads = local_width // HEAD_DIM
    group_width = b_outer.shape[0]
    half_width = KERNEL // 2
    scale_factor = HEAD_DIM ** (-0.5)
    my_index = lax.axis_index("mp")
    queries = (matmul(rows_in, w_query) + b_query).astype(jnp.bfloat16)
    keys_all = matmul(rows_in, w_key).astype(jnp.bfloat16)
    values_all = (matmul(rows_in, w_value) + b_value).astype(jnp.bfloat16)
    tap_masks = tap_mask_list(segment)
    depthwise = jnp.zeros((seq_rows, hidden_width), jnp.float32)
    for tap_index in range(KERNEL):
        moved_rows = shifted(rows_in, tap_index - half_width, half_width).astype(jnp.float32)
        depthwise = (
            depthwise + w_depth[tap_index].astype(jnp.float32) * moved_rows * tap_masks[tap_index]
        )
    depth_low = depthwise.astype(jnp.bfloat16)
    key_conv = matmul(depth_low, w_point) + b_point
    conv_attn = (key_conv * queries.astype(jnp.float32)).astype(jnp.bfloat16)
    logits = lax.psum(matmul(conv_attn, w_kernel), "mp") + b_kernel
    own_logits = lax.dynamic_slice_in_dim(
        logits, my_index * (local_heads * KERNEL), local_heads * KERNEL, 1
    )
    kernel_probs = jax.nn.softmax(own_logits.reshape(seq_rows, local_heads, KERNEL), axis=-1)
    conv_values = (matmul(rows_in, w_conv) + b_conv).reshape(seq_rows, local_heads, HEAD_DIM)
    conv_context = jnp.zeros((seq_rows, local_heads, HEAD_DIM), jnp.float32)
    for tap_index in range(KERNEL):
        weights_now = kernel_probs[:, :, tap_index] * tap_masks[tap_index]
        conv_context = conv_context + weights_now[:, :, None] * shifted(
            conv_values, tap_index - half_width, half_width
        )
    conv_low = conv_context.reshape(seq_rows, local_width).astype(jnp.bfloat16)
    query_heads = queries.reshape(seq_rows, local_heads, HEAD_DIM)
    key_heads = keys_all.reshape(seq_rows, local_heads, HEAD_DIM)
    value_heads = values_all.reshape(seq_rows, local_heads, HEAD_DIM)
    block_rows = min(512, seq_rows)
    contexts = []
    log_sums = []
    for row_start in range(0, seq_rows, block_rows):
        query_block = query_heads[row_start : row_start + block_rows]
        scores = (
            jnp.einsum("qhd,khd->hqk", query_block, key_heads, preferred_element_type=jnp.float32)
            * scale_factor
        )
        allowed = segment[row_start : row_start + block_rows][:, None] == segment[None, :]
        scores = jnp.where(allowed[None], scores, MASK_FILL)
        top_score = jnp.max(scores, axis=-1, keepdims=True)
        exponent = jnp.exp(scores - top_score)
        row_total = jnp.sum(exponent, axis=-1, keepdims=True)
        probs_low = (exponent / row_total).astype(jnp.bfloat16)
        contexts.append(
            jnp.einsum("hqk,khd->qhd", probs_low, value_heads, preferred_element_type=jnp.float32)
        )
        log_sums.append(top_score[:, :, 0] + jnp.log(row_total[:, :, 0]))
    context_low = jnp.concatenate(contexts, 0).reshape(seq_rows, local_width).astype(jnp.bfloat16)
    log_total = jnp.concatenate(log_sums, 1)
    partial_out = matmul(context_low, w_out[0]) + matmul(conv_low, w_out[1])
    branch = lax.psum(partial_out, "mp") + b_out
    residual = rows_in.astype(jnp.float32) + branch
    mean_full = jnp.mean(residual, axis=1, keepdims=True)
    centered_input = residual - mean_full
    first_inverse_deviation = lax.rsqrt(
        jnp.mean(centered_input * centered_input, axis=1, keepdims=True) + EPSILON
    )
    first_standardized = centered_input * first_inverse_deviation
    normalized_rows = first_standardized * first_norm_gain + first_norm_bias
    normed_here = lax.dynamic_slice_in_dim(normalized_rows, my_index * group_width, group_width, 1)
    normed_low = normed_here.astype(jnp.bfloat16)
    inner_pre = matmul(normed_low, w_inner[0]) + b_inner[0]
    activated = gelu(inner_pre).astype(jnp.bfloat16)
    summed_residual = normed_here + (matmul(activated, w_outer[0]) + b_outer)
    row_sums = lax.psum(
        (jnp.sum(summed_residual, axis=1), jnp.sum(summed_residual * summed_residual, axis=1)), "mp"
    )
    second_norm_mean = row_sums[0] / hidden_width
    second_inverse_deviation = lax.rsqrt(
        row_sums[1] / hidden_width - second_norm_mean * second_norm_mean + EPSILON
    )
    second_standardized = (summed_residual - second_norm_mean[:, None]) * second_inverse_deviation[
        :, None
    ]
    layer_output = (second_standardized * second_norm_gain + second_norm_bias).astype(jnp.bfloat16)
    kept_state = (
        queries,
        keys_all,
        values_all,
        depth_low,
        key_conv,
        conv_attn,
        kernel_probs,
        conv_values,
        conv_low,
        context_low,
        log_total,
        first_standardized,
        first_inverse_deviation,
        normed_low,
        inner_pre,
        activated,
        second_standardized,
        second_inverse_deviation,
    )
    return (layer_output, kept_state)


def backward_pass(rows_in, segment, full_weights, small_params, kept_state, grad_rows):
    w_query, w_key, w_value, w_point, w_conv, w_depth, w_out, w_inner, w_outer = full_weights
    (
        b_query,
        b_value,
        b_point,
        w_kernel,
        b_kernel,
        b_conv,
        b_out,
        first_norm_gain,
        first_norm_bias,
        b_inner,
        b_outer,
        second_norm_gain,
        second_norm_bias,
    ) = small_params
    (
        queries,
        keys_all,
        values_all,
        depth_low,
        key_conv,
        conv_attn,
        kernel_probs,
        conv_values,
        conv_low,
        context_low,
        log_total,
        first_standardized,
        first_inverse_deviation,
        normed_low,
        inner_pre,
        activated,
        second_standardized,
        second_inverse_deviation,
    ) = kept_state
    seq_rows, hidden_width = rows_in.shape
    local_width = w_query.shape[1]
    local_heads = local_width // HEAD_DIM
    group_width = b_outer.shape[0]
    half_width = KERNEL // 2
    scale_factor = HEAD_DIM ** (-0.5)
    my_index = lax.axis_index("mp")
    tap_masks = tap_mask_list(segment)
    output_gradient = grad_rows.astype(jnp.float32)
    second_scaled_rows = output_gradient * second_norm_gain
    second_gain_gradient = jnp.sum(output_gradient * second_standardized, axis=0)
    grad_shift_two = jnp.sum(output_gradient, axis=0)
    row_partials = lax.psum(
        (
            jnp.sum(second_scaled_rows, axis=1),
            jnp.sum(second_scaled_rows * second_standardized, axis=1),
        ),
        "mp",
    )
    grad_summed = second_inverse_deviation[:, None] * (
        second_scaled_rows
        - row_partials[0][:, None] / hidden_width
        - second_standardized * (row_partials[1][:, None] / hidden_width)
    )
    outer_low = grad_summed.astype(jnp.bfloat16)
    grad_b_outer = jnp.sum(outer_low, axis=0, dtype=jnp.float32)
    grad_w_outer = matmul_left(activated, outer_low)
    grad_act = matmul_right(outer_low, w_outer[0])
    inner_low = (grad_act * gelu_slope(inner_pre)).astype(jnp.bfloat16)
    grad_b_inner = jnp.sum(inner_low, axis=0, dtype=jnp.float32)
    grad_w_inner = matmul_left(normed_low, inner_low)
    grad_normed_here = grad_summed + matmul_right(inner_low, w_inner[0])
    normalized_gradient = lax.all_gather(grad_normed_here, "mp", axis=1, tiled=True)
    first_scaled_rows = normalized_gradient * first_norm_gain
    first_gain_gradient = jnp.sum(normalized_gradient * first_standardized, axis=0)
    grad_shift_one = jnp.sum(normalized_gradient, axis=0)
    grad_residual = first_inverse_deviation * (
        first_scaled_rows
        - jnp.mean(first_scaled_rows, axis=1, keepdims=True)
        - first_standardized
        * jnp.mean(first_scaled_rows * first_standardized, axis=1, keepdims=True)
    )
    branch_low = grad_residual.astype(jnp.bfloat16)
    residual_here = lax.dynamic_slice_in_dim(grad_residual, my_index * group_width, group_width, 1)
    grad_b_out = jnp.sum(branch_low, axis=0, dtype=jnp.float32)
    grad_w_out = jnp.stack(
        [matmul_left(context_low, branch_low), matmul_left(conv_low, branch_low)]
    )
    grad_context = (
        matmul_right(branch_low, w_out[0])
        .astype(jnp.bfloat16)
        .reshape(seq_rows, local_heads, HEAD_DIM)
    )
    grad_conv = (
        matmul_right(branch_low, w_out[1])
        .astype(jnp.bfloat16)
        .reshape(seq_rows, local_heads, HEAD_DIM)
    )
    tap_grads = []
    grad_values_conv = jnp.zeros((seq_rows, local_heads, HEAD_DIM), jnp.float32)
    for tap_index in range(KERNEL):
        offset_now = tap_index - half_width
        mask_now = tap_masks[tap_index]
        tap_grads.append(
            mask_now * jnp.sum(grad_conv * shifted(conv_values, offset_now, half_width), axis=2)
        )
        weights_now = kernel_probs[:, :, tap_index] * mask_now
        grad_values_conv = grad_values_conv + shifted(
            weights_now[:, :, None] * grad_conv, -offset_now, half_width
        )
    grad_taps = jnp.stack(tap_grads, axis=2)
    grad_logits = kernel_probs * (
        grad_taps - jnp.sum(kernel_probs * grad_taps, axis=2, keepdims=True)
    )
    logits_low = grad_logits.reshape(seq_rows, local_heads * KERNEL).astype(jnp.bfloat16)
    logits_all = lax.all_gather(logits_low, "mp", axis=1, tiled=True)
    grad_b_kernel = jnp.sum(logits_all, axis=0, dtype=jnp.float32)
    grad_w_kernel = matmul_left(conv_attn, logits_all)
    attn_low = matmul_right(logits_all, w_kernel).astype(jnp.bfloat16)
    attn_wide = attn_low.astype(jnp.float32)
    key_low = (attn_wide * queries.astype(jnp.float32)).astype(jnp.bfloat16)
    grad_query_conv = attn_wide * key_conv
    grad_b_point = jnp.sum(key_low, axis=0, dtype=jnp.float32)
    grad_w_point = matmul_left(depth_low, key_low)
    grad_depthwise = matmul_right(key_low, w_point)
    depth_rows = []
    grad_rows_part = jnp.zeros((seq_rows, hidden_width), jnp.float32)
    for tap_index in range(KERNEL):
        offset_now = tap_index - half_width
        masked_grad = grad_depthwise * tap_masks[tap_index]
        moved_rows = shifted(rows_in, offset_now, half_width).astype(jnp.float32)
        depth_rows.append(jnp.sum(masked_grad * moved_rows, axis=0))
        grad_rows_part = grad_rows_part + shifted(
            masked_grad * w_depth[tap_index].astype(jnp.float32), -offset_now, half_width
        )
    grad_w_depth = jnp.stack(depth_rows, axis=0)
    values_conv_low = grad_values_conv.reshape(seq_rows, local_width).astype(jnp.bfloat16)
    grad_b_conv = jnp.sum(values_conv_low, axis=0, dtype=jnp.float32)
    grad_w_conv = matmul_left(rows_in, values_conv_low)
    grad_rows_part = grad_rows_part + matmul_right(values_conv_low, w_conv)
    query_heads = queries.reshape(seq_rows, local_heads, HEAD_DIM)
    key_heads = keys_all.reshape(seq_rows, local_heads, HEAD_DIM)
    value_heads = values_all.reshape(seq_rows, local_heads, HEAD_DIM)
    block_rows = min(512, seq_rows)
    query_parts = []
    grad_keys = jnp.zeros((seq_rows, local_heads, HEAD_DIM), jnp.float32)
    grad_vals = jnp.zeros((seq_rows, local_heads, HEAD_DIM), jnp.float32)
    for row_start in range(0, seq_rows, block_rows):
        query_block = query_heads[row_start : row_start + block_rows]
        scores = (
            jnp.einsum("qhd,khd->hqk", query_block, key_heads, preferred_element_type=jnp.float32)
            * scale_factor
        )
        allowed = segment[row_start : row_start + block_rows][:, None] == segment[None, :]
        scores = jnp.where(allowed[None], scores, MASK_FILL)
        probs = jnp.exp(scores - log_total[:, row_start : row_start + block_rows][:, :, None])
        probs_low = probs.astype(jnp.bfloat16)
        context_block = grad_context[row_start : row_start + block_rows]
        grad_probs = jnp.einsum(
            "qhd,khd->hqk", context_block, value_heads, preferred_element_type=jnp.float32
        )
        grad_scores = probs * (grad_probs - jnp.sum(probs * grad_probs, axis=2, keepdims=True))
        scores_low = grad_scores.astype(jnp.bfloat16)
        query_parts.append(
            jnp.einsum("hqk,khd->qhd", scores_low, key_heads, preferred_element_type=jnp.float32)
            * scale_factor
        )
        grad_keys = (
            grad_keys
            + jnp.einsum(
                "hqk,qhd->khd", scores_low, query_block, preferred_element_type=jnp.float32
            )
            * scale_factor
        )
        grad_vals = grad_vals + jnp.einsum(
            "hqk,qhd->khd", probs_low, context_block, preferred_element_type=jnp.float32
        )
    grad_queries = (
        jnp.concatenate(query_parts, 0).reshape(seq_rows, local_width) + grad_query_conv
    ).astype(jnp.bfloat16)
    grad_b_query = jnp.sum(grad_queries, axis=0, dtype=jnp.float32)
    grad_w_query = matmul_left(rows_in, grad_queries)
    grad_rows_part = grad_rows_part + matmul_right(grad_queries, w_query)
    keys_low = grad_keys.reshape(seq_rows, local_width).astype(jnp.bfloat16)
    grad_w_key = matmul_left(rows_in, keys_low)
    grad_rows_part = grad_rows_part + matmul_right(keys_low, w_key)
    vals_low = grad_vals.reshape(seq_rows, local_width).astype(jnp.bfloat16)
    grad_b_value = jnp.sum(vals_low, axis=0, dtype=jnp.float32)
    grad_w_value = matmul_left(rows_in, vals_low)
    grad_rows_part = grad_rows_part + matmul_right(vals_low, w_value)
    grad_input = (
        lax.psum_scatter(
            grad_rows_part.astype(jnp.bfloat16), "mp", scatter_dimension=1, tiled=True
        ).astype(jnp.float32)
        + residual_here
    )
    big_terms = (
        grad_w_query,
        grad_w_key,
        grad_w_value,
        grad_w_point,
        grad_w_conv,
        grad_w_depth,
        grad_w_out,
        grad_w_inner[None],
        grad_w_outer[None],
    )
    small_terms = (
        grad_b_query,
        grad_b_value,
        grad_b_point,
        grad_w_kernel,
        grad_b_kernel,
        grad_b_conv,
        grad_b_out,
        first_gain_gradient,
        grad_shift_one,
        grad_b_inner[None],
        grad_b_outer,
        second_gain_gradient,
        grad_shift_two,
    )
    return (grad_input, big_terms, small_terms)


def on_device(
    hidden,
    doc_lengths,
    query_weight,
    key_weight,
    value_weight,
    query_bias,
    value_bias,
    depth_weight,
    point_weight,
    point_bias,
    kernel_weight,
    kernel_bias,
    conv_weight,
    conv_bias,
    out_weight,
    out_bias,
    norm1_gain,
    norm1_bias,
    ffn_in_weight,
    ffn_in_bias,
    ffn_out_weight,
    ffn_out_bias,
    norm2_gain,
    norm2_bias,
    out_grad,
):
    small_params = (
        query_bias,
        value_bias,
        point_bias,
        kernel_weight,
        kernel_bias,
        conv_bias,
        out_bias,
        norm1_gain,
        norm1_bias,
        ffn_in_bias,
        ffn_out_bias,
        norm2_gain,
        norm2_bias,
    )
    micro_count = doc_lengths.shape[0]
    seq_rows = hidden.shape[0] // micro_count
    big_totals = None
    small_totals = None
    outputs = []
    input_grads = []
    for micro_index in range(micro_count):
        rows_in = hidden[micro_index * seq_rows : (micro_index + 1) * seq_rows]
        grad_rows = out_grad[micro_index * seq_rows : (micro_index + 1) * seq_rows]
        segment = segment_ids(doc_lengths[micro_index], seq_rows)
        full_weights = gather_layer(
            query_weight,
            key_weight,
            value_weight,
            point_weight,
            conv_weight,
            depth_weight,
            out_weight,
            ffn_in_weight,
            ffn_out_weight,
        )
        layer_output, kept_state = forward_pass(rows_in, segment, full_weights, small_params)
        full_weights = gather_again(
            query_weight,
            key_weight,
            value_weight,
            point_weight,
            conv_weight,
            depth_weight,
            out_weight,
            ffn_in_weight,
            ffn_out_weight,
        )
        grad_input, big_terms, small_terms = backward_pass(
            rows_in, segment, full_weights, small_params, kept_state, grad_rows
        )
        outputs.append(layer_output)
        input_grads.append(grad_input)
        if big_totals is None:
            big_totals = big_terms
            small_totals = small_terms
        else:
            big_totals = jax.tree.map(jnp.add, big_totals, big_terms)
            small_totals = jax.tree.map(jnp.add, small_totals, small_terms)
    big_sums = (
        lax.psum_scatter(big_totals[0], "dp", scatter_dimension=0, tiled=True),
        lax.psum_scatter(big_totals[1], "dp", scatter_dimension=0, tiled=True),
        lax.psum_scatter(big_totals[2], "dp", scatter_dimension=0, tiled=True),
        lax.psum_scatter(big_totals[3], "dp", scatter_dimension=0, tiled=True),
        lax.psum_scatter(big_totals[4], "dp", scatter_dimension=0, tiled=True),
        lax.psum_scatter(big_totals[5], "dp", scatter_dimension=1, tiled=True),
        lax.psum_scatter(big_totals[6], "dp", scatter_dimension=2, tiled=True),
        lax.psum_scatter(big_totals[7], "dp", scatter_dimension=2, tiled=True),
        lax.psum_scatter(big_totals[8], "dp", scatter_dimension=1, tiled=True),
    )
    depth_total = lax.psum(big_sums[5], "mp")
    small_sums = lax.psum(
        (
            small_totals[0],
            small_totals[1],
            small_totals[2],
            small_totals[3],
            small_totals[4],
            small_totals[5],
            small_totals[6],
            small_totals[7],
            small_totals[8],
            small_totals[9],
            small_totals[10],
            small_totals[11],
            small_totals[12],
        ),
        "dp",
    )
    return (
        jnp.concatenate(outputs, 0),
        jnp.concatenate(input_grads, 0),
        big_sums[0],
        big_sums[1],
        big_sums[2],
        small_sums[0],
        small_sums[1],
        depth_total,
        big_sums[3],
        small_sums[2],
        small_sums[3],
        small_sums[4],
        big_sums[4],
        small_sums[5],
        big_sums[6],
        small_sums[6],
        small_sums[7],
        small_sums[8],
        big_sums[7],
        small_sums[9],
        big_sums[8],
        small_sums[10],
        small_sums[11],
        small_sums[12],
    )


def solution(mesh):
    in_specs = (
        P("dp", None),
        P("dp", None),
        P("dp", "mp"),
        P("dp", "mp"),
        P("dp", "mp"),
        P("mp"),
        P("mp"),
        P(None, "dp"),
        P("dp", "mp"),
        P("mp"),
        P("mp", None),
        P(),
        P("dp", "mp"),
        P("mp"),
        P(None, "mp", "dp"),
        P(),
        P(),
        P(),
        P("mp", None, "dp"),
        P("mp", None),
        P("mp", "dp", None),
        P("mp"),
        P("mp"),
        P("mp"),
        P("dp", "mp"),
    )
    out_specs = (
        P("dp", "mp"),
        P("dp", "mp"),
        P("dp", "mp"),
        P("dp", "mp"),
        P("dp", "mp"),
        P("mp"),
        P("mp"),
        P(None, "dp"),
        P("dp", "mp"),
        P("mp"),
        P("mp", None),
        P(),
        P("dp", "mp"),
        P("mp"),
        P(None, "mp", "dp"),
        P(),
        P(),
        P(),
        P("mp", None, "dp"),
        P("mp", None),
        P("mp", "dp", None),
        P("mp"),
        P("mp"),
        P("mp"),
    )
    return jax.shard_map(
        on_device, mesh=mesh, in_specs=in_specs, out_specs=out_specs, check_vma=False
    )
```

profile of v0, /device:TPU:8, one launch (start us, length us, event | category | flops | bytes accessed | tf_op | source)
XLA Modules:
  0.0 1534.1 jit_solution(6422417629129813311)
XLA Ops:
  8.1 20.3 %all_gather.31 = bf16[768,192]{1,0:T(8,128)(2,1)S(1)} all-gather(bf16[48,192]{1,0:T(8,128)(2,1)} %param.27), channel_id=1, replica_groups=mesh['dp'=16,'mp'=2] {'dp'}, dimensions={0}, use_global_device_ids=true | all-gather | bytes 313344 | tf_op jit(solution)/shard_map/all_gather | solution.py:69
  40.3 17.6 %all-gather = bf16[16,48,9]{1,2,0:T(8,128)(2,1)S(1)} all-gather(bf16[1,48,9]{1,2,0:T(8,128)(2,1)S(1)} %bitcast.706), channel_id=1, replica_groups=mesh['dp'=16,'mp'=2] {'dp'}, dimensions={0}, use_global_device_ids=true | all-gather | bytes 14688 | tf_op jit(solution)/shard_map/all_gather | solution.py:74
  58.2 20.0 %all_gather.35 = bf16[768,192]{1,0:T(8,128)(2,1)S(1)} all-gather(bf16[48,192]{1,0:T(8,128)(2,1)S(1)} %copy-done.293), channel_id=1, replica_groups=mesh['dp'=16,'mp'=2] {'dp'}, dimensions={0}, use_global_device_ids=true | all-gather | bytes 313344 | tf_op jit(solution)/shard_map/all_gather | solution.py:72
  80.0 6.0 fusion.128
  86.8 6.2 fusion.78
  93.9 6.3 fusion.103
  104.3 18.5 %all_gather.30 = bf16[768,192]{1,0:T(8,128)(2,1)S(1)} all-gather(bf16[48,192]{1,0:T(8,128)(2,1)S(1)} %copy-done.294), channel_id=1, replica_groups=mesh['dp'=16,'mp'=2] {'dp'}, dimensions={0}, use_global_device_ids=true | all-gather | bytes 313344 | tf_op jit(solution)/shard_map/all_gather | solution.py:71
  129.7 20.1 %all_gather.32 = bf16[768,192]{1,0:T(8,128)(2,1)S(1)} all-gather(bf16[48,192]{1,0:T(8,128)(2,1)S(1)} %copy-done.295), channel_id=1, replica_groups=mesh['dp'=16,'mp'=2] {'dp'}, dimensions={0}, use_global_device_ids=true | all-gather | bytes 313344 | tf_op jit(solution)/shard_map/all_gather | solution.py:70
  152.1 18.7 %all_gather.36 = bf16[768,192]{1,0:T(8,128)(2,1)S(1)} all-gather(bf16[48,192]{1,0:T(8,128)(2,1)S(1)} %copy-done.296), channel_id=1, replica_groups=mesh['dp'=16,'mp'=2] {'dp'}, dimensions={0}, use_global_device_ids=true | all-gather | bytes 313344 | tf_op jit(solution)/shard_map/all_gather | solution.py:73
  173.1 20.9 %all_gather.33 = bf16[2,192,768]{1,2,0:T(8,128)(2,1)S(1)} all-gather(bf16[2,192,48]{1,2,0:T(8,128)(2,1)S(1)} %copy-done.277), channel_id=1, replica_groups=mesh['dp'=16,'mp'=2] {'dp'}, dimensions={2}, use_global_device_ids=true | all-gather | bytes 626688 | tf_op jit(solution)/shard_map/all_gather | solution.py:75
  252.7 6.1 add_convert_fusion.3
  258.8 4.4 convolution_add_fusion.4
  273.7 220.4 %all-reduce.79.cloned.1.call-done = (f32[1024,768]{1,0:T(8,128)}, f32[1024,768]{1,0:T(8,128)}, f32[1024,768]{1,0:T(8,128)}) async-done(((f32[1024,768]{1,0:T(8,128)}, f32[1024,768]{1,0:T(8,128)}, f32[1024,768]{1,0:T(8,128)}), (f32[1024,768]{1,0:T(8,128)}, f32[1024,768]{1,0:T(8,128)}, f32[1024,768]{1,0:T(8,128)})) %all-reduce.79.cloned.1.call-update) | async-done | bytes 9437200 | tf_op jit(solution)/shard_map/psum | solution.py:170
  494.2 6.5 fusion.271
  506.0 4.0 subtract_multiply_fusion.5
  510.1 3.7 fusion.256
  518.4 8.2 multiply_convert_fusion.8
  526.6 5.5 fusion.479
  532.1 3.1 fusion.481
  535.2 3.1 fusion.480
  538.3 7.4 all-reduce.70
  545.8 6.6 convert_reduce_fusion.7
  552.4 8.9 all-reduce.69
  563.4 6.8 convert_reduce_fusion.11
  570.2 7.1 convert_reduce_fusion.2
  582.1 6.8 convert_reduce_fusion
  599.2 6.8 convert_reduce_fusion.1
  618.4 3.5 fusion.362
  627.9 7.1 copy.73
  635.0 38.4 %all-gather.18.cloned.1.call-done = f32[1024,768]{1,0:T(8,128)} async-done(((f32[1024,384]{1,0:T(8,128)}), f32[1024,768]{1,0:T(8,128)}) %all-gather.18.cloned.1.call-update) | async-done | bytes 3145744 | tf_op jit(solution)/shard_map/all_gather | solution.py:287
  673.4 5.4 multiply_reduce_fusion.8
  678.9 40.9 %all-gather.16.cloned.1.call-done = f32[1024,768]{1,0:T(8,128)} async-done(((f32[1024,384]{1,0:T(8,128)}), f32[1024,768]{1,0:T(8,128)}) %all-gather.16.cloned.1.call-update) | async-done | bytes 3145744 | tf_op jit(solution)/shard_map/all_gather | solution.py:287
  719.8 10.7 convert_reduce_fusion.5
  792.4 4.3 convert_reduce_fusion.12
  809.3 4.9 all-gather.3
  816.3 4.3 convert_reduce_fusion.14
  830.7 4.9 all-gather.1
  835.7 3.6 fusion.507
  844.6 4.9 convert_reduce_fusion.13
  859.5 4.9 all-gather.2
  868.9 9.3 fusion.143
  878.4 8.5 fusion.85
  889.5 10.0 fusion.145
  899.6 7.9 fusion.118
  908.9 3.2 fusion.246
  912.0 3.5 copy.72
  915.6 15.4 %fusion.167 = bf16[1024,768]{1,0:T(8,128)(2,1)} fusion(f32[1024,768]{1,0:T(8,128)} %fusion.510, f32[1024,768]{1,0:T(8,128)} %fusion.508, f32[1024,768]{1,0:T(8,128)} %fusion.507, f32[1024,768]{1,0:T(8,128)} %get-tuple-element.299, f32[1024,768]{1,0:T(8,128)} %get-tuple-element.301, f32[1024,768]{1,0:T(8,128)} %get-tuple-element.303, ...), kind=kOutput, calls=%fused_computation.360 | convolution fusion | flops 312999936 | bytes 40012800 | tf_op jit(solution)/shard_map/dot_general | solution.py:27
  944.5 3.5 fusion.515
  948.0 4.2 convert_reduce_fusion.18
  952.6 10.4 multiply_multiply_fusion.10
  963.1 12.3 fusion.165
  978.0 3.7 fusion.513
  996.2 10.8 fusion.166
  1010.6 4.4 fusion.438
  1017.5 3.3 fusion.174
  1074.9 51.1 %all-reduce.67 = (f32[192]{0:T(256)}, f32[192]{0:T(256)}, f32[192]{0:T(256)}, f32[192,54]{0,1:T(8,128)}, f32[54]{0:T(128)}, /*index=5*/f32[192]{0:T(256)}, f32[7...) all-reduce(f32[192]{0:T(256)S(1)} %add_add_fusion.14, ...), channel_id=1, replica_groups=mesh['dp'=16,'mp'=2] {'dp'}, use_global_device_ids=true, to_apply=%region_111.112 | all-reduce | flops 16182 | bytes 129456 | tf_op jit(solution)/shard_map/psum | solution.py:538
  1126.9 5.6 psum.244
  1140.3 19.7 %reduce-scatter.33.cloned.1.call-done = bf16[384,1024]{1,0:T(8,128)(2,1)} async-done(((bf16[768,1024]{1,0:T(8,128)(2,1)}), bf16[384,1024]{1,0:T(8,128)(2,1)}) %reduce-scatter.33.cloned.1.call-update) | async-done | bytes 786448
  1168.0 58.9 %reduce-scatter.29.cloned.1.call-done = f32[1,96,384]{2,1,0:T(8,128)} async-done(((f32[1,1536,384]{2,1,0:T(8,128)}), f32[1,96,384]{2,1,0:T(8,128)}) %reduce-scatter.29.cloned.1.call-update) | async-done | bytes 147472 | tf_op jit(solution)/shard_map/reduce_scatter | solution.py:535
  1226.9 60.0 %reduce-scatter.41.cloned.1.call-done = f32[48,192]{1,0:T(8,128)} async-done(((f32[768,192]{1,0:T(8,128)}), f32[48,192]{1,0:T(8,128)}) %reduce-scatter.41.cloned.1.call-update) | async-done | bytes 36880
  1286.9 59.7 %reduce-scatter.39.cloned.1.call-done = f32[48,192]{1,0:T(8,128)} async-done(((f32[768,192]{1,0:T(8,128)}), f32[48,192]{1,0:T(8,128)}) %reduce-scatter.39.cloned.1.call-update) | async-done | bytes 36880
  1346.6 60.0 %reduce-scatter.27.cloned.1.call-done = f32[48,192]{1,0:T(8,128)} async-done(((f32[768,192]{1,0:T(8,128)}), f32[48,192]{1,0:T(8,128)}) %reduce-scatter.27.cloned.1.call-update) | async-done | bytes 36880 | tf_op jit(solution)/shard_map/reduce_scatter | solution.py:530
  1406.6 59.7 %reduce-scatter.37.cloned.1.call-done = f32[48,192]{1,0:T(8,128)} async-done(((f32[768,192]{1,0:T(8,128)}), f32[48,192]{1,0:T(8,128)}) %reduce-scatter.37.cloned.1.call-update) | async-done | bytes 36880
  1466.3 60.0 %reduce-scatter.45.cloned.1.call-done = f32[48,192]{1,0:T(8,128)} async-done(((f32[768,192]{1,0:T(8,128)}), f32[48,192]{1,0:T(8,128)}) %reduce-scatter.45.cloned.1.call-update) | async-done | bytes 36880
  (1129 shorter events, 358.5 us)
Async XLA Ops:
  8.0 93.3 %copy-start = (bf16[192,54]{0,1:T(8,128)(2,1)S(1)}, bf16[192,54]{0,1:T(8,128)(2,1)}, u32[]{:S(2)}) copy-start(bf16[192,54]{0,1:T(8,128)(2,1)} %param.35) | copy-start | bytes 62212
  8.0 23.3 %copy-start.333 = (f32[192]{0:T(256)S(1)}, f32[192]{0:T(256)}, u32[]{:S(2)}) copy-start(f32[192]{0:T(256)} %param.30) | copy-start | bytes 2308
  8.1 232.5 %all-reduce.81.cloned.1.call-start = ((), (), s32[]{:S(2)}) async-start(), calls=%async_computation.27 | async-start | bytes 1376256 | tf_op jit(solution)/shard_map/psum | solution.py:132
  8.1 26.1 %copy-start.1 = (bf16[3072,768]{1,0:T(8,128)(2,1)S(1)}, bf16[3072,768]{1,0:T(8,128)(2,1)}, u32[]{:S(2)}) copy-start(bf16[3072,768]{1,0:T(8,128)(2,1)} %param.25) | copy-start | bytes 14155780
  35.7 42.5 %copy-start.327 = (pred[1028]{0:T(1024)(128)(4,1)S(1)}, pred[1028]{0:T(1024)(128)(4,1)}, u32[]{:S(2)}) copy-start(pred[1028]{0:T(1024)(128)(4,1)} %constant.65.clone.1) | copy-start | bytes 3088
  37.2 49.6 %copy-start.38 = (bf16[1024,768]{1,0:T(8,128)(2,1)}, bf16[1024,768]{1,0:T(8,128)(2,1)S(1)}, u32[]{:S(2)}) copy-start(bf16[1024,768]{1,0:T(8,128)(2,1)S(1)} %get-tuple-element.291) | copy-start | bytes 4718596
  37.2 56.6 %copy-start.32 = (bf16[1024,768]{1,0:T(8,128)(2,1)}, bf16[1024,768]{1,0:T(8,128)(2,1)S(1)}, u32[]{:S(2)}) copy-start(bf16[1024,768]{1,0:T(8,128)(2,1)S(1)} %get-tuple-element.292) | copy-start | bytes 4718596
  58.1 35.7 %copy-start.197 = (f32[768]{0:T(1024)}, f32[768]{0:T(1024)S(1)}, u32[]{:S(2)}) copy-start(f32[768]{0:T(1024)S(1)} %get-tuple-element.223) | copy-start | bytes 9220
  58.1 35.7 %copy-start.240 = (f32[768]{0:T(1024)}, f32[768]{0:T(1024)S(1)}, u32[]{:S(2)}) copy-start(f32[768]{0:T(1024)S(1)} %get-tuple-element.218) | copy-start | bytes 9220
  58.1 35.7 %copy-start.242 = (f32[768]{0:T(1024)}, f32[768]{0:T(1024)S(1)}, u32[]{:S(2)}) copy-start(f32[768]{0:T(1024)S(1)} %get-tuple-element.222) | copy-start | bytes 9220
  58.1 35.7 %copy-start.244 = (f32[768]{0:T(1024)}, f32[768]{0:T(1024)S(1)}, u32[]{:S(2)}) copy-start(f32[768]{0:T(1024)S(1)} %get-tuple-element.224) | copy-start | bytes 9220
  58.1 35.7 %copy-start.246 = (f32[768]{0:T(1024)}, f32[768]{0:T(1024)S(1)}, u32[]{:S(2)}) copy-start(f32[768]{0:T(1024)S(1)} %get-tuple-element.225) | copy-start | bytes 9220
  58.1 35.7 %copy-start.248 = (f32[768]{0:T(1024)}, f32[768]{0:T(1024)S(1)}, u32[]{:S(2)}) copy-start(f32[768]{0:T(1024)S(1)} %get-tuple-element.226) | copy-start | bytes 9220
  58.1 35.7 %copy-start.258 = (f32[768]{0:T(1024)}, f32[768]{0:T(1024)S(1)}, u32[]{:S(2)}) copy-start(f32[768]{0:T(1024)S(1)} %get-tuple-element.221) | copy-start | bytes 9220
  58.2 35.7 %copy-start.260 = (f32[768]{0:T(1024)}, f32[768]{0:T(1024)S(1)}, u32[]{:S(2)}) copy-start(f32[768]{0:T(1024)S(1)} %get-tuple-element.219) | copy-start | bytes 9220
  58.2 35.7 %copy-start.262 = (f32[768]{0:T(1024)}, f32[768]{0:T(1024)S(1)}, u32[]{:S(2)}) copy-start(f32[768]{0:T(1024)S(1)} %get-tuple-element.220) | copy-start | bytes 9220
  102.3 47.5 %slice-start = ((s8[4718592]{0:T(1024)(128)(4,1)}), s8[524288]{0:T(1024)(128)(4,1)S(1)}, s32[]{:S(2)}) async-start(s8[4718592]{0:T(1024)(128)(4,1)} %bitcast.522), calls=%async_computation.28 | async-start | bytes 1048576
  104.2 390.0 %all-reduce.79.cloned.1.call-start = ((), (), s32[]{:S(2)}) async-start(), calls=%async_computation.26 | async-start | bytes 18874368 | tf_op jit(solution)/shard_map/psum | solution.py:170
  122.8 27.0 %slice-start.1 = ((s8[4718592]{0:T(1024)(128)(4,1)}), s8[4194304]{0:T(1024)(128)(4,1)S(1)}, s32[]{:S(2)}) async-start(s8[4718592]{0:T(1024)(128)(4,1)} %bitcast.522), calls=%async_computation.29 | async-start | bytes 8388608
  125.1 78.7 %copy-start.162 = (bf16[1024,192]{0,1:T(8,128)(2,1)}, bf16[1024,192]{0,1:T(8,128)(2,1)S(1)}, u32[]{:S(2)}) copy-start(bf16[1024,192]{0,1:T(8,128)(2,1)S(1)} %fusion.238) | copy-start | bytes 1179652
  127.4 88.6 %copy-start.164 = (bf16[1024,192]{0,1:T(8,128)(2,1)}, bf16[1024,192]{0,1:T(8,128)(2,1)S(1)}, u32[]{:S(2)}) copy-start(bf16[1024,192]{0,1:T(8,128)(2,1)S(1)} %fusion.236) | copy-start | bytes 1179652
  129.7 99.4 %copy-start.166 = (bf16[1024,192]{0,1:T(8,128)(2,1)}, bf16[1024,192]{0,1:T(8,128)(2,1)S(1)}, u32[]{:S(2)}) copy-start(bf16[1024,192]{0,1:T(8,128)(2,1)S(1)} %fusion.234) | copy-start | bytes 1179652
  150.5 50.3 %copy-start.66 = (bf16[1024,192]{0,1:T(8,128)(2,1)}, bf16[1024,192]{0,1:T(8,128)(2,1)S(1)}, u32[]{:S(2)}) copy-start(bf16[1024,192]{0,1:T(8,128)(2,1)S(1)} %convolution_convert_fusion.9) | copy-start | bytes 1179652
  151.2 61.8 %copy-start.71 = (bf16[1024,192]{0,1:T(8,128)(2,1)}, bf16[1024,192]{0,1:T(8,128)(2,1)S(1)}, u32[]{:S(2)}) copy-start(bf16[1024,192]{0,1:T(8,128)(2,1)S(1)} %convolution_convert_fusion.10) | copy-start | bytes 1179652
  151.9 74.3 %copy-start.68 = (bf16[1024,192]{0,1:T(8,128)(2,1)}, bf16[1024,192]{0,1:T(8,128)(2,1)S(1)}, u32[]{:S(2)}) copy-start(bf16[1024,192]{0,1:T(8,128)(2,1)S(1)} %convolution_convert_fusion.11) | copy-start | bytes 1179652
  151.9 67.7 %copy-start.152 = (bf16[512,192]{0,1:T(8,128)(2,1)}, bf16[512,192]{0,1:T(8,128)(2,1)S(1)}, u32[]{:S(2)}) copy-start(bf16[512,192]{0,1:T(8,128)(2,1)S(1)} %get-tuple-element.397) | copy-start | bytes 589828
  152.0 74.2 %copy-start.140 = (bf16[512,192]{0,1:T(8,128)(2,1)}, bf16[512,192]{0,1:T(8,128)(2,1)S(1)}, u32[]{:S(2)}) copy-start(bf16[512,192]{0,1:T(8,128)(2,1)S(1)} %get-tuple-element.398) | copy-start | bytes 589828
  152.0 55.2 %copy-start.150 = (bf16[512,192]{0,1:T(8,128)(2,1)}, bf16[512,192]{0,1:T(8,128)(2,1)S(1)}, u32[]{:S(2)}) copy-start(bf16[512,192]{0,1:T(8,128)(2,1)S(1)} %get-tuple-element.395) | copy-start | bytes 589828
  152.0 61.0 %copy-start.136 = (bf16[512,192]{0,1:T(8,128)(2,1)}, bf16[512,192]{0,1:T(8,128)(2,1)S(1)}, u32[]{:S(2)}) copy-start(bf16[512,192]{0,1:T(8,128)(2,1)S(1)} %get-tuple-element.396) | copy-start | bytes 589828
  152.1 42.6 %copy-start.151 = (bf16[512,192]{0,1:T(8,128)(2,1)}, bf16[512,192]{0,1:T(8,128)(2,1)S(1)}, u32[]{:S(2)}) copy-start(bf16[512,192]{0,1:T(8,128)(2,1)S(1)} %get-tuple-element.393) | copy-start | bytes 589828
  152.1 48.7 %copy-start.138 = (bf16[512,192]{0,1:T(8,128)(2,1)}, bf16[512,192]{0,1:T(8,128)(2,1)S(1)}, u32[]{:S(2)}) copy-start(bf16[512,192]{0,1:T(8,128)(2,1)S(1)} %get-tuple-element.394) | copy-start | bytes 589828
  170.8 64.5 %copy-start.96 = (bf16[768,192]{1,0:T(8,128)(2,1)}, bf16[768,192]{1,0:T(8,128)(2,1)S(1)}, u32[]{:S(2)}) copy-start(bf16[768,192]{1,0:T(8,128)(2,1)S(1)} %all_gather.36) | copy-start | bytes 884740
  173.1 90.2 %copy-start.127 = (f32[1024,192]{0,1:T(8,128)}, f32[1024,192]{0,1:T(8,128)S(1)}, u32[]{:S(2)}) copy-start(f32[1024,192]{0,1:T(8,128)S(1)} %convolution_add_fusion.16) | copy-start | bytes 2359300
  194.0 75.2 %copy-start.12 = (bf16[2,192,768]{1,2,0:T(8,128)(2,1)}, bf16[2,192,768]{1,2,0:T(8,128)(2,1)S(1)}, u32[]{:S(2)}) copy-start(bf16[2,192,768]{1,2,0:T(8,128)(2,1)S(1)} %all_gather.33) | copy-start | bytes 1769476
  200.8 32.0 %copy-start.193 = (bf16[3,64,512]{2,1,0:T(8,128)(2,1)}, bf16[3,64,512]{2,1,0:T(8,128)(2,1)S(1)}, u32[]{:S(2)}) copy-start(bf16[3,64,512]{2,1,0:T(8,128)(2,1)S(1)} %fusion.263) | copy-start | bytes 589828
  206.6 26.3 %copy-start.195 = (bf16[3,64,512]{2,1,0:T(8,128)(2,1)}, bf16[3,64,512]{2,1,0:T(8,128)(2,1)S(1)}, u32[]{:S(2)}) copy-start(bf16[3,64,512]{2,1,0:T(8,128)(2,1)S(1)} %fusion.262) | copy-start | bytes 589828
  235.9 31.5 %copy-start.129 = (f32[1024,192]{0,1:T(8,128)}, f32[1024,192]{0,1:T(8,128)S(1)}, u32[]{:S(2)}) copy-start(f32[1024,192]{0,1:T(8,128)S(1)} %convolution_add_fusion.20) | copy-start | bytes 2359300
  272.2 221.9 %copy-start.284 = (f32[768]{0:T(1024)S(1)}, f32[768]{0:T(1024)}, u32[]{:S(2)}) copy-start(f32[768]{0:T(1024)} %param.40) | copy-start | bytes 9220
  272.3 237.8 %all-gather.10.cloned.1.call-start = ((), (), s32[]{:S(2)}) async-start(), calls=%async_computation.10 | async-start | bytes 1253376 | tf_op jit(solution)/shard_map/all_gather | solution.py:76
  272.9 253.7 %all-gather.12.cloned.1.call-start = ((), (), s32[]{:S(2)}) async-start(), calls=%async_computation.11 | async-start | bytes 1253376 | tf_op jit(solution)/shard_map/all_gather | solution.py:77
  273.4 361.6 %all-gather.14.cloned.1.call-start = ((), (), s32[]{:S(2)}) async-start(), calls=%async_computation.12 | async-start | bytes 4718592 | tf_op jit(solution)/shard_map/all_gather | solution.py:287
  273.7 308.4 %copy-start.292 = (f32[1536]{0:T(1024)}, f32[1536]{0:T(1024)S(1)}, u32[]{:S(2)}) copy-start(f32[1536]{0:T(1024)S(1)} %reduce.21) | copy-start | bytes 18436
  582.0 91.4 %all-gather.18.cloned.1.call-start = ((), (), s32[]{:S(2)}) async-start(), calls=%async_computation.14 | async-start | bytes 4718592 | tf_op jit(solution)/shard_map/all_gather | solution.py:287
  593.7 126.1 %all-gather.16.cloned.1.call-start = ((), (), s32[]{:S(2)}) async-start(), calls=%async_computation.13 | async-start | bytes 4718592 | tf_op jit(solution)/shard_map/all_gather | solution.py:287
  595.6 185.7 %copy-start.252 = (f32[3,512]{1,0:T(4,128)}, f32[3,512]{1,0:T(4,128)S(1)}, u32[]{:S(2)}) copy-start(f32[3,512]{1,0:T(4,128)S(1)} %log_add_fusion.1) | copy-start | bytes 18436
  596.3 191.3 %copy-start.256 = (f32[3,512]{1,0:T(4,128)}, f32[3,512]{1,0:T(4,128)S(1)}, u32[]{:S(2)}) copy-start(f32[3,512]{1,0:T(4,128)S(1)} %log_add_fusion) | copy-start | bytes 18436
  597.1 166.2 %copy-start.250 = (f32[3,512]{1,0:T(4,128)}, f32[3,512]{1,0:T(4,128)S(1)}, u32[]{:S(2)}) copy-start(f32[3,512]{1,0:T(4,128)S(1)} %log_add_fusion.3) | copy-start | bytes 18436
  597.8 171.6 %copy-start.254 = (f32[3,512]{1,0:T(4,128)}, f32[3,512]{1,0:T(4,128)S(1)}, u32[]{:S(2)}) copy-start(f32[3,512]{1,0:T(4,128)S(1)} %log_add_fusion.2) | copy-start | bytes 18436
  610.7 515.4 %reduce-scatter.43.cloned.1.call-start = ((), (), s32[]{:S(2)}) async-start(), calls=%async_computation.23 | async-start | bytes 417792
  635.0 84.8 %copy-start.281 = (f32[1024]{0:T(1024)S(1)}, f32[1024]{0:T(1024)}, u32[]{:S(2)}) copy-start(f32[1024]{0:T(1024)} %copy-done.280) | copy-start | bytes 12292
  635.0 84.8 %copy-start.283 = (f32[1024]{0:T(1024)S(1)}, f32[1024]{0:T(1024)}, u32[]{:S(2)}) copy-start(f32[1024]{0:T(1024)} %copy-done.282) | copy-start | bytes 12292
  678.9 51.7 %copy-start.279 = (f32[1024]{0:T(1024)S(1)}, f32[1024]{0:T(1024)}, u32[]{:S(2)}) copy-start(f32[1024]{0:T(1024)} %copy-done.278) | copy-start | bytes 12292
  814.2 51.6 %copy-start.144 = (bf16[54,1024]{1,0:T(8,128)(2,1)}, bf16[54,1024]{1,0:T(8,128)(2,1)S(1)}, u32[]{:S(2)}) copy-start(bf16[54,1024]{1,0:T(8,128)(2,1)S(1)} %reshape.1443) | copy-start | bytes 331780
  908.8 223.7 %all-reduce.77.cloned.1.call-start = ((), (), s32[]{:S(2)}) async-start(), calls=%async_computation.25 | async-start | bytes 7864320
  915.6 220.1 %reduce-scatter.31.cloned.1.call-start = ((), (), s32[]{:S(2)}) async-start(), calls=%async_computation.17 | async-start | bytes 2359296
  944.4 193.6 %reduce-scatter.35.cloned.1.call-start = ((), (), s32[]{:S(2)}) async-start(), calls=%async_computation.19 | async-start | bytes 2359296
  981.6 178.3 %reduce-scatter.33.cloned.1.call-start = ((), (), s32[]{:S(2)}) async-start(), calls=%async_computation.18 | async-start | bytes 2359296
  1008.7 218.2 %reduce-scatter.29.cloned.1.call-start = ((), (), s32[]{:S(2)}) async-start(), calls=%async_computation.16 | async-start | bytes 2506752 | tf_op jit(solution)/shard_map/reduce_scatter | solution.py:535
  1020.9 266.1 %reduce-scatter.41.cloned.1.call-start = ((), (), s32[]{:S(2)}) async-start(), calls=%async_computation.22 | async-start | bytes 835584
  1044.7 301.9 %reduce-scatter.39.cloned.1.call-start = ((), (), s32[]{:S(2)}) async-start(), calls=%async_computation.21 | async-start | bytes 835584
  1052.8 353.7 %reduce-scatter.27.cloned.1.call-start = ((), (), s32[]{:S(2)}) async-start(), calls=%async_computation.15 | async-start | bytes 835584 | tf_op jit(solution)/shard_map/reduce_scatter | solution.py:530
  1058.4 407.9 %reduce-scatter.37.cloned.1.call-start = ((), (), s32[]{:S(2)}) async-start(), calls=%async_computation.20 | async-start | bytes 835584
  1070.2 456.2 %reduce-scatter.45.cloned.1.call-start = ((), (), s32[]{:S(2)}) async-start(), calls=%async_computation.24 | async-start | bytes 835584
  1140.3 23.9 %copy-start.65 = (f32[1024,768]{1,0:T(8,128)S(1)}, f32[1024,768]{1,0:T(8,128)}, u32[]{:S(2)}) copy-start(f32[1024,768]{1,0:T(8,128)} %get-tuple-element.437) | copy-start | bytes 9437188
  (319 other events, 1858.6 us)
Sparse Core Ops, SparseCore 0:
  104.3 32.5 all-reduce.80
  272.4 221.7 all-reduce.78
  582.1 44.9 all-gather.13
  628.5 44.9 all-gather.17
  674.8 44.9 all-gather.15
Sparse Core Ops, SparseCore 1:
  275.0 37.4 all-gather.9
  314.7 37.4 all-gather.11
  908.9 55.4 reduce-scatter.42
  968.5 107.6 all-reduce.76
  1078.5 24.9 reduce-scatter.30
  1105.8 26.0 reduce-scatter.34
  1134.1 25.9 reduce-scatter.32
  1164.2 62.6 reduce-scatter.28
  1231.3 55.6 reduce-scatter.40
  1291.1 55.5 reduce-scatter.38
  1351.0 55.5 reduce-scatter.26
  1410.7 55.5 reduce-scatter.36
  1470.7 55.5 reduce-scatter.44
where the time goes:
time: 1550 us; the launch traced here: 1530 us
  waiting for transfers between devices  679 us (44%)
  matrix products  323 us (21%)
  blocking collectives  224 us (14%)
  other arithmetic  193 us (12%)
  local copies, waits for them, and re-layouts  91.8 us (6%)
  between operations  22.3 us (1%)
    unnamed x27, waiting for transfers between devices  260 us
    psum x1, waiting for transfers between devices, forward_pass(): branch = lax.psum(partial_out, 'mp') + b_out  220 us
    dot_general x30, matrix products, matmul_right(): lax.dot_general(left, right, (((1,), (1,)), ((), ())), preferred_element_...  132 us
    all_gather x3, waiting for transfers between devices, backward_pass(): lax.all_gather(grad_normed_here, 'mp', axis=1, tiled=True)  79.4 us
    dot_general x30, matrix products, matmul(): return jnp.dot(left, right, preferred_element_type=jnp.float32)  65.2 us
    unnamed x778, local copies, waits for them, and re-layouts  62.1 us
    reduce_scatter x1, waiting for transfers between devices, on_device(): lax.psum_scatter(big_totals[3], 'dp', scatter_dimension=0, tiled=True)  60 us
    reduce_scatter x1, waiting for transfers between devices, on_device(): lax.psum_scatter(big_totals[8], 'dp', scatter_dimension=1, tiled=True)  58.9 us
  transfers between devices with their start and end apart: 18, of which 10 were waited for; matrix products, arithmetic and copies ran while one was open for 20% of the time, Pallas kernels for 0%

commit v1 on v0

v1 whole, which is shorter than its diff:
```python
import functools
import jax
import jax.numpy as jnp
from jax import lax
from jax.experimental import pallas as pl
from jax.experimental.pallas import tpu as pltpu

from jax.sharding import PartitionSpec as P

MESH = pl.DeviceIdType.MESH


def at(dp, mp):
    return (dp, mp)


def places(count):
    dp = lax.axis_index("dp")
    core = lax.rem(dp, 2)
    side = lax.rem(lax.div(dp, 2), 2)
    deep = lax.div(dp, 4)
    return lax.axis_index("mp"), core, side, deep, count // 4


def index_of(deep, side, core):
    return (deep * 2 + side) * 2 + core


def greet(count):
    mp, core, side, deep, parts = places(count)
    barrier = pltpu.get_barrier_semaphore()
    peers = [index_of(lax.rem(deep + k, parts), side, core) for k in range(1, parts)]
    peers += [index_of(deep, 1 - side, core), index_of(deep, side, 1 - core)]
    for peer in peers:
        pl.semaphore_signal(barrier, inc=1, device_id=at(peer, mp), device_id_type=MESH)
    pl.semaphore_wait(barrier, len(peers))


def gather_kernel(count, own_ref, out_ref, own_sem, send_sem, recv_sem):
    mp, core, side, deep, parts = places(count)
    me = index_of(deep, side, core)
    greet(count)
    local = pltpu.make_async_copy(own_ref.at[0], out_ref.at[me], own_sem)
    local.start()
    started = []

    def push(source, block, target):
        copy = pltpu.make_async_remote_copy(
            src_ref=source,
            dst_ref=out_ref.at[block],
            send_sem=send_sem.at[len(started)],
            recv_sem=recv_sem.at[block],
            device_id=at(target, mp),
            device_id_type=MESH,
        )
        copy.start()
        started.append(copy)

    def arrive(block):
        pltpu.make_async_copy(own_ref.at[0], out_ref.at[block], recv_sem.at[block]).wait()

    beside = index_of(deep, 1 - side, core)
    twin = index_of(deep, side, 1 - core)
    for k in range(1, parts):
        push(own_ref.at[0], me, index_of(lax.rem(deep + k, parts), side, core))
    push(own_ref.at[0], me, beside)
    push(own_ref.at[0], me, twin)
    arrive(beside)
    push(out_ref.at[beside], beside, twin)
    for k in range(1, parts):
        block = index_of(lax.rem(deep + parts - k, parts), side, core)
        arrive(block)
        push(out_ref.at[block], block, beside)
        push(out_ref.at[block], block, twin)
    for k in range(1, parts):
        block = index_of(lax.rem(deep + parts - k, parts), 1 - side, core)
        arrive(block)
        push(out_ref.at[block], block, twin)
    for k in range(parts):
        for other in range(2):
            arrive(index_of(lax.rem(deep + parts - k, parts), other, 1 - core))
    for copy in started:
        copy.wait_send()
    local.wait()


def gather(own, count, ident):
    parts = count // 4
    sends = (parts - 1) * 4 + 3
    shape = (count,) + own.shape[1:]
    return pl.pallas_call(
        functools.partial(gather_kernel, count),
        out_shape=jax.ShapeDtypeStruct(shape, own.dtype),
        in_specs=[pl.BlockSpec(memory_space=pl.ANY)],
        out_specs=pl.BlockSpec(memory_space=pl.ANY),
        scratch_shapes=[
            pltpu.SemaphoreType.DMA,
            pltpu.SemaphoreType.DMA((sends,)),
            pltpu.SemaphoreType.DMA((count,)),
        ],
        compiler_params=pltpu.CompilerParams(collective_id=ident, has_side_effects=True),
        name="weight_gather",
    )(own)


def scatter_kernel(
    count, in_ref, small_ref, out_ref, total_ref,
    twin_in, side_in, deep_in, twin_sum, side_sum,
    small_in, small_out, send_sem, recv_sem, small_send, small_recv,
):
    mp, core, side, deep, parts = places(count)
    me = index_of(deep, side, core)
    barrier = pltpu.get_barrier_semaphore()
    pl.semaphore_signal(barrier, inc=1, device_id=at(me, 1 - mp), device_id_type=MESH)
    peers = [index_of(lax.rem(deep + k, parts), side, core) for k in range(1, parts)]
    peers += [index_of(deep, 1 - side, core), index_of(deep, side, 1 - core)]
    for peer in peers:
        pl.semaphore_signal(barrier, inc=1, device_id=at(peer, mp), device_id_type=MESH)
    pl.semaphore_wait(barrier, len(peers) + 1)
    beside = index_of(deep, 1 - side, core)
    twin = index_of(deep, side, 1 - core)
    started = []
    rows = in_ref.shape[1]
    step = rows // 4 if rows % 64 == 0 else rows

    def push(source, target_ref, slot, target, sends=send_sem, recvs=recv_sem, plane=mp):
        copy = pltpu.make_async_remote_copy(
            src_ref=source,
            dst_ref=target_ref,
            send_sem=sends.at[slot],
            recv_sem=recvs.at[slot],
            device_id=at(target, plane),
            device_id_type=MESH,
        )
        copy.start()
        started.append(copy)
        return copy

    def add(target, first, second):
        @pl.loop(0, rows // step)
        def _(i):
            part = pl.ds(pl.multiple_of(i * step, step), step)
            total = first[part, :].astype(jnp.float32) + second[part, :].astype(jnp.float32)
            target[part, :] = total.astype(target.dtype)

    small_hop = push(small_ref, small_in.at[0], 0, me, small_send, small_recv, 1 - mp)
    order = [(k, other) for k in list(range(1, parts)) + [0] for other in (1, 0)]
    hop = {}
    for slot, (k, other) in enumerate(order):
        z = lax.rem(deep + k, parts)
        s = 1 - side if other else side
        hop[(k, other)] = push(
            in_ref.at[index_of(z, s, 1 - core)], twin_in.at[slot], slot, twin
        )
    small_hop.wait_recv()
    shared = small_ref.shape[0] - SHARED_ROWS
    small_out[0, pl.ds(0, shared), :] = small_ref[pl.ds(0, shared), :]
    small_out[0, pl.ds(shared, SHARED_ROWS), :] = (
        small_ref[pl.ds(shared, SHARED_ROWS), :] + small_in[0, pl.ds(shared, SHARED_ROWS), :]
    )
    small_hop = push(small_out.at[0], small_in.at[1], 1, twin, small_send, small_recv)
    base = len(order)
    hop2 = {}
    for slot, (k, other) in enumerate(order):
        z = lax.rem(deep + k, parts)
        s = 1 - side if other else side
        hop[(k, other)].wait_recv()
        add(twin_sum.at[slot], in_ref.at[index_of(z, s, core)], twin_in.at[slot])
        if other:
            place = slot // 2
            hop2[k] = push(twin_sum.at[slot], side_in.at[place], base + place, beside)
        if slot == 1:
            small_hop.wait_recv()
            small_out[1] = small_out[0] + small_in[1]
            small_hop = push(small_out.at[1], small_in.at[2], 2, beside, small_send, small_recv)
    base2 = base + parts
    hop3 = []
    small_hops = []
    for place, k in enumerate(list(range(1, parts)) + [0]):
        hop2[k].wait_recv()
        add(side_sum.at[place], twin_sum.at[2 * place + 1], side_in.at[place])
        if k:
            z = lax.rem(deep + k, parts)
            hop3.append(
                push(side_sum.at[place], deep_in.at[place], base2 + place, index_of(z, side, core))
            )
        if place == 0:
            small_hop.wait_recv()
            small_out[2] = small_out[1] + small_in[2]
            for j in range(1, parts):
                z = lax.rem(deep + j, parts)
                small_hops.append(
                    push(small_out.at[2], small_in.at[2 + j], 2 + j, index_of(z, side, core), small_send, small_recv)
                )
    for copy in small_hops:
        copy.wait_recv()
    total = small_out[2]
    for j in range(1, parts):
        total = total + small_in[2 + j]
    total_ref[...] = total
    for copy in hop3:
        copy.wait_recv()

    @pl.loop(0, rows // step)
    def _(i):
        part = pl.ds(pl.multiple_of(i * step, step), step)
        total = side_sum[parts - 1, part, :].astype(jnp.float32)
        for place in range(parts - 1):
            total = total + deep_in[place, part, :].astype(jnp.float32)
        out_ref[part, :] = total

    for copy in started:
        copy.wait_send()


def scatter(blocks, small, count, ident):
    parts = count // 4
    _, rows, columns = blocks.shape
    sends = 4 * parts - 1
    kind = blocks.dtype
    return pl.pallas_call(
        functools.partial(scatter_kernel, count),
        out_shape=(
            jax.ShapeDtypeStruct((rows, columns), jnp.float32),
            jax.ShapeDtypeStruct(small.shape, jnp.float32),
        ),
        in_specs=[pl.BlockSpec(memory_space=pltpu.VMEM)] * 2,
        out_specs=(pl.BlockSpec(memory_space=pltpu.VMEM),) * 2,
        scratch_shapes=[
            pltpu.VMEM((2 * parts, rows, columns), kind),
            pltpu.VMEM((parts, rows, columns), kind),
            pltpu.VMEM((max(parts - 1, 1), rows, columns), kind),
            pltpu.VMEM((2 * parts, rows, columns), kind),
            pltpu.VMEM((parts, rows, columns), kind),
            pltpu.VMEM((parts + 2,) + small.shape, jnp.float32),
            pltpu.VMEM((3,) + small.shape, jnp.float32),
            pltpu.SemaphoreType.DMA((sends,)),
            pltpu.SemaphoreType.DMA((sends,)),
            pltpu.SemaphoreType.DMA((parts + 2,)),
            pltpu.SemaphoreType.DMA((parts + 2,)),
        ],
        compiler_params=pltpu.CompilerParams(
            collective_id=ident, has_side_effects=True, vmem_limit_bytes=60 << 20
        ),
        name="gradient_scatter",
    )(blocks, small)

HEAD_DIM = 64
KERNEL = 9
HALF = KERNEL // 2
EPSILON = 1e-06
MASK_FILL = -1e30
INV_ROOT2 = 0.7071067811865476
INV_ROOT_TWO_PI = 0.3989422804014327
SHARED_ROWS = 24
SWAP = [(0, 1), (1, 0)]
BF16 = jnp.bfloat16
F32 = jnp.float32


class Group:
    def __init__(self, **parts):
        self.__dict__.update(parts)


def total_of(groups):
    return Group(**{k: sum(vars(g)[k] for g in groups) for k in vars(groups[0])})


def nn(left, right):
    return jnp.dot(left, right, preferred_element_type=F32)


def tn(left, right):
    return lax.dot_general(left, right, (((0,), (0,)), ((), ())), preferred_element_type=F32)


def nt(left, right):
    return lax.dot_general(left, right, (((1,), (1,)), ((), ())), preferred_element_type=F32)


def swap(value):
    return lax.ppermute(value, "mp", SWAP)


def shifted(tensor, offset, half_width):
    filler = jnp.zeros((half_width,) + tensor.shape[1:], tensor.dtype)
    padded = jnp.concatenate([filler, tensor, filler], axis=0)
    return padded[half_width + offset : half_width + offset + tensor.shape[0]]


def same_segment(segment, offset, half_width):
    filler = jnp.full((half_width,), -1, dtype=jnp.int32)
    padded = jnp.concatenate([filler, segment, filler])
    return padded[half_width + offset : half_width + offset + segment.shape[0]] == segment


def segment_ids(lengths_row, seq_rows):
    doc_ends = jnp.cumsum(lengths_row)
    positions = jnp.arange(seq_rows, dtype=jnp.int32)
    return jnp.sum((positions[:, None] >= doc_ends[None, :]).astype(jnp.int32), axis=1)


def tap_mask_list(segment):
    return [
        same_segment(segment, tap - HALF, HALF).astype(F32)[:, None] for tap in range(KERNEL)
    ]


def gelu(tensor):
    return 0.5 * tensor * (1.0 + lax.erf(tensor * INV_ROOT2))


def gelu_slope(tensor):
    normal_cdf = 0.5 * (1.0 + lax.erf(tensor * INV_ROOT2))
    return normal_cdf + tensor * jnp.exp(-0.5 * tensor * tensor) * INV_ROOT_TWO_PI


def halves(value, me):
    width = value.shape[1] // 2
    return (
        lax.dynamic_slice_in_dim(value, me * width, width, 1),
        lax.dynamic_slice_in_dim(value, (1 - me) * width, width, 1),
    )


def joined(own, other, me):
    return jnp.where(me == 0, jnp.concatenate([own, other], 1), jnp.concatenate([other, own], 1))


def part_a(rows_in, segment, w, p, me):
    seq_rows = rows_in.shape[0]
    width = w.query.shape[1]
    heads = width // HEAD_DIM
    queries = (nn(rows_in, w.query) + p.query_bias).astype(BF16)
    keys = nn(rows_in, w.key).astype(BF16)
    values = (nn(rows_in, w.value) + p.value_bias).astype(BF16)
    masks = tap_mask_list(segment)
    depthwise = jnp.zeros(rows_in.shape, F32)
    for tap in range(KERNEL):
        moved = shifted(rows_in, tap - HALF, HALF).astype(F32)
        depthwise = depthwise + w.depth[tap].astype(F32) * moved * masks[tap]
    depthwise = depthwise.astype(BF16)
    key_conv = nn(depthwise, w.point) + p.point_bias
    conv_attn = (key_conv * queries.astype(F32)).astype(BF16)
    own, other = halves(nn(conv_attn, p.kernel_weight), me)
    logits = own + swap(other) + halves(p.kernel_bias[None], me)[0]
    kernel_probs = jax.nn.softmax(logits.reshape(seq_rows, heads, KERNEL), axis=-1)
    conv_values = (nn(rows_in, w.conv) + p.conv_bias).reshape(seq_rows, heads, HEAD_DIM)
    conv_context = jnp.zeros((seq_rows, heads, HEAD_DIM), F32)
    for tap in range(KERNEL):
        now = kernel_probs[:, :, tap] * masks[tap]
        conv_context = conv_context + now[:, :, None] * shifted(conv_values, tap - HALF, HALF)
    conv_context = conv_context.reshape(seq_rows, width).astype(BF16)
    query_heads = queries.reshape(seq_rows, heads, HEAD_DIM)
    key_heads = keys.reshape(seq_rows, heads, HEAD_DIM)
    value_heads = values.reshape(seq_rows, heads, HEAD_DIM)
    scores = jnp.einsum("qhd,khd->hqk", query_heads, key_heads, preferred_element_type=F32) * 0.125
    scores = jnp.where((segment[:, None] == segment[None, :])[None], scores, MASK_FILL)
    top = jnp.max(scores, axis=-1, keepdims=True)
    exponent = jnp.exp(scores - top)
    total = jnp.sum(exponent, axis=-1, keepdims=True)
    probs_low = (exponent / total).astype(BF16)
    context = jnp.einsum("hqk,khd->qhd", probs_low, value_heads, preferred_element_type=F32)
    context = context.reshape(seq_rows, width).astype(BF16)
    log_total = top[:, :, 0] + jnp.log(total[:, :, 0])
    return (queries, keys, values, depthwise, key_conv, conv_attn, kernel_probs, conv_values, conv_context, context, log_total)


def moments(sum_own, square_own, sum_other, square_other, width):
    mean = (sum_own + sum_other) / (2 * width)
    apart = (sum_own - sum_other) / width
    spread = (square_own + square_other + apart * apart * (width / 2)) / (2 * width)
    return mean, lax.rsqrt(spread + EPSILON)


def transposed_stats(columns):
    rows = columns[0].shape[0]
    lane = lax.broadcasted_iota(jnp.int32, (rows, 128), 1)
    packed = jnp.zeros((rows, 128), F32)
    for place, column in enumerate(columns):
        packed = jnp.where(lane == place, column, packed)
    return jnp.transpose(packed)[:8]


def stat_columns(message, amount):
    rows = message.shape[1]
    wide = jnp.concatenate([message, jnp.zeros((120, rows), F32)], 0)
    tall = jnp.transpose(wide)
    return [tall[:, k : k + 1] for k in range(amount)]


def row_sums(value):
    rows, columns = value.shape
    return jnp.sum(value.reshape(rows // 8, 8, columns), axis=0)


SLOTS = 4
FFN_STEP = 256


def middle_kernel(
    blocks,
    context_ref, conv_ref, hidden_ref, grad_ref, grad_late_ref, out0_ref, out1_ref, inner_ref, outer_ref, vec_ref,
    output_ref, residual_ref, branch_ref, big_inner_ref, big_outer_ref, small_ref,
    state, scale_ring, act_ring, slope_ring, low_ring, summed_ring, normed_ring, stat_ring,
    acc_inner, acc_outer, acc_small, acc_bias,
    branch_out, branch_in, stat1_out, stat1_in, stat2_out, stat2_in, stat3_out, stat3_in, back_out, back_in,
    send_sem, recv_sem,
):
    i = pl.program_id(0)
    me = lax.axis_index("mp")
    dp = lax.axis_index("dp")
    width = summed_ring.shape[2]
    hidden_units = inner_ref.shape[0]
    inverse = 1.0 / (2 * width)

    def message(kind, source, target, slot):
        return pltpu.make_async_remote_copy(
            src_ref=source.at[slot],
            dst_ref=target.at[slot],
            send_sem=send_sem.at[kind, slot],
            recv_sem=recv_sem.at[kind, slot],
            device_id=(dp, 1 - me),
            device_id_type=MESH,
        )

    kinds = [
        (branch_out, branch_in), (stat1_out, stat1_in), (stat2_out, stat2_in), (stat3_out, stat3_in), (back_out, back_in),
    ]

    def fresh(kind, b, slot):
        @pl.when(b >= SLOTS)
        def _():
            message(kind, *kinds[kind], slot).wait_send()

    def vec(row):
        return vec_ref[row : row + 1, :width]

    @pl.when(i == 0)
    def _():
        barrier = pltpu.get_barrier_semaphore()
        pl.semaphore_signal(barrier, inc=1, device_id=(dp, 1 - me), device_id_type=MESH)
        pl.semaphore_wait(barrier, 1)
        acc_inner[...] = jnp.zeros_like(acc_inner)
        acc_outer[...] = jnp.zeros_like(acc_outer)
        acc_small[...] = jnp.zeros_like(acc_small)
        acc_bias[...] = jnp.zeros_like(acc_bias)

    @pl.when(i < blocks)
    def _():
        b = i
        slot = lax.rem(b, SLOTS)
        fresh(0, b, slot)
        theirs = pl.ds(pl.multiple_of((1 - me) * width, width), width)
        ours = pl.ds(pl.multiple_of(me * width, width), width)
        other = nt(context_ref[...], out0_ref[theirs, :]) + nt(conv_ref[...], out1_ref[theirs, :])
        branch_out[slot] = other.astype(BF16)
        message(0, *kinds[0], slot).start()
        own = nt(context_ref[...], out0_ref[ours, :]) + nt(conv_ref[...], out1_ref[ours, :])
        state[lax.rem(b, 8)] = hidden_ref[:, ours].astype(F32) + (own + vec(0))

    @pl.when(jnp.logical_and(i >= 1, i < blocks + 1))
    def _():
        b = i - 1
        slot = lax.rem(b, SLOTS)
        message(0, *kinds[0], slot).wait_recv()
        fresh(1, b, slot)
        residual = state[lax.rem(b, 8)] + branch_in[slot].astype(F32)
        state[lax.rem(b, 8)] = residual
        total = jnp.sum(residual, axis=1, keepdims=True)
        apart = residual - total * (1.0 / width)
        stat1_out[slot] = transposed_stats([total, jnp.sum(apart * apart, axis=1, keepdims=True)])
        message(1, *kinds[1], slot).start()

    @pl.when(jnp.logical_and(i >= 2, i < blocks + 2))
    def _():
        b = i - 2
        slot = lax.rem(b, SLOTS)
        two = lax.rem(b, 2)
        message(1, *kinds[1], slot).wait_recv()
        fresh(2, b, slot)
        total, square = stat_columns(stat1_out[slot], 2)
        total_o, square_o = stat_columns(stat1_in[slot], 2)
        mean, scale = moments(total, square, total_o, square_o, width)
        standard = (state[lax.rem(b, 8)] - mean) * scale
        state[lax.rem(b, 8)] = standard
        scale_ring[lax.rem(b, 4)] = jnp.broadcast_to(scale, scale_ring.shape[1:])
        normed = standard * vec(1) + vec(2)
        low = normed.astype(BF16)
        low_ring[two] = low
        summed = normed + vec(3)
        for start in range(0, hidden_units, FFN_STEP):
            part = pl.ds(start, FFN_STEP)
            inner = nt(low, inner_ref[part, :]) + vec_ref[7:8, start : start + FFN_STEP]
            cdf = 0.5 * (1.0 + lax.erf(inner * INV_ROOT2))
            act = (inner * cdf).astype(BF16)
            act_ring[two, :, part] = act
            slope_ring[two, :, part] = cdf + inner * jnp.exp(-0.5 * inner * inner) * INV_ROOT_TWO_PI
            summed = summed + nn(act, outer_ref[part, :])
        summed_ring[two] = summed
        scaled = grad_ref[...].astype(F32) * vec(4)
        total = jnp.sum(summed, axis=1, keepdims=True)
        apart = summed - total * (1.0 / width)
        stat2_out[slot] = transposed_stats(
            [
                total,
                jnp.sum(apart * apart, axis=1, keepdims=True),
                jnp.sum(scaled, axis=1, keepdims=True),
                jnp.sum(scaled * apart, axis=1, keepdims=True),
            ]
        )
        message(2, *kinds[2], slot).start()

    @pl.when(jnp.logical_and(i >= 3, i < blocks + 3))
    def _():
        b = i - 3
        slot = lax.rem(b, SLOTS)
        two = lax.rem(b, 2)
        message(2, *kinds[2], slot).wait_recv()
        fresh(3, b, slot)
        total, square, grads, cross = stat_columns(stat2_out[slot], 4)
        total_o, square_o, grads_o, cross_o = stat_columns(stat2_in[slot], 4)
        mean, scale = moments(total, square, total_o, square_o, width)
        mean_grad = (grads + grads_o) * inverse
        product = cross + cross_o + (total * (1.0 / width) - mean) * grads + (total_o * (1.0 / width) - mean) * grads_o
        mean_product = product * scale * inverse
        standard = (summed_ring[two] - mean) * scale
        output_ref[...] = (standard * vec(4) + vec(5)).astype(BF16)
        gradient = grad_late_ref[...].astype(F32)
        grad_summed = scale * (gradient * vec(4) - mean_grad - standard * mean_product)
        low = grad_summed.astype(BF16)
        acc_small[0] += row_sums(low.astype(F32))
        acc_small[1] += row_sums(gradient * standard)
        acc_small[2] += row_sums(gradient)
        normed_low = low_ring[two]
        grad_normed = grad_summed
        for start in range(0, hidden_units, FFN_STEP):
            part = pl.ds(start, FFN_STEP)
            grad_inner = nt(low, outer_ref[part, :]) * slope_ring[two, :, part]
            inner_low = grad_inner.astype(BF16)
            acc_bias[:, part] += row_sums(inner_low.astype(F32))
            grad_normed = grad_normed + nn(inner_low, inner_ref[part, :])
            acc_outer[part, :] += tn(act_ring[two, :, part], low)
            acc_inner[part, :] += tn(inner_low, normed_low)
        normed_ring[two] = grad_normed
        standard1 = state[lax.rem(b, 8)]
        scaled = grad_normed * vec(1)
        acc_small[3] += row_sums(grad_normed * standard1)
        acc_small[4] += row_sums(grad_normed)
        sums = transposed_stats(
            [jnp.sum(scaled, axis=1, keepdims=True), jnp.sum(scaled * standard1, axis=1, keepdims=True)]
        )
        stat3_out[slot] = sums
        message(3, *kinds[3], slot).start()

    @pl.when(jnp.logical_and(i >= 4, i < blocks + 4))
    def _():
        b = i - 4
        slot = lax.rem(b, SLOTS)
        message(3, *kinds[3], slot).wait_recv()
        fresh(4, b, slot)
        first, second = stat_columns(stat3_out[slot] + stat3_in[slot], 2)
        standard = state[lax.rem(b, 8)]
        scaled = normed_ring[lax.rem(b, 2)] * vec(1)
        residual = scale_ring[lax.rem(b, 4)][:, :1] * (scaled - first * inverse - standard * (second * inverse))
        residual_ref[...] = residual
        low = residual.astype(BF16)
        acc_small[5] += row_sums(low.astype(F32))
        back_out[slot] = low
        message(4, *kinds[4], slot).start()

    @pl.when(i >= 5)
    def _():
        b = i - 5
        slot = lax.rem(b, SLOTS)
        message(4, *kinds[4], slot).wait_recv()
        theirs = pl.ds(pl.multiple_of((1 - me) * width, width), width)
        ours = pl.ds(pl.multiple_of(me * width, width), width)
        branch_ref[:, ours] = back_out[slot]
        branch_ref[:, theirs] = back_in[slot]

    @pl.when(i == blocks + 4)
    def _():
        for kind in range(5):
            for slot in range(SLOTS):
                message(kind, *kinds[kind], slot).wait_send()
        big_inner_ref[...] = acc_inner[...].astype(BF16)
        big_outer_ref[...] = acc_outer[...].astype(BF16)
        small_ref[...] = jnp.zeros_like(small_ref)
        for row in range(6):
            small_ref[row : row + 1, :width] = jnp.sum(acc_small[row], axis=0, keepdims=True)
        small_ref[6:7, :] = jnp.sum(acc_bias[...], axis=0, keepdims=True)


def middle(context, conv_context, hidden, out_grad, w, p, me, ident):
    tokens, model = hidden.shape
    width = model // 2
    local = context.shape[1]
    units = w.inner.shape[0]
    rows = 256
    blocks = tokens // rows

    def mine(value):
        return lax.dynamic_slice_in_dim(value, me * width, width, 0)

    vectors = [
        mine(p.out_bias), mine(p.norm1_gain), mine(p.norm1_bias), p.ffn_out_bias, p.norm2_gain, p.norm2_bias,
    ]
    table = jnp.stack([jnp.pad(v, (0, units - width)) for v in vectors] + [jnp.zeros((units,), F32), p.ffn_in_bias])

    def block(columns, lag):
        return pl.BlockSpec((rows, columns), lambda i: (jnp.clip(i - lag, 0, blocks - 1), 0))

    whole = pl.BlockSpec(memory_space=pltpu.VMEM)
    stat = pltpu.VMEM((SLOTS, 8, rows), F32)
    half = pltpu.VMEM((SLOTS, rows, width), BF16)
    return pl.pallas_call(
        functools.partial(middle_kernel, blocks),
        grid=(blocks + 5,),
        out_shape=(
            jax.ShapeDtypeStruct((tokens, width), BF16),
            jax.ShapeDtypeStruct((tokens, width), F32),
            jax.ShapeDtypeStruct((tokens, model), BF16),
            jax.ShapeDtypeStruct((units, width), BF16),
            jax.ShapeDtypeStruct((units, width), BF16),
            jax.ShapeDtypeStruct((8, units), F32),
        ),
        in_specs=[
            block(local, 0), block(local, 0), block(model, 0), block(width, 2), block(width, 3),
            whole, whole, whole, whole, whole,
        ],
        out_specs=(block(width, 3), block(width, 4), block(model, 5), whole, whole, whole),
        scratch_shapes=[
            pltpu.VMEM((8, rows, width), F32),
            pltpu.VMEM((4, rows, 128), F32),
            pltpu.VMEM((2, rows, units), BF16),
            pltpu.VMEM((2, rows, units), F32),
            pltpu.VMEM((2, rows, width), BF16),
            pltpu.VMEM((2, rows, width), F32),
            pltpu.VMEM((2, rows, width), F32),
            pltpu.VMEM((8, 128), F32),
            pltpu.VMEM((units, width), F32),
            pltpu.VMEM((units, width), F32),
            pltpu.VMEM((6, 8, width), F32),
            pltpu.VMEM((8, units), F32),
            half, half, stat, stat, stat, stat, stat, stat, half, half,
            pltpu.SemaphoreType.DMA((5, SLOTS)),
            pltpu.SemaphoreType.DMA((5, SLOTS)),
        ],
        compiler_params=pltpu.CompilerParams(
            collective_id=ident, has_side_effects=True, vmem_limit_bytes=60 << 20
        ),
        name="middle",
    )(context, conv_context, hidden, out_grad, out_grad, w.out0, w.out1, w.inner, w.outer, table)


def part_c(rows_in, segment, grad_branch, grad_residual, kept, w, p, me):
    (queries, keys, values, depthwise, key_conv, conv_attn, kernel_probs, conv_values, conv_context, context, log_total) = kept
    seq_rows = rows_in.shape[0]
    width = queries.shape[1]
    heads = width // HEAD_DIM
    masks = tap_mask_list(segment)
    big = Group(out0=tn(grad_branch, context), out1=tn(grad_branch, conv_context))
    small = Group()
    grad_context = nn(grad_branch, w.out0).astype(BF16).reshape(seq_rows, heads, HEAD_DIM)
    grad_conv = nn(grad_branch, w.out1).astype(BF16).reshape(seq_rows, heads, HEAD_DIM)
    tap_grads = []
    grad_conv_values = jnp.zeros((seq_rows, heads, HEAD_DIM), F32)
    for tap in range(KERNEL):
        tap_grads.append(
            masks[tap] * jnp.sum(grad_conv * shifted(conv_values, tap - HALF, HALF), axis=2)
        )
        now = kernel_probs[:, :, tap] * masks[tap]
        grad_conv_values = grad_conv_values + shifted(now[:, :, None] * grad_conv, HALF - tap, HALF)
    grad_taps = jnp.stack(tap_grads, axis=2)
    grad_logits = kernel_probs * (grad_taps - jnp.sum(kernel_probs * grad_taps, axis=2, keepdims=True))
    logits_own = grad_logits.reshape(seq_rows, heads * KERNEL).astype(BF16)
    logits_low = joined(logits_own, swap(logits_own), me)
    small.kernel_bias = jnp.sum(logits_low, axis=0, dtype=F32)
    small.kernel_weight = tn(conv_attn, logits_low)
    attn_wide = nt(logits_low, p.kernel_weight).astype(BF16).astype(F32)
    key_low = (attn_wide * queries.astype(F32)).astype(BF16)
    small.point_bias = jnp.sum(key_low, axis=0, dtype=F32)
    big.point = tn(depthwise, key_low)
    grad_depthwise = nt(key_low, w.point)
    depth_rows = []
    grad_rows = jnp.zeros(rows_in.shape, F32)
    for tap in range(KERNEL):
        masked = grad_depthwise * masks[tap]
        moved = shifted(rows_in, tap - HALF, HALF).astype(F32)
        depth_rows.append(jnp.sum(masked * moved, axis=0))
        grad_rows = grad_rows + shifted(masked * w.depth[tap].astype(F32), HALF - tap, HALF)
    small.depth = jnp.stack(depth_rows, axis=0)
    conv_low = grad_conv_values.reshape(seq_rows, width).astype(BF16)
    small.conv_bias = jnp.sum(conv_low, axis=0, dtype=F32)
    big.conv = tn(rows_in, conv_low)
    grad_rows = grad_rows + nt(conv_low, w.conv)
    query_heads = queries.reshape(seq_rows, heads, HEAD_DIM)
    key_heads = keys.reshape(seq_rows, heads, HEAD_DIM)
    value_heads = values.reshape(seq_rows, heads, HEAD_DIM)
    scores = jnp.einsum("qhd,khd->hqk", query_heads, key_heads, preferred_element_type=F32) * 0.125
    scores = jnp.where((segment[:, None] == segment[None, :])[None], scores, MASK_FILL)
    probs = jnp.exp(scores - log_total[:, :, None])
    probs_low = probs.astype(BF16)
    grad_probs = jnp.einsum("qhd,khd->hqk", grad_context, value_heads, preferred_element_type=F32)
    scores_low = (probs * (grad_probs - jnp.sum(probs * grad_probs, axis=2, keepdims=True))).astype(BF16)
    grad_queries = jnp.einsum("hqk,khd->qhd", scores_low, key_heads, preferred_element_type=F32) * 0.125
    grad_queries = (grad_queries.reshape(seq_rows, width) + attn_wide * key_conv).astype(BF16)
    grad_keys = jnp.einsum("hqk,qhd->khd", scores_low, query_heads, preferred_element_type=F32) * 0.125
    grad_keys = grad_keys.reshape(seq_rows, width).astype(BF16)
    grad_values = jnp.einsum("hqk,qhd->khd", probs_low, grad_context, preferred_element_type=F32)
    grad_values = grad_values.reshape(seq_rows, width).astype(BF16)
    small.query_bias = jnp.sum(grad_queries, axis=0, dtype=F32)
    small.value_bias = jnp.sum(grad_values, axis=0, dtype=F32)
    big.query = tn(rows_in, grad_queries)
    big.key = tn(rows_in, grad_keys)
    big.value = tn(rows_in, grad_values)
    grad_rows = grad_rows + nt(grad_queries, w.query) + nt(grad_keys, w.key) + nt(grad_values, w.value)
    own, other = halves(grad_rows, me)
    grad_input = own + grad_residual + swap(other.astype(BF16)).astype(F32)
    return grad_input, big, small


def padded(value, multiple):
    rows = value.shape[-2]
    extra = -rows % multiple
    return jnp.pad(value, [(0, 0)] * (value.ndim - 2) + [(0, extra), (0, 0)])


def on_device(
    count,
    hidden, doc_lengths, query_weight, key_weight, value_weight, query_bias, value_bias,
    depth_weight, point_weight, point_bias, kernel_weight, kernel_bias, conv_weight, conv_bias,
    out_weight, out_bias, norm1_gain, norm1_bias, ffn_in_weight, ffn_in_bias, ffn_out_weight,
    ffn_out_bias, norm2_gain, norm2_bias, out_grad,
):
    me = lax.axis_index("mp")
    share, width = query_weight.shape
    model = hidden.shape[1]
    group = ffn_out_bias.shape[0]
    share_ffn = ffn_out_weight.shape[1]
    depth_wide = jnp.pad(depth_weight.T, ((0, 0), (0, width - KERNEL)))
    first = jnp.concatenate(
        [
            jnp.concatenate([query_weight, key_weight], 1),
            jnp.concatenate([value_weight, conv_weight], 1),
            jnp.concatenate([point_weight, depth_wide], 1),
        ],
        0,
    )
    out_cut = jnp.concatenate([out_weight[0].T, out_weight[1].T], 1)
    second = jnp.concatenate([out_cut, ffn_in_weight[0].T, ffn_out_weight[0]], 0)
    first_all = gather(padded(first, 16)[None], count, 1)
    second_all = gather(padded(second, 16)[None], count, 2)

    def cut(source, start, size, low, high):
        return source[:, start : start + size, low:high].reshape(count * size, high - low)

    w = Group(
        query=cut(first_all, 0, share, 0, width),
        key=cut(first_all, 0, share, width, 2 * width),
        value=cut(first_all, share, share, 0, width),
        conv=cut(first_all, share, share, width, 2 * width),
        point=cut(first_all, 2 * share, share, 0, width),
        depth=cut(first_all, 2 * share, share, width, width + KERNEL).T,
        out0=cut(second_all, 0, share, 0, width),
        out1=cut(second_all, 0, share, width, 2 * width),
        inner=cut(second_all, share, share_ffn, 0, group),
        outer=cut(second_all, share + share_ffn, share_ffn, 0, group),
    )
    p = Group(
        query_bias=query_bias, value_bias=value_bias, point_bias=point_bias, kernel_weight=kernel_weight,
        kernel_bias=kernel_bias, conv_bias=conv_bias, out_bias=out_bias, norm1_gain=norm1_gain,
        norm1_bias=norm1_bias, ffn_in_bias=ffn_in_bias[0], ffn_out_bias=ffn_out_bias,
        norm2_gain=norm2_gain, norm2_bias=norm2_bias,
    )
    seqs = doc_lengths.shape[0]
    seq_rows = hidden.shape[0] // seqs
    spans = [slice(s * seq_rows, (s + 1) * seq_rows) for s in range(seqs)]
    segments = [segment_ids(doc_lengths[s], seq_rows) for s in range(seqs)]
    kept = [part_a(hidden[spans[s]], segments[s], w, p, me) for s in range(seqs)]
    output, grad_residual, grad_branch, big_inner, big_outer, sums_mid = middle(
        jnp.concatenate([k[9] for k in kept], 0),
        jnp.concatenate([k[8] for k in kept], 0),
        hidden, out_grad, w, p, me, 4,
    )
    last = [
        part_c(hidden[spans[s]], segments[s], grad_branch[spans[s]], grad_residual[spans[s]], kept[s], w, p, me)
        for s in range(seqs)
    ]
    grad_input = jnp.concatenate([t[0] for t in last], 0)
    big = total_of([t[1] for t in last])
    small = total_of([t[2] for t in last])

    def widened(value):
        empty = jnp.zeros_like(value)
        return jnp.where(me == 0, jnp.concatenate([value, empty]), jnp.concatenate([empty, value]))


    def blocks(value):
        return value.reshape(count, value.shape[0] // count, value.shape[1])

    pieces = jnp.concatenate(
        [
            blocks(jnp.concatenate([big.query, big.key], 1)),
            blocks(jnp.concatenate([big.value, big.conv], 1)),
            blocks(jnp.concatenate([big.point, jnp.zeros_like(big.point)], 1)),
            blocks(jnp.concatenate([big.out0, big.out1], 1)),
        ],
        1,
    ).astype(BF16)
    pieces = jnp.concatenate([pieces, blocks(big_inner), blocks(big_outer)], 1)
    own_parts = [
        small.query_bias, small.value_bias, small.point_bias, small.kernel_weight, small.kernel_bias,
        small.conv_bias, sums_mid[6], sums_mid[0, :group], sums_mid[1, :group], sums_mid[2, :group],
    ]
    columns = group

    def table(parts, rows):
        flat = jnp.concatenate([part.reshape(-1) for part in parts])
        return jnp.pad(flat, (0, rows * columns - flat.shape[0])).reshape(rows, columns)

    own_size = sum(part.size for part in own_parts)
    own_rows = -(-own_size // columns)
    own_rows += -own_rows % 8
    shared_parts = [small.depth] + [widened(sums_mid[k, :group]) for k in (3, 4, 5)]
    smalls = jnp.concatenate([table(own_parts, own_rows), table(shared_parts, SHARED_ROWS)], 0)
    sums, totals = scatter(padded(pieces, 16), smalls, count, 3)

    def untable(value, parts):
        flat, result, start = value.reshape(-1), [], 0
        for part in parts:
            result.append(flat[start : start + part.size].reshape(part.shape))
            start += part.size
        return result

    query_b, value_b, point_b, kernel_w, kernel_b, conv_b, in_b, outer_b, gain2, bias2 = untable(
        totals[:own_rows], own_parts
    )
    depth_g, gain1, bias1, out_b = untable(totals[own_rows:], shared_parts)
    place = lax.axis_index("dp")
    depth_own = lax.dynamic_slice_in_dim(depth_g, place * share, share, 1)
    at_rows = lambda k: sums[k * share : (k + 1) * share]
    qk, vc, po, oo = at_rows(0), at_rows(1), at_rows(2), at_rows(3)
    inner_own = sums[4 * share : 4 * share + share_ffn]
    outer_own = sums[4 * share + share_ffn : 4 * share + 2 * share_ffn]
    return (
        output,
        grad_input,
        qk[:, :width],
        qk[:, width:],
        vc[:, :width],
        query_b,
        value_b,
        depth_own,
        po[:, :width],
        point_b,
        kernel_w,
        kernel_b,
        vc[:, width:],
        conv_b,
        jnp.stack([oo[:, :width].T, oo[:, width:].T]),
        out_b,
        gain1,
        bias1,
        inner_own.T[None],
        in_b[None],
        outer_own[None],
        outer_b,
        gain2,
        bias2,
    )


def solution(mesh):
    in_specs = (
        P("dp", None),
        P("dp", None),
        P("dp", "mp"),
        P("dp", "mp"),
        P("dp", "mp"),
        P("mp"),
        P("mp"),
        P(None, "dp"),
        P("dp", "mp"),
        P("mp"),
        P("mp", None),
        P(),
        P("dp", "mp"),
        P("mp"),
        P(None, "mp", "dp"),
        P(),
        P(),
        P(),
        P("mp", None, "dp"),
        P("mp", None),
        P("mp", "dp", None),
        P("mp"),
        P("mp"),
        P("mp"),
        P("dp", "mp"),
    )
    out_specs = (
        P("dp", "mp"),
        P("dp", "mp"),
        P("dp", "mp"),
        P("dp", "mp"),
        P("dp", "mp"),
        P("mp"),
        P("mp"),
        P(None, "dp"),
        P("dp", "mp"),
        P("mp"),
        P("mp", None),
        P(),
        P("dp", "mp"),
        P("mp"),
        P(None, "mp", "dp"),
        P(),
        P(),
        P(),
        P("mp", None, "dp"),
        P("mp", None),
        P("mp", "dp", None),
        P("mp"),
        P("mp"),
        P("mp"),
    )
    return jax.shard_map(
        functools.partial(on_device, mesh.shape["dp"]), mesh=mesh, in_specs=in_specs, out_specs=out_specs, check_vma=False
    )
```

time: 1550 us -> 778 us (0.50)
  waiting for transfers between devices: 679 us -> 29.9 us
  Pallas kernels: 0 us -> 229 us
  blocking collectives: 224 us -> 0 us
  matrix products: 323 us -> 231 us
  other arithmetic: 193 us -> 155 us
  between operations: 22.3 us -> 4.94 us
  local copies, waits for them, and re-layouts: 91.8 us -> 109 us
    unnamed x27 -> x0, waiting for transfers between devices: 260 us -> none
    pallas_call x0 -> x4, Pallas kernels: none -> 229 us  [the longest x1 127 us: middle(): pl.pallas_call(functools.partial(middle_kernel, blocks), grid=(blocks + 5...]
    psum x2 -> x0, waiting for transfers between devices: 220 us -> none  [the longest x1 220 us: forward_pass(): branch = lax.psum(partial_out, 'mp') + b_out]
    all_gather x10 -> x0, blocking collectives: 151 us -> none  [the longest x1 20.9 us: gather_layer(): lax.all_gather(w_out, 'dp', axis=2, tiled=True)]
    reduce_scatter x2 -> x0, waiting for transfers between devices: 119 us -> none  [the longest x1 60 us: on_device(): lax.psum_scatter(big_totals[3], 'dp', scatter_dimension=0, tiled=True)]
    dot_general x126 -> x84, matrix products: 323 us -> 231 us  [the longest x18 96.1 us: nt(): lax.dot_general(left, right, (((1,), (1,)), ((), ())), preferred_element_...]
    all_gather x5 -> x0, waiting for transfers between devices: 79.4 us -> none  [the longest x3 79.4 us: backward_pass(): lax.all_gather(grad_normed_here, 'mp', axis=1, tiled=True)]
    psum x4 -> x0, blocking collectives: 73.1 us -> none  [the longest x1 51.1 us: on_device(): lax.psum((small_totals[0], small_totals[1], small_totals[2], small_totals...]
  transfers between devices with their start and end apart: 18 -> 9, of which waited for: 10 -> 2; matrix products, arithmetic and copies ran while one was open for 20% -> 24% of each run, Pallas kernels for 0% -> 4%
where the time goes in v1:
time: 778 us; the launch traced here: 769 us
  matrix products  231 us (30%)
  Pallas kernels  229 us (29%)
  other arithmetic  155 us (20%)
  local copies, waits for them, and re-layouts  109 us (14%)
  waiting for transfers between devices  29.9 us (4%)
  starting transfers between devices  9.11 us (1%)
    pallas_call x1, Pallas kernels, middle(): pl.pallas_call(functools.partial(middle_kernel, blocks), grid=(blocks + 5...  127 us
    dot_general x18, matrix products, nt(): lax.dot_general(left, right, (((1,), (1,)), ((), ())), preferred_element_...  96.1 us
    pallas_call x1, Pallas kernels, scatter(): pl.pallas_call(functools.partial(scatter_kernel, count), out_shape=(jax.S...  54.7 us
    pallas_call x2, Pallas kernels, gather(): pl.pallas_call(functools.partial(gather_kernel, count), out_shape=jax.Sha...  46.9 us
    dot_general x24, matrix products, tn(): lax.dot_general(left, right, (((0,), (0,)), ((), ())), preferred_element_...  42.9 us
    unnamed x550, local copies, waits for them, and re-layouts  39.2 us
    ppermute x9, waiting for transfers between devices, swap(): return lax.ppermute(value, 'mp', SWAP)  29.9 us
    dot_general x24, matrix products, nn(): return jnp.dot(left, right, preferred_element_type=F32)  28.4 us
  transfers between devices with their start and end apart: 9, of which 2 were waited for; matrix products, arithmetic and copies ran while one was open for 24% of the time, Pallas kernels for 4%

profile of v1, /device:TPU:8, one launch (start us, length us, event | category | flops | bytes accessed | tf_op | source)
XLA Modules:
  0.0 768.6 jit_solution(5808316102547864302)
XLA Ops:
  3.0 19.7 %weight_gather.2 = bf16[16,144,384]{2,1,0:T(8,128)(2,1)} custom-call(bf16[1,144,384]{2,1,0:T(8,128)(2,1)} %fusion.265.own_ref), custom_call_target="tpu_custom_call" | custom-call | tf_op jit(solution)/shard_map/weight_gather/pallas_call | solution.py:91
  23.8 3.0 fusion.371
  27.8 4.3 fusion.368
  34.7 2.5 fusion.151
  37.2 6.2 fusion.66
  50.2 13.7 %fusion.118 = bf16[1024,768]{1,0:T(8,128)(2,1)S(1)} fusion(bf16[1024,768]{1,0:T(8,128)(2,1)} %get-tuple-element.177, f32[1024]{0:T(1024)S(1)} %get-tuple-element.341, f32[1024]{0:T(1024)S(1)} %get-tuple-element.336, f32[1024]{0:T(1024)S(1)} %get-tuple-element.340, f32[1024]{0:T(1024)S(1)} %get-tuple-element.335, f32[1024]{0:T(1024)S(1)} %get-tuple-element.337, ...), kind=kLoop, calls=%fused_computation.266 | loop fusion | flops 27525120 | bytes 3206144 | tf_op jit(solution)/shard_map/convert_element_type | solution.py:343
  69.7 5.8 fusion.92
  96.2 27.2 %weight_gather.3 = bf16[16,240,384]{2,1,0:T(8,128)(2,1)} custom-call(bf16[1,240,384]{2,1,0:T(8,128)(2,1)} %maximum_bitcast_fusion.own_ref), custom_call_target="tpu_custom_call" | custom-call | tf_op jit(solution)/shard_map/weight_gather/pallas_call | solution.py:91
  125.8 3.3 fusion.369
  129.1 3.2 fusion.377
  134.2 2.8 copy-done.3
  137.0 3.2 fusion.158
  142.2 3.9 fusion.376
  147.9 2.8 copy-done.2
  150.7 3.0 fusion.157
  155.8 3.2 fusion.375
  160.8 2.9 copy-done.1
  163.6 2.5 fusion.156
  167.2 2.5 pad_maximum_fusion.1.context_ref
  195.8 5.6 add_convert_fusion.2
  202.5 2.6 add_convert_fusion
  205.8 6.3 add_convert_fusion.1
  213.2 2.5 pad_maximum_fusion.2.conv_ref
  215.7 127.0 %middle.1 = (bf16[3072,384]{1,0:T(8,128)(2,1)}, f32[3072,384]{1,0:T(8,128)}, bf16[3072,768]{1,0:T(8,128)(2,1)}, bf16[1536,384]{1,0:T(8,128)(2,1)}, bf16[1536,384]{1,0:T(8,128)(2,1)}, /*index=5*/f32[8,1536]{1,0:T(8,128)}) custom-call(bf16[3072,192]{1,0:T(8,128)(2,1)} %pad_maximum_fusion.1.context_ref, bf16[3072,192]{1,0:T(8,128)(2,1)} %pad_maximum_fusion.2.conv_ref, ...), custom_call_target="tpu_custom_call" | custom-call | tf_op jit(solution)/shard_map/middle/pallas_call | solution.py:618
  345.9 2.8 fusion.184
  348.6 2.7 fusion.182
  359.3 4.5 convert_reduce_fusion.2
  363.8 2.7 fusion.350
  368.8 3.4 convert_reduce_fusion.8
  372.2 5.9 multiply_reduce_fusion.2
  378.1 10.4 %multiply_convert_fusion.2 = bf16[3,1024,1024]{1,2,0:T(8,128)(2,1)S(1)} fusion(f32[3,1024,1024]{1,2,0:T(8,128)} %get-tuple-element.355, f32[3,1024,1024]{1,2,0:T(8,128)} %copy-done.3, f32[3,1024]{1,0:T(4,128)S(1)} %get-tuple-element.354, f32[3,1024]{1,0:T(4,128)S(1)} %log_add_fusion.2), kind=kLoop, calls=%fused_computation.9 | loop fusion | flops 12582912 | bytes 31481856 | tf_op jit(solution)/shard_map/convert_element_type | solution.py:707
  392.7 2.7 fusion.354
  397.7 2.8 convert_reduce_fusion.7
  400.4 6.8 multiply_reduce_fusion.1
  407.2 9.2 %multiply_convert_fusion.1 = bf16[3,1024,1024]{1,2,0:T(8,128)(2,1)} fusion(f32[3,1024,1024]{1,2,0:T(8,128)} %get-tuple-element.357, f32[3,1024,1024]{1,2,0:T(8,128)S(1)} %bitcast.431, f32[3,1024]{1,0:T(4,128)S(1)} %get-tuple-element.356, f32[3,1024]{1,0:T(4,128)S(1)} %log_add_fusion.1), kind=kLoop, calls=%fused_computation.6 | loop fusion | flops 12582912 | bytes 31481856 | tf_op jit(solution)/shard_map/convert_element_type | solution.py:707
  416.4 5.0 fusion.136
  423.5 3.4 convert_reduce_fusion.6
  426.9 3.6 multiply_reduce_fusion
  430.5 5.6 multiply_convert_fusion
  436.2 5.7 fusion.137
  450.3 2.7 fusion.165
  455.1 2.7 fusion.164
  457.8 2.7 fusion.352
  461.7 4.2 convert_reduce_fusion.1
  487.1 3.8 convert_reduce_fusion
  491.0 2.4 fusion.384
  493.4 2.6 fusion.166
  517.0 2.8 fusion.356
  519.9 2.3 fusion.379
  530.1 2.4 fusion.385
  533.8 9.5 %fusion.73 = (f32[768]{0:T(1024)}, f32[768]{0:T(1024)}, f32[768]{0:T(1024)}, f32[768]{0:T(1024)}, f32[1024,768]{1,0:T(8,128)}, /*index=5*/f32[1024,768]{1,0:T(8,...) fusion(f32[1024]{0:T(1024)} %get-tuple-element.321, ...), kind=kOutput, calls=%fused_computation.221 | convolution fusion | flops 319288320 | bytes 21183488 | tf_op jit(solution)/shard_map/dot_general | solution.py:279
  550.0 8.9 %fusion.134 = (f32[768]{0:T(1024)}, f32[768]{0:T(1024)}, f32[768]{0:T(1024)}, f32[768]{0:T(1024)}, f32[768]{0:T(1024)}, /*index=5*/f32[768]{0:T(1024)}, f32[768]...) fusion(f32[1024]{0:T(1024)S(1)} %copy-done.215, ...), kind=kOutput, calls=%fused_computation.282 | convolution fusion | flops 328722432 | bytes 11761664 | tf_op jit(solution)/shard_map/dot_general | solution.py:279
  576.3 10.5 %fusion.100 = (f32[768]{0:T(1024)S(1)}, f32[768]{0:T(1024)S(1)}, f32[768]{0:T(1024)S(1)}, f32[768]{0:T(1024)S(1)}, f32[768]{0:T(1024)S(1)}, /*index=5*/f32[768]{...) fusion(bf16[3072,768]{1,0:T(8,128)(2,1)} %hidden_ref.1, ...), kind=kOutput, calls=%fused_computation.248 | convolution fusion | flops 327150336 | bytes 36919296 | tf_op jit(solution)/shard_map/dot_general | solution.py:279
  587.0 7.3 fusion.108
  600.4 54.7 %gradient_scatter.1 = (f32[384,384]{1,0:T(8,128)}, f32[64,384]{1,0:T(8,128)}) custom-call(bf16[16,384,384]{2,1,0:T(8,128)(2,1)} %constant_dynamic-update-slice_fusion.in_ref, f32[64,384]{1,0:T(8,128)} %pad_maximum_fusion.6.small_ref), custom_call_target="tpu_custom_call" | custom-call | tf_op jit(solution)/shard_map/gradient_scatter/pallas_call | solution.py:221
  658.5 13.8 %multiply_multiply_fusion.10 = (f32[1024,768]{1,0:T(8,128)}, f32[1024,768]{1,0:T(8,128)}, f32[1024,768]{1,0:T(8,128)}, f32[1024,768]{1,0:T(8,128)}, f32[1024,768...) fusion(f32[1024,768]{1,0:T(8,128)S(1)} %copy-done.9, ...), kind=kLoop, calls=%fused_computation.293 | loop fusion | flops 15728640 | bytes 37808128 | tf_op jit(solution)/shard_map/mul | solution.py:693
  672.3 12.8 %fusion.32 = f32[1024,768]{1,0:T(8,128)} fusion(f32[1024,768]{1,0:T(8,128)S(1)} %copy-done.30, f32[1024,768]{1,0:T(8,128)S(1)} %copy-done.31, f32[1024,768]{1,0:T(8,128)S(1)} %copy-done.29, f32[1024,768]{1,0:T(8,128)} %get-tuple-element.184, f32[1024,768]{1,0:T(8,128)} %get-tuple-element.183, f32[1024,768]{1,0:T(8,128)} %get-tuple-element.182, ...), kind=kOutput, calls=%fused_computation.180 | convolution fusion | flops 312213504 | bytes 41585664 | tf_op jit(solution)/shard_map/dot_general | solution.py:279
  685.1 2.4 dynamic-slice_convert_fusion.2
  693.0 15.2 %fusion.44 = f32[1024,768]{1,0:T(8,128)} fusion(f32[1024,768]{1,0:T(8,128)} %fusion.383, f32[1024,768]{1,0:T(8,128)} %fusion.382, f32[1024,768]{1,0:T(8,128)} %fusion.381, f32[1024,768]{1,0:T(8,128)} %get-tuple-element.198, f32[1024,768]{1,0:T(8,128)} %get-tuple-element.197, f32[1024,768]{1,0:T(8,128)} %get-tuple-element.196, ...), kind=kOutput, calls=%fused_computation.192 | convolution fusion | flops 312213504 | bytes 41585664 | tf_op jit(solution)/shard_map/dot_general | solution.py:279
  709.8 13.2 %fusion.56 = f32[1024,768]{1,0:T(8,128)} fusion(f32[1024,768]{1,0:T(8,128)} %fusion.386, f32[1024,768]{1,0:T(8,128)} %fusion.385, f32[1024,768]{1,0:T(8,128)} %fusion.384, f32[1024,768]{1,0:T(8,128)S(1)} %copy-done.27, f32[1024,768]{1,0:T(8,128)S(1)} %copy-done.28, f32[1024,768]{1,0:T(8,128)} %get-tuple-element.316, f32[1024,768]{1,0:T(8,128)} %get-tuple-element.317, ...), kind=kOutput, calls=%fused_computation.204 | convolution fusion | flops 312213504 | bytes 41585664 | tf_op jit(solution)/shard_map/dot_general | solution.py:279
  730.0 15.1 %collective-permute-done.8 = bf16[1024,384]{1,0:T(8,128)(2,1)S(1)} collective-permute-done((bf16[1024,384]{1,0:T(8,128)(2,1)S(1)}, bf16[1024,384]{1,0:T(8,128)(2,1)S(1)}, u32[]{:S(2)}, u32[]{:S(2)}) %collective-permute-start.8) | collective-permute-done | bytes 786464 | tf_op jit(solution)/shard_map/ppermute | solution.py:283
  745.1 14.7 %collective-permute-done.6 = bf16[1024,384]{1,0:T(8,128)(2,1)S(1)} collective-permute-done((bf16[1024,384]{1,0:T(8,128)(2,1)S(1)}, bf16[1024,384]{1,0:T(8,128)(2,1)S(1)}, u32[]{:S(2)}, u32[]{:S(2)}) %collective-permute-start.6) | collective-permute-done | bytes 786464 | tf_op jit(solution)/shard_map/ppermute | solution.py:283
  759.8 4.3 convert_add_fusion.2
  764.1 2.5 pad_maximum_fusion
  (817 shorter events, 212.9 us)
Async XLA Ops:
  0.7 44.4 %copy-start = (bf16[192,54]{0,1:T(8,128)(2,1)S(1)}, bf16[192,54]{0,1:T(8,128)(2,1)}, u32[]{:S(2)}) copy-start(bf16[192,54]{0,1:T(8,128)(2,1)} %param.35) | copy-start | bytes 62212
  3.0 23.8 %copy-start.238 = (s32[3,8]{1,0:T(4,128)S(1)}, s32[3,8]{1,0:T(4,128)}, u32[]{:S(2)}) copy-start(s32[3,8]{1,0:T(4,128)} %param.26) | copy-start | bytes 292
  32.1 37.5 %copy-start.10 = (bf16[1024,768]{1,0:T(8,128)(2,1)}, bf16[1024,768]{1,0:T(8,128)(2,1)S(1)}, u32[]{:S(2)}) copy-start(bf16[1024,768]{1,0:T(8,128)(2,1)S(1)} %get-tuple-element.178) | copy-start | bytes 4718596
  34.5 35.0 %copy-start.126 = (f32[768]{0:T(1024)}, f32[768]{0:T(1024)S(1)}, u32[]{:S(2)}) copy-start(f32[768]{0:T(1024)S(1)} %get-tuple-element.157) | copy-start | bytes 9220
  34.6 35.0 %copy-start.170 = (f32[768]{0:T(1024)}, f32[768]{0:T(1024)S(1)}, u32[]{:S(2)}) copy-start(f32[768]{0:T(1024)S(1)} %get-tuple-element.152) | copy-start | bytes 9220
  34.6 35.0 %copy-start.173 = (f32[768]{0:T(1024)}, f32[768]{0:T(1024)S(1)}, u32[]{:S(2)}) copy-start(f32[768]{0:T(1024)S(1)} %get-tuple-element.156) | copy-start | bytes 9220
  34.6 35.0 %copy-start.176 = (f32[768]{0:T(1024)}, f32[768]{0:T(1024)S(1)}, u32[]{:S(2)}) copy-start(f32[768]{0:T(1024)S(1)} %get-tuple-element.158) | copy-start | bytes 9220
  34.6 35.0 %copy-start.179 = (f32[768]{0:T(1024)}, f32[768]{0:T(1024)S(1)}, u32[]{:S(2)}) copy-start(f32[768]{0:T(1024)S(1)} %get-tuple-element.159) | copy-start | bytes 9220
  34.6 35.0 %copy-start.182 = (f32[768]{0:T(1024)}, f32[768]{0:T(1024)S(1)}, u32[]{:S(2)}) copy-start(f32[768]{0:T(1024)S(1)} %get-tuple-element.160) | copy-start | bytes 9220
  34.6 35.0 %copy-start.185 = (f32[768]{0:T(1024)}, f32[768]{0:T(1024)S(1)}, u32[]{:S(2)}) copy-start(f32[768]{0:T(1024)S(1)} %get-tuple-element.155) | copy-start | bytes 9220
  34.6 35.0 %copy-start.188 = (f32[768]{0:T(1024)}, f32[768]{0:T(1024)S(1)}, u32[]{:S(2)}) copy-start(f32[768]{0:T(1024)S(1)} %get-tuple-element.153) | copy-start | bytes 9220
  34.6 35.0 %copy-start.190 = (f32[768]{0:T(1024)}, f32[768]{0:T(1024)S(1)}, u32[]{:S(2)}) copy-start(f32[768]{0:T(1024)S(1)} %get-tuple-element.154) | copy-start | bytes 9220
  46.0 17.9 %copy-start.33 = (bf16[16,48,192]{2,1,0:T(8,128)(2,1)S(1)}, bf16[16,48,192]{2,1,0:T(8,128)(2,1)}, u32[]{:S(2)}) copy-start(bf16[16,48,192]{2,1,0:T(8,128)(2,1)} %get-tuple-element.207) | copy-start | bytes 884740
  46.0 127.6 %collective-permute-start = (f32[1024,27]{0,1:T(8,128)}, f32[1024,27]{0,1:T(8,128)}, u32[]{:S(2)}, u32[]{:S(2)}) collective-permute-start(f32[1024,27]{0,1:T(8,128)} %constant_dynamic-slice_fusion.3), channel_id=1, source_target_pairs={{0,1},{1,0},{2,3},{3,2},{4,5},{5,4},{6,7},{7,6},{8,9},{9,8},{10,11... | collective-permute-start | bytes 331784 | tf_op jit(solution)/shard_map/ppermute | solution.py:283
  49.7 386.4 %copy-start.37 = (bf16[192,1024]{1,0:T(8,128)(2,1)}, bf16[192,1024]{1,0:T(8,128)(2,1)S(1)}, u32[]{:S(2)}) copy-start(bf16[192,1024]{1,0:T(8,128)(2,1)S(1)} %fusion.155) | copy-start | bytes 1179652
  50.1 15.6 %copy-start.195 = (f32[1024]{0:T(1024)}, f32[1024]{0:T(1024)S(1)}, u32[]{:S(2)}) copy-start(f32[1024]{0:T(1024)S(1)} %get-tuple-element.337) | copy-start | bytes 12292
  50.1 15.6 %copy-start.198 = (f32[1024]{0:T(1024)}, f32[1024]{0:T(1024)S(1)}, u32[]{:S(2)}) copy-start(f32[1024]{0:T(1024)S(1)} %get-tuple-element.338) | copy-start | bytes 12292
  50.1 15.6 %copy-start.201 = (f32[1024]{0:T(1024)}, f32[1024]{0:T(1024)S(1)}, u32[]{:S(2)}) copy-start(f32[1024]{0:T(1024)S(1)} %get-tuple-element.339) | copy-start | bytes 12292
  50.2 16.9 %copy-start.46 = (bf16[16,48,192]{2,1,0:T(8,128)(2,1)S(1)}, bf16[16,48,192]{2,1,0:T(8,128)(2,1)}, u32[]{:S(2)}) copy-start(bf16[16,48,192]{2,1,0:T(8,128)(2,1)} %get-tuple-element.210) | copy-start | bytes 884740
  66.5 107.1 %collective-permute-start.2 = (f32[1024,27]{0,1:T(8,128)}, f32[1024,27]{0,1:T(8,128)}, u32[]{:S(2)}, u32[]{:S(2)}) collective-permute-start(f32[1024,27]{0,1:T(8,128)} %constant_dynamic-slice_fusion.1), channel_id=1, source_target_pairs={{0,1},{1,0},{2,3},{3,2},{4,5},{5,4},{6,7},{7,6},{8,9},{9,8},{10,11... | collective-permute-start | bytes 331784 | tf_op jit(solution)/shard_map/ppermute | solution.py:283
  69.2 347.2 %copy-start.39 = (bf16[192,1024]{1,0:T(8,128)(2,1)}, bf16[192,1024]{1,0:T(8,128)(2,1)S(1)}, u32[]{:S(2)}) copy-start(bf16[192,1024]{1,0:T(8,128)(2,1)S(1)} %fusion.153) | copy-start | bytes 1179652
  77.2 96.4 %collective-permute-start.1 = (f32[1024,27]{0,1:T(8,128)}, f32[1024,27]{0,1:T(8,128)}, u32[]{:S(2)}, u32[]{:S(2)}) collective-permute-start(f32[1024,27]{0,1:T(8,128)} %constant_dynamic-slice_fusion.2), channel_id=1, source_target_pairs={{0,1},{1,0},{2,3},{3,2},{4,5},{5,4},{6,7},{7,6},{8,9},{9,8},{10,11... | collective-permute-start | bytes 331784 | tf_op jit(solution)/shard_map/ppermute | solution.py:283
  83.4 72.4 %copy-start.71 = (bf16[192,1024]{1,0:T(8,128)(2,1)}, bf16[192,1024]{1,0:T(8,128)(2,1)S(1)}, u32[]{:S(2)}) copy-start(bf16[192,1024]{1,0:T(8,128)(2,1)S(1)} %convolution_convert_fusion.9) | copy-start | bytes 1179652
  169.7 19.8 %copy-start.129 = (f32[1024]{0:T(1024)S(1)}, f32[1024]{0:T(1024)}, u32[]{:S(2)}) copy-start(f32[1024]{0:T(1024)} %copy-done.128) | copy-start | bytes 12292
  169.7 19.9 %copy-start.132 = (f32[1024]{0:T(1024)S(1)}, f32[1024]{0:T(1024)}, u32[]{:S(2)}) copy-start(f32[1024]{0:T(1024)} %copy-done.131) | copy-start | bytes 12292
  169.7 19.9 %copy-start.135 = (f32[1024]{0:T(1024)S(1)}, f32[1024]{0:T(1024)}, u32[]{:S(2)}) copy-start(f32[1024]{0:T(1024)} %copy-done.134) | copy-start | bytes 12292
  175.0 26.5 %copy-start.96 = (f32[1024,27]{0,1:T(8,128)}, f32[1024,27]{0,1:T(8,128)S(1)}, u32[]{:S(2)}) copy-start(f32[1024,27]{0,1:T(8,128)S(1)} %get-tuple-element.346) | copy-start | bytes 331780
  175.0 26.5 %copy-start.100 = (f32[1024,27]{0,1:T(8,128)}, f32[1024,27]{0,1:T(8,128)S(1)}, u32[]{:S(2)}) copy-start(f32[1024,27]{0,1:T(8,128)S(1)} %get-tuple-element.347) | copy-start | bytes 331780
  175.8 26.7 %copy-start.52 = (f32[192,1024]{1,0:T(8,128)S(1)}, f32[192,1024]{1,0:T(8,128)}, u32[]{:S(2)}) copy-start(f32[192,1024]{1,0:T(8,128)} %convolution_add_fusion) | copy-start | bytes 2359300
  215.7 130.2 %copy-start.83 = (bf16[1024,3,64]{0,2,1:T(8,128)(2,1)S(1)}, bf16[1024,3,64]{0,2,1:T(8,128)(2,1)}, u32[]{:S(2)}) copy-start(bf16[1024,3,64]{0,2,1:T(8,128)(2,1)} %copy-done.82) | copy-start | bytes 1179652
  215.7 132.9 %copy-start.121 = (bf16[3,64,1024]{2,1,0:T(8,128)(2,1)S(1)}, bf16[3,64,1024]{2,1,0:T(8,128)(2,1)}, u32[]{:S(2)}) copy-start(bf16[3,64,1024]{2,1,0:T(8,128)(2,1)} %fusion.158) | copy-start | bytes 1179652
  378.1 19.6 %slice-start.3 = ((s8[12582912]{0:T(1024)(128)(4,1)}), s8[4194304]{0:T(1024)(128)(4,1)S(1)}, s32[]{:S(2)}) async-start(s8[12582912]{0:T(1024)(128)(4,1)} %bitcast.430), calls=%async_computation.3 | async-start | bytes 8388608
  378.1 19.6 %slice-start.4 = ((s8[12582912]{0:T(1024)(128)(4,1)}), s8[4194304]{0:T(1024)(128)(4,1)S(1)}, s32[]{:S(2)}) async-start(s8[12582912]{0:T(1024)(128)(4,1)} %bitcast.430), calls=%async_computation.4 | async-start | bytes 8388608
  400.4 106.8 %copy-start.51 = (bf16[3,64,1024]{2,1,0:T(8,128)(2,1)}, bf16[3,64,1024]{2,1,0:T(8,128)(2,1)S(1)}, u32[]{:S(2)}) copy-start(bf16[3,64,1024]{2,1,0:T(8,128)(2,1)S(1)} %get-tuple-element.368) | copy-start | bytes 1179652
  400.4 23.1 %slice-start = ((s8[12582912]{0:T(1024)(128)(4,1)}), s8[4194304]{0:T(1024)(128)(4,1)S(1)}, s32[]{:S(2)}) async-start(s8[12582912]{0:T(1024)(128)(4,1)} %bitcast.428), calls=%async_computation | async-start | bytes 8388608
  400.4 23.1 %slice-start.1 = ((s8[12582912]{0:T(1024)(128)(4,1)}), s8[4194304]{0:T(1024)(128)(4,1)S(1)}, s32[]{:S(2)}) async-start(s8[12582912]{0:T(1024)(128)(4,1)} %bitcast.428), calls=%async_computation.1 | async-start | bytes 8388608
  407.2 16.3 %slice-start.2 = ((s8[12582912]{0:T(1024)(128)(4,1)}), s8[4194304]{0:T(1024)(128)(4,1)S(1)}, s32[]{:S(2)}) async-start(s8[12582912]{0:T(1024)(128)(4,1)} %bitcast.428), calls=%async_computation.2 | async-start | bytes 8388608
  468.2 75.1 %copy-start.105 = (bf16[1024,27]{0,1:T(8,128)(2,1)}, bf16[1024,27]{0,1:T(8,128)(2,1)S(1)}, u32[]{:S(2)}) copy-start(bf16[1024,27]{0,1:T(8,128)(2,1)S(1)} %multiply_convert_fusion.4) | copy-start | bytes 165892
  468.2 54.8 %collective-permute-start.5 = (bf16[1024,27]{0,1:T(8,128)(2,1)S(1)}, bf16[1024,27]{0,1:T(8,128)(2,1)S(1)}, u32[]{:S(2)}, u32[]{:S(2)}) collective-permute-start(bf16[1024,27]{0,1:T(8,128)(2,1)S(1)} %multiply_convert_fusion.4), channel_id=1, source_target_pairs={{0,1},{1,0},{2,3},{3,2},{4,5},{5,4},{6,7},{7,6},{8,9},{9,8},{10,11... | collective-permute-start | bytes 165896 | tf_op jit(solution)/shard_map/ppermute | solution.py:283
  481.9 62.0 %copy-start.108 = (bf16[1024,27]{0,1:T(8,128)(2,1)}, bf16[1024,27]{0,1:T(8,128)(2,1)S(1)}, u32[]{:S(2)}) copy-start(bf16[1024,27]{0,1:T(8,128)(2,1)S(1)} %multiply_convert_fusion.5) | copy-start | bytes 165892
  481.9 33.2 %collective-permute-start.3 = (bf16[1024,27]{0,1:T(8,128)(2,1)S(1)}, bf16[1024,27]{0,1:T(8,128)(2,1)}, u32[]{:S(2)}, u32[]{:S(2)}) collective-permute-start(bf16[1024,27]{0,1:T(8,128)(2,1)S(1)} %multiply_convert_fusion.5), channel_id=1, source_target_pairs={{0,1},{1,0},{2,3},{3,2},{4,5},{5,4},{6,7},{7,6},{8,9},{9,8},{10,11... | collective-permute-start | bytes 165896 | tf_op jit(solution)/shard_map/ppermute | solution.py:283
  498.3 45.3 %copy-start.107 = (bf16[1024,27]{0,1:T(8,128)(2,1)}, bf16[1024,27]{0,1:T(8,128)(2,1)S(1)}, u32[]{:S(2)}) copy-start(bf16[1024,27]{0,1:T(8,128)(2,1)S(1)} %multiply_convert_fusion.3) | copy-start | bytes 165892
  498.3 29.3 %collective-permute-start.7 = (bf16[1024,27]{0,1:T(8,128)(2,1)S(1)}, bf16[1024,27]{0,1:T(8,128)(2,1)S(1)}, u32[]{:S(2)}, u32[]{:S(2)}) collective-permute-start(bf16[1024,27]{0,1:T(8,128)(2,1)S(1)} %multiply_convert_fusion.3), channel_id=1, source_target_pairs={{0,1},{1,0},{2,3},{3,2},{4,5},{5,4},{6,7},{7,6},{8,9},{9,8},{10,11... | collective-permute-start | bytes 165896 | tf_op jit(solution)/shard_map/ppermute | solution.py:283
  523.0 20.3 %copy-start.115 = (bf16[1024,27]{0,1:T(8,128)(2,1)}, bf16[1024,27]{0,1:T(8,128)(2,1)S(1)}, u32[]{:S(2)}) copy-start(bf16[1024,27]{0,1:T(8,128)(2,1)S(1)} %collective-permute-done.5) | copy-start | bytes 165892
  527.6 15.9 %copy-start.116 = (bf16[1024,27]{0,1:T(8,128)(2,1)}, bf16[1024,27]{0,1:T(8,128)(2,1)S(1)}, u32[]{:S(2)}) copy-start(bf16[1024,27]{0,1:T(8,128)(2,1)S(1)} %collective-permute-done.7) | copy-start | bytes 165892
  599.7 58.6 %copy-start.9 = (f32[1024,768]{1,0:T(8,128)S(1)}, f32[1024,768]{1,0:T(8,128)}, u32[]{:S(2)}) copy-start(f32[1024,768]{1,0:T(8,128)} %copy-done.8) | copy-start | bytes 9437188
  599.7 58.7 %copy-start.172 = (f32[768]{0:T(1024)S(1)}, f32[768]{0:T(1024)}, u32[]{:S(2)}) copy-start(f32[768]{0:T(1024)} %copy-done.170) | copy-start | bytes 9220
  599.7 58.7 %copy-start.175 = (f32[768]{0:T(1024)S(1)}, f32[768]{0:T(1024)}, u32[]{:S(2)}) copy-start(f32[768]{0:T(1024)} %copy-done.173) | copy-start | bytes 9220
  599.7 58.7 %copy-start.178 = (f32[768]{0:T(1024)S(1)}, f32[768]{0:T(1024)}, u32[]{:S(2)}) copy-start(f32[768]{0:T(1024)} %copy-done.176) | copy-start | bytes 9220
  599.7 58.7 %copy-start.181 = (f32[768]{0:T(1024)S(1)}, f32[768]{0:T(1024)}, u32[]{:S(2)}) copy-start(f32[768]{0:T(1024)} %copy-done.179) | copy-start | bytes 9220
  599.7 58.7 %copy-start.184 = (f32[768]{0:T(1024)S(1)}, f32[768]{0:T(1024)}, u32[]{:S(2)}) copy-start(f32[768]{0:T(1024)} %copy-done.182) | copy-start | bytes 9220
  599.7 58.7 %copy-start.187 = (f32[768]{0:T(1024)S(1)}, f32[768]{0:T(1024)}, u32[]{:S(2)}) copy-start(f32[768]{0:T(1024)} %copy-done.185) | copy-start | bytes 9220
  599.7 58.7 %copy-start.194 = (f32[1024]{0:T(1024)S(1)}, f32[1024]{0:T(1024)}, u32[]{:S(2)}) copy-start(f32[1024]{0:T(1024)} %copy-done.192) | copy-start | bytes 12292
  599.7 58.7 %copy-start.197 = (f32[1024]{0:T(1024)S(1)}, f32[1024]{0:T(1024)}, u32[]{:S(2)}) copy-start(f32[1024]{0:T(1024)} %copy-done.195) | copy-start | bytes 12292
  599.8 58.7 %copy-start.200 = (f32[1024]{0:T(1024)S(1)}, f32[1024]{0:T(1024)}, u32[]{:S(2)}) copy-start(f32[1024]{0:T(1024)} %copy-done.198) | copy-start | bytes 12292
  599.8 58.7 %copy-start.203 = (f32[1024]{0:T(1024)S(1)}, f32[1024]{0:T(1024)}, u32[]{:S(2)}) copy-start(f32[1024]{0:T(1024)} %copy-done.201) | copy-start | bytes 12292
  687.5 42.5 %collective-permute-start.4 = (bf16[1024,384]{1,0:T(8,128)(2,1)}, bf16[1024,384]{1,0:T(8,128)(2,1)}, u32[]{:S(2)}, u32[]{:S(2)}) collective-permute-start(bf16[1024,384]{1,0:T(8,128)(2,1)} %dynamic-slice_convert_fusion.2), channel_id=1, source_target_pairs={{0,1},{1,0},{2,3},{3,2},{4,5},{5,4},{6,7},{7,6},{8,9},{9,8},{10,11... | collective-permute-start | bytes 2359304 | tf_op jit(solution)/shard_map/ppermute | solution.py:283
  693.0 16.7 %copy-start.26 = (f32[1024,768]{1,0:T(8,128)S(1)}, f32[1024,768]{1,0:T(8,128)}, u32[]{:S(2)}) copy-start(f32[1024,768]{1,0:T(8,128)} %get-tuple-element.360) | copy-start | bytes 9437188
  693.0 16.7 %copy-start.27 = (f32[1024,768]{1,0:T(8,128)S(1)}, f32[1024,768]{1,0:T(8,128)}, u32[]{:S(2)}) copy-start(f32[1024,768]{1,0:T(8,128)} %get-tuple-element.314) | copy-start | bytes 9437188
  693.0 16.7 %copy-start.28 = (f32[1024,768]{1,0:T(8,128)S(1)}, f32[1024,768]{1,0:T(8,128)}, u32[]{:S(2)}) copy-start(f32[1024,768]{1,0:T(8,128)} %get-tuple-element.315) | copy-start | bytes 9437188
  709.8 19.5 %copy-start.114 = (f32[384,384]{1,0:T(8,128)S(1)}, f32[384,384]{1,0:T(8,128)}, u32[]{:S(2)}) copy-start(f32[384,384]{1,0:T(8,128)} %get-tuple-element.38) | copy-start | bytes 1769476
  709.8 50.0 %copy-start.41 = (f32[1024,768]{1,0:T(8,128)S(1)}, f32[1024,768]{1,0:T(8,128)}, u32[]{:S(2)}) copy-start(f32[1024,768]{1,0:T(8,128)} %fusion.32) | copy-start | bytes 9437188
  724.5 20.5 %collective-permute-start.8 = (bf16[1024,384]{1,0:T(8,128)(2,1)S(1)}, bf16[1024,384]{1,0:T(8,128)(2,1)S(1)}, u32[]{:S(2)}, u32[]{:S(2)}) collective-permute-start(bf16[1024,384]{1,0:T(8,128)(2,1)S(1)} %dynamic-slice_convert_fusion), channel_id=1, source_target_pairs={{0,1},{1,0},{2,3},{3,2},{4,5},{5,4},{6,7},{7,6},{8,9},{9,8},{10,11... | collective-permute-start | bytes 2359304 | tf_op jit(solution)/shard_map/ppermute | solution.py:283
  726.1 33.7 %collective-permute-start.6 = (bf16[1024,384]{1,0:T(8,128)(2,1)S(1)}, bf16[1024,384]{1,0:T(8,128)(2,1)S(1)}, u32[]{:S(2)}, u32[]{:S(2)}) collective-permute-start(bf16[1024,384]{1,0:T(8,128)(2,1)S(1)} %dynamic-slice_convert_fusion.1), channel_id=1, source_target_pairs={{0,1},{1,0},{2,3},{3,2},{4,5},{5,4},{6,7},{7,6},{8,9},{9,8},{10,11... | collective-permute-start | bytes 2359304 | tf_op jit(solution)/shard_map/ppermute | solution.py:283
  (202 other events, 1203.5 us)

commit v2 on v1

--- a/solution.py
+++ b/solution.py
@@ -263,10 +263,6 @@
         self.__dict__.update(parts)
 
 
-def total_of(groups):
-    return Group(**{k: sum(vars(g)[k] for g in groups) for k in vars(groups[0])})
-
-
 def nn(left, right):
     return jnp.dot(left, right, preferred_element_type=F32)
 
@@ -328,50 +324,290 @@
     return jnp.where(me == 0, jnp.concatenate([own, other], 1), jnp.concatenate([other, own], 1))
 
 
-def part_a(rows_in, segment, w, p, me):
-    seq_rows = rows_in.shape[0]
-    width = w.query.shape[1]
-    heads = width // HEAD_DIM
-    queries = (nn(rows_in, w.query) + p.query_bias).astype(BF16)
-    keys = nn(rows_in, w.key).astype(BF16)
-    values = (nn(rows_in, w.value) + p.value_bias).astype(BF16)
-    masks = tap_mask_list(segment)
-    depthwise = jnp.zeros(rows_in.shape, F32)
-    for tap in range(KERNEL):
-        moved = shifted(rows_in, tap - HALF, HALF).astype(F32)
-        depthwise = depthwise + w.depth[tap].astype(F32) * moved * masks[tap]
-    depthwise = depthwise.astype(BF16)
-    key_conv = nn(depthwise, w.point) + p.point_bias
-    conv_attn = (key_conv * queries.astype(F32)).astype(BF16)
-    own, other = halves(nn(conv_attn, p.kernel_weight), me)
-    logits = own + swap(other) + halves(p.kernel_bias[None], me)[0]
-    kernel_probs = jax.nn.softmax(logits.reshape(seq_rows, heads, KERNEL), axis=-1)
-    conv_values = (nn(rows_in, w.conv) + p.conv_bias).reshape(seq_rows, heads, HEAD_DIM)
-    conv_context = jnp.zeros((seq_rows, heads, HEAD_DIM), F32)
-    for tap in range(KERNEL):
-        now = kernel_probs[:, :, tap] * masks[tap]
-        conv_context = conv_context + now[:, :, None] * shifted(conv_values, tap - HALF, HALF)
-    conv_context = conv_context.reshape(seq_rows, width).astype(BF16)
-    query_heads = queries.reshape(seq_rows, heads, HEAD_DIM)
-    key_heads = keys.reshape(seq_rows, heads, HEAD_DIM)
-    value_heads = values.reshape(seq_rows, heads, HEAD_DIM)
-    scores = jnp.einsum("qhd,khd->hqk", query_heads, key_heads, preferred_element_type=F32) * 0.125
-    scores = jnp.where((segment[:, None] == segment[None, :])[None], scores, MASK_FILL)
-    top = jnp.max(scores, axis=-1, keepdims=True)
-    exponent = jnp.exp(scores - top)
-    total = jnp.sum(exponent, axis=-1, keepdims=True)
-    probs_low = (exponent / total).astype(BF16)
-    context = jnp.einsum("hqk,khd->qhd", probs_low, value_heads, preferred_element_type=F32)
-    context = context.reshape(seq_rows, width).astype(BF16)
-    log_total = top[:, :, 0] + jnp.log(total[:, :, 0])
-    return (queries, keys, values, depthwise, key_conv, conv_attn, kernel_probs, conv_values, conv_context, context, log_total)
-
-
 def moments(sum_own, square_own, sum_other, square_other, width):
     mean = (sum_own + sum_other) / (2 * width)
     apart = (sum_own - sum_other) / width
     spread = (square_own + square_other + apart * apart * (width / 2)) / (2 * width)
     return mean, lax.rsqrt(spread + EPSILON)
+
+
+TAP_ROWS = 16
+WIDE = 256
+LANES = 128
+EDGE = 8
+
+
+def spread_marks(marks_ref, columns_ref, masks_ref):
+    rows = marks_ref.shape[2]
+    columns_ref[...] = jnp.transpose(
+        jnp.concatenate([marks_ref[0], jnp.zeros((LANES - TAP_ROWS, rows), F32)], 0)
+    )
+    for tap in range(KERNEL):
+        masks_ref[tap] = jnp.broadcast_to(columns_ref[:, tap : tap + 1], (rows, LANES))
+
+
+def head_lanes(head):
+    lane = lax.broadcasted_iota(jnp.int32, (1, WIDE), 1)
+    return jnp.logical_and(lane >= head * HEAD_DIM, lane < (head + 1) * HEAD_DIM)
+
+
+def only(value, head):
+    return jnp.where(head_lanes(head), value.astype(F32), 0.0)
+
+
+def high_low(weights, heads):
+    high = weights.astype(BF16).astype(F32)
+    low = weights - high
+    rest = jnp.zeros((LANES - 2 * heads * TAP_ROWS, weights.shape[1]), F32)
+    return jnp.transpose(jnp.concatenate([high, low, rest], 0)).astype(BF16)
+
+
+def front_kernel(
+    seqs, count,
+    hidden_ref, marks_ref, query_ref, key_ref, value_ref, conv_ref, point_ref, taps_ref, vec_ref, depth_ref, bias_ref,
+    expand_ref, second_ref,
+    q_ref, k_ref, v_ref, cv_ref, dl_ref, kc_ref, ca_ref, probs_ref, cc_ref, ctx_ref, lse_ref, second_all_ref,
+    rows_pad, conv_pad, masks, columns, weights, tops, tap_out, tap_in,
+    send_sem, recv_sem, own_sem, gather_send, gather_recv,
+):
+    s = pl.program_id(0)
+    mp, core, side, deep, parts = places(count)
+    me = index_of(deep, side, core)
+    rows, model = hidden_ref.shape
+    chunks = model // LANES
+    heads = probs_ref.shape[1] // TAP_ROWS
+    tap_rows = heads * TAP_ROWS
+    beside = index_of(deep, 1 - side, core)
+    twin = index_of(deep, side, 1 - core)
+
+    def push(source, block, target, slot):
+        return pltpu.make_async_remote_copy(
+            src_ref=source,
+            dst_ref=second_all_ref.at[block],
+            send_sem=gather_send.at[slot],
+            recv_sem=gather_recv.at[block],
+            device_id=at(target, mp),
+            device_id_type=MESH,
+        )
+
+    def arrive(block):
+        pltpu.make_async_copy(second_ref.at[0], second_all_ref.at[block], gather_recv.at[block]).wait()
+
+    own_copy = pltpu.make_async_copy(second_ref.at[0], second_all_ref.at[me], own_sem)
+    first_hops = [
+        push(second_ref.at[0], me, index_of(lax.rem(deep + k, parts), side, core), k - 1) for k in range(1, parts)
+    ]
+    first_hops += [push(second_ref.at[0], me, beside, parts - 1), push(second_ref.at[0], me, twin, parts)]
+    second_hops = [(beside, twin, parts + 1)]
+    for k in range(1, parts):
+        block = index_of(lax.rem(deep + parts - k, parts), side, core)
+        second_hops += [(block, beside, parts + 2 * k), (block, twin, parts + 2 * k + 1)]
+    third_hops = [
+        (index_of(lax.rem(deep + parts - k, parts), 1 - side, core), twin, 3 * parts + k - 1) for k in range(1, parts)
+    ]
+
+    @pl.when(s == 0)
+    def _():
+        barrier = pltpu.get_barrier_semaphore()
+        pl.semaphore_signal(barrier, inc=1, device_id=at(me, 1 - mp), device_id_type=MESH)
+        peers = [index_of(lax.rem(deep + k, parts), side, core) for k in range(1, parts)] + [beside, twin]
+        for peer in peers:
+            pl.semaphore_signal(barrier, inc=1, device_id=at(peer, mp), device_id_type=MESH)
+        pl.semaphore_wait(barrier, len(peers) + 1)
+        own_copy.start()
+        for copy in first_hops:
+            copy.start()
+        rows_pad[:, :EDGE, :] = jnp.zeros((chunks, EDGE, LANES), F32)
+        rows_pad[:, pl.ds(EDGE + rows, EDGE), :] = jnp.zeros((chunks, EDGE, LANES), F32)
+        conv_pad[:, :EDGE, :] = jnp.zeros((2, EDGE, LANES), F32)
+        conv_pad[:, pl.ds(EDGE + rows, EDGE), :] = jnp.zeros((2, EDGE, LANES), F32)
+
+    spread_marks(marks_ref, columns, masks)
+    hidden = hidden_ref[...]
+    for c in range(chunks):
+        rows_pad[c, pl.ds(EDGE, rows), :] = hidden[:, c * LANES : (c + 1) * LANES].astype(F32)
+
+    step = 32
+
+    def depth_step(i, carry):
+        base = pl.multiple_of(i * step, step)
+        total = [jnp.zeros((step, LANES), F32)] * chunks
+        for tap in range(KERNEL):
+            mask = masks[tap, pl.ds(base, step), :]
+            for c in range(chunks):
+                moved = rows_pad[c, pl.ds(base + EDGE + tap - HALF, step), :]
+                total[c] = total[c] + (moved * mask) * depth_ref[tap : tap + 1, c * LANES : (c + 1) * LANES]
+        for c in range(chunks):
+            dl_ref[pl.ds(base, step), c * LANES : (c + 1) * LANES] = total[c].astype(BF16)
+        return carry
+
+    lax.fori_loop(0, rows // step, depth_step, 0)
+    queries = (nn(hidden, query_ref[...]) + vec_ref[0:1, :]).astype(BF16)
+    q_ref[...] = queries
+    key_conv = nn(dl_ref[...], point_ref[...]) + vec_ref[2:3, :]
+    kc_ref[...] = key_conv
+    conv_attn = (key_conv * queries.astype(F32)).astype(BF16)
+    ca_ref[...] = conv_attn
+    tap_terms = nt(taps_ref[...], conv_attn)
+    slot = lax.rem(s, 2)
+    tap_out[slot] = tap_terms[tap_rows : 2 * tap_rows]
+    swap_taps = pltpu.make_async_remote_copy(
+        src_ref=tap_out.at[slot],
+        dst_ref=tap_in.at[slot],
+        send_sem=send_sem.at[slot],
+        recv_sem=recv_sem.at[slot],
+        device_id=at(me, 1 - mp),
+        device_id_type=MESH,
+    )
+    swap_taps.start()
+    own_terms = tap_terms[:tap_rows]
+    k_ref[...] = nn(hidden, key_ref[...]).astype(BF16)
+    v_ref[...] = (nn(hidden, value_ref[...]) + vec_ref[1:2, :]).astype(BF16)
+    conv_values = nn(hidden, conv_ref[...]) + vec_ref[3:4, :]
+    cv_ref[...] = conv_values
+    for c in range(2):
+        conv_pad[c, pl.ds(EDGE, rows), :] = conv_values[:, c * LANES : (c + 1) * LANES]
+
+    block = 256
+    seg_row = marks_ref[0, KERNEL : KERNEL + 1, :]
+    lane = lax.broadcasted_iota(jnp.int32, (block, LANES), 1)
+
+    def attention_step(i, carry):
+        part = pl.ds(pl.multiple_of(i * block, block), block)
+        allowed = columns[part, KERNEL : KERNEL + 1] == seg_row
+        query = q_ref[part, :]
+        total = jnp.zeros((block, WIDE), F32)
+        packed = jnp.zeros((block, LANES), F32)
+        for head in range(heads):
+            mine = (only(query, head) * (HEAD_DIM**-0.5)).astype(BF16)
+            scores = jnp.where(allowed, nt(mine, k_ref[...]), MASK_FILL)
+            top = jnp.max(scores, axis=1, keepdims=True)
+            exponent = jnp.exp(scores - top)
+            amount = jnp.sum(exponent, axis=1, keepdims=True)
+            probs = (exponent * (1.0 / amount)).astype(BF16)
+            total = total + nn(probs, only(v_ref[...], head).astype(BF16))
+            packed = jnp.where(lane == head, top + jnp.log(amount), packed)
+        ctx_ref[part, :] = total.astype(BF16)
+        tops[part, :] = packed
+        return carry
+
+    lax.fori_loop(0, rows // block, attention_step, 0)
+    lse_ref[0] = jnp.transpose(tops[...])[:8]
+
+    swap_taps.wait()
+    logits = (own_terms + tap_in[slot] + bias_ref[:, :1]).reshape(heads, TAP_ROWS, rows)
+    tap = lax.broadcasted_iota(jnp.int32, (heads, TAP_ROWS, rows), 1)
+    logits = jnp.where(tap < KERNEL, logits, MASK_FILL)
+    exponent = jnp.exp(logits - jnp.max(logits, axis=1, keepdims=True))
+    probs = exponent / jnp.sum(exponent, axis=1, keepdims=True)
+    probs_ref[0] = probs.reshape(tap_rows, rows)
+    tap_mask = jnp.where(tap[0] < KERNEL, marks_ref[0], 0.0)
+    weights[...] = high_low((probs * tap_mask[None]).reshape(tap_rows, rows), heads)
+    conv_block = 128
+
+    def conv_step(i, carry):
+        base = pl.multiple_of(i * conv_block, conv_block)
+        part = pl.ds(base, conv_block)
+        scale = nn(weights[part, :], expand_ref[...])
+        for c in range(2):
+            total = jnp.zeros((conv_block, LANES), F32)
+            for tap in range(KERNEL):
+                low = tap * WIDE + c * LANES
+                moved = conv_pad[c, pl.ds(base + EDGE + tap - HALF, conv_block), :]
+                total = total + scale[:, low : low + LANES] * moved
+            cc_ref[part, c * LANES : (c + 1) * LANES] = total.astype(BF16)
+        return carry
+
+    lax.fori_loop(0, rows // conv_block, conv_step, 0)
+
+    @pl.when(s == 0)
+    def _():
+        for block, target, place in second_hops:
+            if target is twin and place == parts + 1:
+                arrive(block)
+            elif target is beside:
+                arrive(block)
+            push(second_all_ref.at[block], block, target, place).start()
+
+    @pl.when(s == min(1, seqs - 1))
+    def _():
+        for block, target, place in third_hops:
+            arrive(block)
+            push(second_all_ref.at[block], block, target, place).start()
+
+    @pl.when(s == seqs - 1)
+    def _():
+        for k in range(parts):
+            for other in range(2):
+                arrive(index_of(lax.rem(deep + parts - k, parts), other, 1 - core))
+        for copy in first_hops:
+            copy.wait_send()
+        for block, target, place in second_hops + third_hops:
+            push(second_all_ref.at[block], block, target, place).wait_send()
+        own_copy.wait()
+
+
+def whole():
+    return pl.BlockSpec(memory_space=pltpu.VMEM)
+
+
+def by_seq(rows, columns):
+    return pl.BlockSpec((rows, columns), lambda s: (s, 0))
+
+
+def by_seq_row(rows, columns):
+    return pl.BlockSpec((1, rows, columns), lambda s: (s, 0, 0))
+
+
+def front(hidden, marks, w, vectors, depth, bias, expand, taps, second, count, ident):
+    seqs, _, rows = marks.shape
+    tokens, model = hidden.shape
+    tap_rows = bias.shape[0]
+    parts = count // 4
+
+    def wide(kind):
+        return jax.ShapeDtypeStruct((tokens, WIDE), kind)
+
+    return pl.pallas_call(
+        functools.partial(front_kernel, seqs, count),
+        grid=(seqs,),
+        out_shape=(
+            wide(BF16), wide(BF16), wide(BF16), wide(F32),
+            jax.ShapeDtypeStruct((tokens, model), BF16),
+            wide(F32), wide(BF16),
+            jax.ShapeDtypeStruct((seqs, tap_rows, rows), F32),
+            wide(BF16), wide(BF16),
+            jax.ShapeDtypeStruct((seqs, 8, rows), F32),
+            jax.ShapeDtypeStruct((count,) + second.shape[1:], BF16),
+        ),
+        in_specs=[by_seq(rows, model), by_seq_row(TAP_ROWS, rows)] + [whole()] * 10 + [pl.BlockSpec(memory_space=pl.ANY)],
+        out_specs=(
+            by_seq(rows, WIDE), by_seq(rows, WIDE), by_seq(rows, WIDE), by_seq(rows, WIDE), by_seq(rows, model),
+            by_seq(rows, WIDE), by_seq(rows, WIDE), by_seq_row(tap_rows, rows), by_seq(rows, WIDE), by_seq(rows, WIDE),
+            by_seq_row(8, rows), pl.BlockSpec(memory_space=pl.ANY),
+        ),
+        scratch_shapes=[
+            pltpu.VMEM((model // LANES, rows + 2 * EDGE, LANES), F32),
+            pltpu.VMEM((2, rows + 2 * EDGE, LANES), F32),
+            pltpu.VMEM((KERNEL, rows, LANES), F32),
+            pltpu.VMEM((rows, LANES), F32),
+            pltpu.VMEM((rows, LANES), BF16),
+            pltpu.VMEM((rows, LANES), F32),
+            pltpu.VMEM((2, tap_rows, rows), F32),
+            pltpu.VMEM((2, tap_rows, rows), F32),
+            pltpu.SemaphoreType.DMA((2,)),
+            pltpu.SemaphoreType.DMA((2,)),
+            pltpu.SemaphoreType.DMA,
+            pltpu.SemaphoreType.DMA((4 * parts - 1,)),
+            pltpu.SemaphoreType.DMA((count,)),
+        ],
+        compiler_params=pltpu.CompilerParams(
+            collective_id=ident, has_side_effects=True, vmem_limit_bytes=60 << 20
+        ),
+        name="front",
+    )(
+        hidden, marks, w.query, w.key, w.value, w.conv, w.point, taps, vectors, depth, bias, expand, second,
+    )
 
 
 def transposed_stats(columns):
@@ -401,9 +637,9 @@
 
 def middle_kernel(
     blocks,
-    context_ref, conv_ref, hidden_ref, grad_ref, grad_late_ref, out0_ref, out1_ref, inner_ref, outer_ref, vec_ref,
-    output_ref, residual_ref, branch_ref, big_inner_ref, big_outer_ref, small_ref,
-    state, scale_ring, act_ring, slope_ring, low_ring, summed_ring, normed_ring, stat_ring,
+    context_ref, conv_ref, context_late_ref, conv_late_ref, hidden_ref, grad_ref, grad_late_ref, out0_ref, out1_ref, inner_ref, outer_ref, vec_ref,
+    output_ref, residual_ref, grad_context_ref, grad_conv_ref, big_inner_ref, big_outer_ref, big_out_ref, small_ref,
+    branch_ref, acc_out0, acc_out1, state, scale_ring, act_ring, slope_ring, low_ring, summed_ring, normed_ring, stat_ring,
     acc_inner, acc_outer, acc_small, acc_bias,
     branch_out, branch_in, stat1_out, stat1_in, stat2_out, stat2_in, stat3_out, stat3_in, back_out, back_in,
     send_sem, recv_sem,
@@ -444,6 +680,8 @@
         pl.semaphore_wait(barrier, 1)
         acc_inner[...] = jnp.zeros_like(acc_inner)
         acc_outer[...] = jnp.zeros_like(acc_outer)
+        acc_out0[...] = jnp.zeros_like(acc_out0)
+        acc_out1[...] = jnp.zeros_like(acc_out1)
         acc_small[...] = jnp.zeros_like(acc_small)
         acc_bias[...] = jnp.zeros_like(acc_bias)
 
@@ -579,6 +817,11 @@
         ours = pl.ds(pl.multiple_of(me * width, width), width)
         branch_ref[:, ours] = back_out[slot]
         branch_ref[:, theirs] = back_in[slot]
+        branch = branch_ref[...]
+        grad_context_ref[...] = nn(branch, out0_ref[...]).astype(BF16)
+        grad_conv_ref[...] = nn(branch, out1_ref[...]).astype(BF16)
+        acc_out0[...] += tn(branch, context_late_ref[...])
+        acc_out1[...] += tn(branch, conv_late_ref[...])
 
     @pl.when(i == blocks + 4)
     def _():
@@ -587,6 +830,7 @@
                 message(kind, *kinds[kind], slot).wait_send()
         big_inner_ref[...] = acc_inner[...].astype(BF16)
         big_outer_ref[...] = acc_outer[...].astype(BF16)
+        big_out_ref[...] = jnp.concatenate([acc_out0[:, : width // 2], acc_out1[:, : width // 2]], 1).astype(BF16)
         small_ref[...] = jnp.zeros_like(small_ref)
         for row in range(6):
             small_ref[row : row + 1, :width] = jnp.sum(acc_small[row], axis=0, keepdims=True)
@@ -621,17 +865,23 @@
         out_shape=(
             jax.ShapeDtypeStruct((tokens, width), BF16),
             jax.ShapeDtypeStruct((tokens, width), F32),
-            jax.ShapeDtypeStruct((tokens, model), BF16),
+            jax.ShapeDtypeStruct((tokens, local), BF16),
+            jax.ShapeDtypeStruct((tokens, local), BF16),
             jax.ShapeDtypeStruct((units, width), BF16),
             jax.ShapeDtypeStruct((units, width), BF16),
+            jax.ShapeDtypeStruct((model, width), BF16),
             jax.ShapeDtypeStruct((8, units), F32),
         ),
         in_specs=[
-            block(local, 0), block(local, 0), block(model, 0), block(width, 2), block(width, 3),
+            block(local, 0), block(local, 0), block(local, 5), block(local, 5), block(model, 0), block(width, 2),
+            block(width, 3),
             whole, whole, whole, whole, whole,
         ],
-        out_specs=(block(width, 3), block(width, 4), block(model, 5), whole, whole, whole),
+        out_specs=(block(width, 3), block(width, 4), block(local, 5), block(local, 5), whole, whole, whole, whole),
         scratch_shapes=[
+            pltpu.VMEM((rows, model), BF16),
+            pltpu.VMEM((model, local), F32),
+            pltpu.VMEM((model, local), F32),
             pltpu.VMEM((8, rows, width), F32),
             pltpu.VMEM((4, rows, 128), F32),
             pltpu.VMEM((2, rows, units), BF16),
@@ -652,74 +902,277 @@
             collective_id=ident, has_side_effects=True, vmem_limit_bytes=60 << 20
         ),
         name="middle",
-    )(context, conv_context, hidden, out_grad, out_grad, w.out0, w.out1, w.inner, w.outer, table)
-
-
-def part_c(rows_in, segment, grad_branch, grad_residual, kept, w, p, me):
-    (queries, keys, values, depthwise, key_conv, conv_attn, kernel_probs, conv_values, conv_context, context, log_total) = kept
-    seq_rows = rows_in.shape[0]
-    width = queries.shape[1]
-    heads = width // HEAD_DIM
-    masks = tap_mask_list(segment)
-    big = Group(out0=tn(grad_branch, context), out1=tn(grad_branch, conv_context))
-    small = Group()
-    grad_context = nn(grad_branch, w.out0).astype(BF16).reshape(seq_rows, heads, HEAD_DIM)
-    grad_conv = nn(grad_branch, w.out1).astype(BF16).reshape(seq_rows, heads, HEAD_DIM)
-    tap_grads = []
-    grad_conv_values = jnp.zeros((seq_rows, heads, HEAD_DIM), F32)
-    for tap in range(KERNEL):
-        tap_grads.append(
-            masks[tap] * jnp.sum(grad_conv * shifted(conv_values, tap - HALF, HALF), axis=2)
-        )
-        now = kernel_probs[:, :, tap] * masks[tap]
-        grad_conv_values = grad_conv_values + shifted(now[:, :, None] * grad_conv, HALF - tap, HALF)
-    grad_taps = jnp.stack(tap_grads, axis=2)
-    grad_logits = kernel_probs * (grad_taps - jnp.sum(kernel_probs * grad_taps, axis=2, keepdims=True))
-    logits_own = grad_logits.reshape(seq_rows, heads * KERNEL).astype(BF16)
-    logits_low = joined(logits_own, swap(logits_own), me)
-    small.kernel_bias = jnp.sum(logits_low, axis=0, dtype=F32)
-    small.kernel_weight = tn(conv_attn, logits_low)
-    attn_wide = nt(logits_low, p.kernel_weight).astype(BF16).astype(F32)
-    key_low = (attn_wide * queries.astype(F32)).astype(BF16)
-    small.point_bias = jnp.sum(key_low, axis=0, dtype=F32)
-    big.point = tn(depthwise, key_low)
-    grad_depthwise = nt(key_low, w.point)
-    depth_rows = []
-    grad_rows = jnp.zeros(rows_in.shape, F32)
-    for tap in range(KERNEL):
-        masked = grad_depthwise * masks[tap]
-        moved = shifted(rows_in, tap - HALF, HALF).astype(F32)
-        depth_rows.append(jnp.sum(masked * moved, axis=0))
-        grad_rows = grad_rows + shifted(masked * w.depth[tap].astype(F32), HALF - tap, HALF)
-    small.depth = jnp.stack(depth_rows, axis=0)
-    conv_low = grad_conv_values.reshape(seq_rows, width).astype(BF16)
-    small.conv_bias = jnp.sum(conv_low, axis=0, dtype=F32)
-    big.conv = tn(rows_in, conv_low)
-    grad_rows = grad_rows + nt(conv_low, w.conv)
-    query_heads = queries.reshape(seq_rows, heads, HEAD_DIM)
-    key_heads = keys.reshape(seq_rows, heads, HEAD_DIM)
-    value_heads = values.reshape(seq_rows, heads, HEAD_DIM)
-    scores = jnp.einsum("qhd,khd->hqk", query_heads, key_heads, preferred_element_type=F32) * 0.125
-    scores = jnp.where((segment[:, None] == segment[None, :])[None], scores, MASK_FILL)
-    probs = jnp.exp(scores - log_total[:, :, None])
-    probs_low = probs.astype(BF16)
-    grad_probs = jnp.einsum("qhd,khd->hqk", grad_context, value_heads, preferred_element_type=F32)
-    scores_low = (probs * (grad_probs - jnp.sum(probs * grad_probs, axis=2, keepdims=True))).astype(BF16)
-    grad_queries = jnp.einsum("hqk,khd->qhd", scores_low, key_heads, preferred_element_type=F32) * 0.125
-    grad_queries = (grad_queries.reshape(seq_rows, width) + attn_wide * key_conv).astype(BF16)
-    grad_keys = jnp.einsum("hqk,qhd->khd", scores_low, query_heads, preferred_element_type=F32) * 0.125
-    grad_keys = grad_keys.reshape(seq_rows, width).astype(BF16)
-    grad_values = jnp.einsum("hqk,qhd->khd", probs_low, grad_context, preferred_element_type=F32)
-    grad_values = grad_values.reshape(seq_rows, width).astype(BF16)
-    small.query_bias = jnp.sum(grad_queries, axis=0, dtype=F32)
-    small.value_bias = jnp.sum(grad_values, axis=0, dtype=F32)
-    big.query = tn(rows_in, grad_queries)
-    big.key = tn(rows_in, grad_keys)
-    big.value = tn(rows_in, grad_values)
-    grad_rows = grad_rows + nt(grad_queries, w.query) + nt(grad_keys, w.key) + nt(grad_values, w.value)
-    own, other = halves(grad_rows, me)
-    grad_input = own + grad_residual + swap(other.astype(BF16)).astype(F32)
-    return grad_input, big, small
+    )(context, conv_context, context, conv_context, hidden, out_grad, out_grad, w.out0, w.out1, w.inner, w.outer, table)
+
+
+def back_kernel(
+    seqs,
+    hidden_ref, grad_context, grad_conv_ref, residual_ref, marks_ref, q_ref, k_ref, v_ref, cv_ref, dl_ref, kc_ref, ca_ref, probs_ref,
+    lse_ref,
+    inputs_ref, point_ref, taps_ref, depth_ref, expand_ref, gather_ref,
+    own_ref, other_ref, big_qk_ref, big_vc_ref, big_point_ref, bias_ref, tap_grad_ref, tap_bias_ref, depth_grad_ref,
+    depth_pad, conv_pad, grad_pad, masks, columns, weights, shifted_weights, tap_terms, products,
+    grads, grad_q, grad_k, grad_v, rows_total, tap_all,
+    acc_in, acc_point, acc_bias, acc_tap, acc_tap_bias, acc_depth,
+    tap_out, tap_in, send_sem, recv_sem,
+):
+    s = pl.program_id(0)
+    mp = lax.axis_index("mp")
+    dp = lax.axis_index("dp")
+    rows, model = hidden_ref.shape
+    chunks = model // LANES
+    heads = probs_ref.shape[1] // TAP_ROWS
+    tap_rows = heads * TAP_ROWS
+    half = chunks // 2
+    slot = lax.rem(s, 2)
+
+    @pl.when(s == 0)
+    def _():
+        barrier = pltpu.get_barrier_semaphore()
+        pl.semaphore_signal(barrier, inc=1, device_id=(dp, 1 - mp), device_id_type=MESH)
+        pl.semaphore_wait(barrier, 1)
+        for pad in (depth_pad, conv_pad, grad_pad):
+            for start in (0, EDGE + rows):
+                pad[:, pl.ds(start, EDGE), :] = jnp.zeros((pad.shape[0], EDGE, LANES), F32)
+        for acc in (acc_in, acc_point, acc_bias, acc_tap, acc_tap_bias, acc_depth):
+            acc[...] = jnp.zeros_like(acc)
+
+    spread_marks(marks_ref, columns, masks)
+    block = 256
+
+    for c in range(2):
+        lanes = slice(c * LANES, (c + 1) * LANES)
+        grad_pad[c, pl.ds(EDGE, rows), :] = grad_conv_ref[:, lanes].astype(F32)
+        conv_pad[c, pl.ds(EDGE, rows), :] = cv_ref[:, lanes]
+
+    probs = probs_ref[0].reshape(heads, TAP_ROWS, rows)
+    tap = lax.broadcasted_iota(jnp.int32, (heads, TAP_ROWS, rows), 1)
+    tap_mask = jnp.where(tap < KERNEL, jnp.broadcast_to(marks_ref[...], (heads, TAP_ROWS, rows)), 0.0)
+    masked = (probs * tap_mask).reshape(tap_rows, rows)
+    flat_tap = tap.reshape(tap_rows, rows)
+    moved = jnp.zeros_like(masked)
+    for j in range(KERNEL):
+        turn = (j - HALF) % rows
+        turned = pltpu.roll(masked, turn, 1) if turn else masked
+        moved = jnp.where(flat_tap == j, turned, moved)
+    shifted_weights[...] = high_low(moved, heads)
+    conv_block = 128
+
+    def conv_step(i, carry):
+        base = pl.multiple_of(i * conv_block, conv_block)
+        part = pl.ds(base, conv_block)
+        scale = nn(shifted_weights[part, :], expand_ref[...])
+        for c in range(2):
+            here = grad_pad[c, pl.ds(base + EDGE, conv_block), :]
+            total = jnp.zeros((conv_block, LANES), F32)
+            for j in range(KERNEL):
+                low = j * WIDE + c * LANES
+                products[:, low : low + LANES] = (
+                    here * conv_pad[c, pl.ds(base + EDGE + j - HALF, conv_block), :]
+                ).astype(BF16)
+                total = total + scale[:, low : low + LANES] * grad_pad[
+                    c, pl.ds(base + EDGE + HALF - j, conv_block), :
+                ]
+            grads[part, 3 * WIDE + c * LANES : 3 * WIDE + (c + 1) * LANES] = total.astype(BF16)
+        tap_terms[part, :] = nn(products[...], gather_ref[...])
+        return carry
+
+    lax.fori_loop(0, rows // conv_block, conv_step, 0)
+    grad_taps = jnp.transpose(tap_terms[...])[:tap_rows].reshape(heads, TAP_ROWS, rows) * tap_mask
+    grad_logits = probs * (grad_taps - jnp.sum(probs * grad_taps, axis=1, keepdims=True))
+    grad_logits = grad_logits.reshape(tap_rows, rows).astype(BF16)
+    tap_out[slot] = grad_logits
+    swap_taps = pltpu.make_async_remote_copy(
+        src_ref=tap_out.at[slot],
+        dst_ref=tap_in.at[slot],
+        send_sem=send_sem.at[slot],
+        recv_sem=recv_sem.at[slot],
+        device_id=(dp, 1 - mp),
+        device_id_type=MESH,
+    )
+    swap_taps.start()
+
+    grad_k[...] = jnp.zeros_like(grad_k)
+    grad_v[...] = jnp.zeros_like(grad_v)
+
+    def attention_step(i, carry):
+        part = pl.ds(pl.multiple_of(i * block, block), block)
+        allowed = columns[:, KERNEL : KERNEL + 1] == marks_ref[0, KERNEL : KERNEL + 1, part]
+        query = q_ref[part, :]
+        context = grad_context[part, :]
+        total = jnp.zeros((block, WIDE), F32)
+        for head in range(heads):
+            mine = (only(query, head) * (HEAD_DIM**-0.5)).astype(BF16)
+            grad_mine = only(context, head).astype(BF16)
+            scores = jnp.where(allowed, nt(k_ref[...], mine), MASK_FILL)
+            probs = jnp.exp(scores - lse_ref[0, head : head + 1, part])
+            grad_v[...] += nn(probs.astype(BF16), grad_mine)
+            grad_probs = nt(v_ref[...], grad_mine)
+            mixed = probs * grad_probs
+            grad_scores = (mixed - probs * jnp.sum(mixed, axis=0, keepdims=True)).astype(BF16)
+            grad_k[...] += nn(grad_scores, mine)
+            total = total + tn(grad_scores, only(k_ref[...], head).astype(BF16))
+        grad_q[part, :] = total
+        return carry
+
+    lax.fori_loop(0, rows // block, attention_step, 0)
+
+    swap_taps.wait()
+    tap_all[...] = jnp.zeros_like(tap_all)
+    tap_all[:tap_rows, :] = tap_out[slot].astype(F32)
+    tap_all[tap_rows : 2 * tap_rows, :] = tap_in[slot].astype(F32)
+    every = tap_all[...]
+    acc_tap[...] += nn(every.astype(BF16), ca_ref[...])
+    acc_tap_bias[...] += sum(every[:, c * LANES : (c + 1) * LANES] for c in range(rows // LANES))
+    weights[...] = jnp.transpose(every).astype(BF16)
+
+    def key_step(i, carry):
+        base = pl.multiple_of(i * block, block)
+        part = pl.ds(base, block)
+        grad_attn = nn(weights[part, :], taps_ref[...]).astype(BF16).astype(F32)
+        query = q_ref[part, :].astype(F32)
+        key_low = (grad_attn * query).astype(BF16)
+        grads[part, 4 * WIDE : 5 * WIDE] = key_low
+        grad_query = grad_q[part, :] * (HEAD_DIM**-0.5) + grad_attn * kc_ref[part, :]
+        grads[part, :WIDE] = grad_query.astype(BF16)
+        grads[part, WIDE : 2 * WIDE] = grad_k[part, :].astype(BF16)
+        grads[part, 2 * WIDE : 3 * WIDE] = grad_v[part, :].astype(BF16)
+        acc_bias[...] += row_sums(grads[part, :].astype(F32))
+        grad_depth = nt(key_low, point_ref[...])
+        total = nt(grads[part, : 4 * WIDE], inputs_ref[...])
+        for c in range(chunks):
+            lanes = slice(c * LANES, (c + 1) * LANES)
+            depth_pad[c, pl.ds(base + EDGE, block), :] = grad_depth[:, lanes]
+            rows_total[c, part, :] = total[:, lanes]
+        return carry
+
+    lax.fori_loop(0, rows // block, key_step, 0)
+    acc_point[...] += tn(dl_ref[...], grads[:, 4 * WIDE : 5 * WIDE])
+    acc_in[...] += tn(hidden_ref[...], grads[:, : 4 * WIDE])
+    step = 64
+
+    for c in range(chunks):
+        lanes = slice(c * LANES, (c + 1) * LANES)
+
+        def depth_step(i, carry, c=c, lanes=lanes):
+            base = pl.multiple_of(i * step, step)
+            part = pl.ds(base, step)
+            here = hidden_ref[part, lanes].astype(F32)
+            total = rows_total[c, part, :]
+            sums = []
+            for j in range(KERNEL):
+                mirror = KERNEL - 1 - j
+                near = depth_pad[c, pl.ds(base + EDGE + j - HALF, step), :] * masks[j, part, :]
+                total = total + near * depth_ref[mirror : mirror + 1, lanes]
+                sums.append(carry[j] + jnp.sum((near * here).reshape(step // 8, 8, LANES), axis=0))
+            rows_total[c, part, :] = total
+            return tuple(sums)
+
+        sums = lax.fori_loop(0, rows // step, depth_step, tuple(jnp.zeros((8, LANES), F32) for _ in range(KERNEL)))
+        for j in range(KERNEL):
+            acc_depth[KERNEL - 1 - j, :, lanes] += sums[j]
+    for c in range(half):
+        lanes = slice(c * LANES, (c + 1) * LANES)
+        own_ref[:, lanes] = rows_total[mp * half + c] + residual_ref[:, lanes]
+        other_ref[:, lanes] = rows_total[(1 - mp) * half + c].astype(BF16)
+
+    @pl.when(s == seqs - 1)
+    def _():
+        width = heads * HEAD_DIM
+
+        def pair(first, second):
+            return jnp.concatenate([first[:, :width], second[:, :width]], 1).astype(BF16)
+
+        big_qk_ref[...] = pair(acc_in[:, :WIDE], acc_in[:, WIDE : 2 * WIDE])
+        big_vc_ref[...] = pair(acc_in[:, 2 * WIDE : 3 * WIDE], acc_in[:, 3 * WIDE :])
+        big_point_ref[...] = pair(acc_point[...], jnp.zeros_like(acc_point))
+        bias_ref[...] = jnp.sum(acc_bias[...], axis=0, keepdims=True) + jnp.zeros_like(bias_ref)
+        tap_grad_ref[...] = acc_tap[...]
+        tap_bias_ref[...] = jnp.sum(acc_tap_bias[...], axis=1, keepdims=True) + jnp.zeros_like(tap_bias_ref)
+        for j in range(KERNEL):
+            depth_grad_ref[j : j + 1, :] = jnp.sum(acc_depth[j], axis=0, keepdims=True)
+        depth_grad_ref[KERNEL:, :] = jnp.zeros((TAP_ROWS - KERNEL, model), F32)
+
+
+def back(hidden, grad_context, grad_conv, residual, marks, kept, w, taps, depth, expand, ident):
+    q, k, v, cv, dl, kc, ca, probs, lse = kept
+    seqs, _, rows = marks.shape
+    tokens, model = hidden.shape
+    width = model // 2
+    tap_rows = probs.shape[1]
+
+    def seq(columns):
+        return by_seq(rows, columns)
+
+    def shape(columns, kind, count=tokens):
+        return jax.ShapeDtypeStruct((count, columns), kind)
+
+    padded_rows = rows + 2 * EDGE
+    vmem = pltpu.VMEM
+    return pl.pallas_call(
+        functools.partial(back_kernel, seqs),
+        grid=(seqs,),
+        out_shape=(
+            shape(width, F32), shape(width, BF16),
+            shape(width, BF16, model), shape(width, BF16, model), shape(width, BF16, model),
+            shape(5 * WIDE, F32, 8), shape(WIDE, F32, LANES), shape(LANES, F32, LANES), shape(model, F32, TAP_ROWS),
+        ),
+        in_specs=[
+            seq(model), seq(WIDE), seq(WIDE), seq(width), by_seq_row(TAP_ROWS, rows), seq(WIDE), seq(WIDE), seq(WIDE), seq(WIDE),
+            seq(model), seq(WIDE), seq(WIDE), by_seq_row(tap_rows, rows), by_seq_row(8, rows),
+        ] + [whole()] * 6,
+        out_specs=(seq(width), seq(width)) + (whole(),) * 7,
+        scratch_shapes=[
+            vmem((model // LANES, padded_rows, LANES), F32),
+            vmem((2, padded_rows, LANES), F32),
+            vmem((2, padded_rows, LANES), F32),
+            vmem((KERNEL, rows, LANES), F32),
+            vmem((rows, LANES), F32),
+            vmem((rows, LANES), BF16),
+            vmem((rows, LANES), BF16),
+            vmem((rows, LANES), F32),
+            vmem((128, KERNEL * WIDE), BF16),
+            vmem((rows, 5 * WIDE), BF16),
+            vmem((rows, WIDE), F32),
+            vmem((rows, WIDE), F32),
+            vmem((rows, WIDE), F32),
+            vmem((model // LANES, rows, LANES), F32),
+            vmem((LANES, rows), F32),
+            vmem((model, 4 * WIDE), F32),
+            vmem((model, WIDE), F32),
+            vmem((8, 5 * WIDE), F32),
+            vmem((LANES, WIDE), F32),
+            vmem((LANES, LANES), F32),
+            vmem((TAP_ROWS, 8, model), F32),
+            vmem((2, tap_rows, rows), BF16),
+            vmem((2, tap_rows, rows), BF16),
+            pltpu.SemaphoreType.DMA((2,)),
+            pltpu.SemaphoreType.DMA((2,)),
+        ],
+        compiler_params=pltpu.CompilerParams(
+            collective_id=ident, has_side_effects=True, vmem_limit_bytes=62 << 20
+        ),
+        name="back",
+    )(
+        hidden, grad_context, grad_conv, residual, marks, q, k, v, cv, dl, kc, ca, probs, lse,
+        jnp.concatenate([w.query, w.key, w.value, w.conv], 1), w.point, taps, depth, expand,
+        jnp.pad(expand[:tap_rows], ((0, LANES - tap_rows), (0, 0))).T,
+    )
+
+
+def marks_of(segment):
+    masks = [same_segment(segment, tap - HALF, HALF) for tap in range(KERNEL)]
+    blank = jnp.zeros_like(segment)
+    return jnp.stack([m.astype(F32) for m in masks] + [segment.astype(F32)] + [blank.astype(F32)] * (TAP_ROWS - KERNEL - 1))
+
+
+def expansion(heads):
+    row = lax.broadcasted_iota(jnp.int32, (LANES, KERNEL * WIDE), 0)
+    column = lax.broadcasted_iota(jnp.int32, (LANES, KERNEL * WIDE), 1)
+    tap, lane = column // WIDE, column % WIDE
+    wanted = (lane // HEAD_DIM) * TAP_ROWS + tap
+    inside = jnp.logical_and(lane < heads * HEAD_DIM, row < 2 * heads * TAP_ROWS)
+    return jnp.logical_and(inside, row % (heads * TAP_ROWS) == wanted).astype(BF16)
 
 
 def padded(value, multiple):
@@ -752,22 +1205,20 @@
     out_cut = jnp.concatenate([out_weight[0].T, out_weight[1].T], 1)
     second = jnp.concatenate([out_cut, ffn_in_weight[0].T, ffn_out_weight[0]], 0)
     first_all = gather(padded(first, 16)[None], count, 1)
-    second_all = gather(padded(second, 16)[None], count, 2)
 
     def cut(source, start, size, low, high):
         return source[:, start : start + size, low:high].reshape(count * size, high - low)
 
+    def cut_wide(source, start, low):
+        return jnp.pad(cut(source, start, share, low, low + width), ((0, 0), (0, WIDE - width)))
+
     w = Group(
-        query=cut(first_all, 0, share, 0, width),
-        key=cut(first_all, 0, share, width, 2 * width),
-        value=cut(first_all, share, share, 0, width),
-        conv=cut(first_all, share, share, width, 2 * width),
-        point=cut(first_all, 2 * share, share, 0, width),
-        depth=cut(first_all, 2 * share, share, width, width + KERNEL).T,
-        out0=cut(second_all, 0, share, 0, width),
-        out1=cut(second_all, 0, share, width, 2 * width),
-        inner=cut(second_all, share, share_ffn, 0, group),
-        outer=cut(second_all, share + share_ffn, share_ffn, 0, group),
+        query=cut_wide(first_all, 0, 0),
+        key=cut_wide(first_all, 0, width),
+        value=cut_wide(first_all, share, 0),
+        conv=cut_wide(first_all, share, width),
+        point=cut_wide(first_all, 2 * share, 0),
+        depth=cut(first_all, 2 * share, share, width, width + TAP_ROWS).T,
     )
     p = Group(
         query_bias=query_bias, value_bias=value_bias, point_bias=point_bias, kernel_weight=kernel_weight,
@@ -778,20 +1229,46 @@
     seqs = doc_lengths.shape[0]
     seq_rows = hidden.shape[0] // seqs
     spans = [slice(s * seq_rows, (s + 1) * seq_rows) for s in range(seqs)]
-    segments = [segment_ids(doc_lengths[s], seq_rows) for s in range(seqs)]
-    kept = [part_a(hidden[spans[s]], segments[s], w, p, me) for s in range(seqs)]
-    output, grad_residual, grad_branch, big_inner, big_outer, sums_mid = middle(
-        jnp.concatenate([k[9] for k in kept], 0),
-        jnp.concatenate([k[8] for k in kept], 0),
-        hidden, out_grad, w, p, me, 4,
-    )
-    last = [
-        part_c(hidden[spans[s]], segments[s], grad_branch[spans[s]], grad_residual[spans[s]], kept[s], w, p, me)
-        for s in range(seqs)
-    ]
-    grad_input = jnp.concatenate([t[0] for t in last], 0)
-    big = total_of([t[1] for t in last])
-    small = total_of([t[2] for t in last])
+    segments = [segment_ids(doc_lengths[q], seq_rows) for q in range(seqs)]
+    marks = jnp.stack([marks_of(segment) for segment in segments])
+    heads = width // HEAD_DIM
+    vectors = jnp.stack(
+        [jnp.pad(b, (0, WIDE - width)) for b in (query_bias, value_bias, point_bias, conv_bias)] * 2
+    )
+    order = kernel_weight.T.reshape(2, heads, KERNEL, width)
+    order = jnp.where(me == 0, order, order[::-1])
+    taps = jnp.pad(order, ((0, 0), (0, 0), (0, TAP_ROWS - KERNEL), (0, WIDE - width))).reshape(-1, WIDE)
+    taps = jnp.pad(taps, ((0, LANES - taps.shape[0]), (0, 0)))
+    bias = lax.dynamic_slice_in_dim(kernel_bias.reshape(2, heads, KERNEL), me, 1, 0)[0]
+    bias = jnp.pad(bias, ((0, 0), (0, TAP_ROWS - KERNEL))).reshape(-1, 1)
+    bias = jnp.broadcast_to(bias, (bias.shape[0], LANES))
+    expand = expansion(heads)
+    q, k, v, cv, dl, kc, ca, probs, cc, ctx, lse, second_all = front(
+        hidden, marks, w, vectors, w.depth.astype(F32), bias, expand, taps, padded(second, 16)[None], count, 2
+    )
+    w.out0 = cut_wide(second_all, 0, 0)
+    w.out1 = cut_wide(second_all, 0, width)
+    w.inner = cut(second_all, share, share_ffn, 0, group)
+    w.outer = cut(second_all, share + share_ffn, share_ffn, 0, group)
+    output, grad_residual, grad_context, grad_conv, big_inner, big_outer, big_out, sums_mid = middle(
+        ctx, cc, hidden, out_grad, w, p, me, 4
+    )
+    depth = w.depth.astype(F32)
+    part_own, part_other, big_qk, big_vc, big_point, bias_sums, tap_grads, tap_bias, depth_grads = back(
+        hidden, grad_context, grad_conv, grad_residual, marks, (q, k, v, cv, dl, kc, ca, probs, lse),
+        w, taps, depth, expand, 5,
+    )
+    grad_input = part_own + swap(part_other).astype(F32)
+
+    def both(value):
+        value = value[: 2 * heads * TAP_ROWS].reshape(2, heads, TAP_ROWS, -1)[:, :, :KERNEL]
+        return jnp.where(me == 0, value, value[::-1]).reshape(2 * heads * KERNEL, -1)
+
+    kernel_weight_grad = both(tap_grads)[:, :width].T
+    kernel_bias_grad = both(tap_bias)[:, 0]
+
+    def bias_of(place):
+        return bias_sums[0, place * WIDE : place * WIDE + width]
 
     def widened(value):
         empty = jnp.zeros_like(value)
@@ -801,19 +1278,11 @@
     def blocks(value):
         return value.reshape(count, value.shape[0] // count, value.shape[1])
 
-    pieces = jnp.concatenate(
-        [
-            blocks(jnp.concatenate([big.query, big.key], 1)),
-            blocks(jnp.concatenate([big.value, big.conv], 1)),
-            blocks(jnp.concatenate([big.point, jnp.zeros_like(big.point)], 1)),
-            blocks(jnp.concatenate([big.out0, big.out1], 1)),
-        ],
-        1,
-    ).astype(BF16)
-    pieces = jnp.concatenate([pieces, blocks(big_inner), blocks(big_outer)], 1)
+    pieces = [blocks(value) for value in (big_qk, big_vc, big_point, big_out, big_inner, big_outer)]
+    pieces = jnp.concatenate(pieces, 1)
     own_parts = [
-        small.query_bias, small.value_bias, small.point_bias, small.kernel_weight, small.kernel_bias,
-        small.conv_bias, sums_mid[6], sums_mid[0, :group], sums_mid[1, :group], sums_mid[2, :group],
+        bias_of(0), bias_of(2), bias_of(4), kernel_weight_grad, kernel_bias_grad,
+        bias_of(3), sums_mid[6], sums_mid[0, :group], sums_mid[1, :group], sums_mid[2, :group],
     ]
     columns = group
 
@@ -824,7 +1293,7 @@
     own_size = sum(part.size for part in own_parts)
     own_rows = -(-own_size // columns)
     own_rows += -own_rows % 8
-    shared_parts = [small.depth] + [widened(sums_mid[k, :group]) for k in (3, 4, 5)]
+    shared_parts = [depth_grads[:KERNEL]] + [widened(sums_mid[k, :group]) for k in (3, 4, 5)]
     smalls = jnp.concatenate([table(own_parts, own_rows), table(shared_parts, SHARED_ROWS)], 0)
     sums, totals = scatter(padded(pieces, 16), smalls, count, 3)
 

time: 778 us -> 459 us (0.59); the launches traced: 769 us -> 458 us
  matrix products: 231 us -> 0 us
  Pallas kernels: 229 us -> 383 us
  other arithmetic: 155 us -> 18.3 us
  local copies, waits for them, and re-layouts: 109 us -> 54.4 us
  waiting for transfers between devices: 29.9 us -> 0.01 us
  starting transfers between devices: 9.11 us -> 0.79 us
    dot_general x84 -> x0, matrix products: 231 us -> none  [the longest x18 96.1 us: nt(): lax.dot_general(left, right, (((1,), (1,)), ((), ())), preferred_element_...]
    pallas_call x0 -> x2, Pallas kernels: none -> 172 us  [the longest x1 101 us: back(): pl.pallas_call(functools.partial(back_kernel, seqs), grid=(seqs,), out_sh...]
    convert_element_type x15 -> x5, other arithmetic: 69.5 us -> 1.31 us  [the longest x1 1.26 us: expansion(): jnp.logical_and(inside, row % (heads * TAP_ROWS) == wanted).astype(BF16)]
    unnamed x550 -> x66, local copies, waits for them, and re-layouts: 39.2 us -> 8.25 us
    reduce_sum x16 -> x0, other arithmetic: 30.7 us -> none  [the longest x3 12.5 us: part_c(): small.conv_bias = jnp.sum(conv_low, axis=0, dtype=F32)]
    ppermute x9 -> x1, waiting for transfers between devices: 29.9 us -> 0.01 us  [swap(): return lax.ppermute(value, 'mp', SWAP)]
    pallas_call x2 -> x1, Pallas kernels: 46.9 us -> 19.7 us  [gather(): pl.pallas_call(functools.partial(gather_kernel, count), out_shape=jax.Sha...]
    mul x20 -> x0, other arithmetic: 25.3 us -> none  [the longest x1 13.8 us: part_c(): masked * w.depth[tap].astype(F32)]
  transfers between devices with their start and end apart: 9 -> 1, of which waited for: 2 -> 0; matrix products, arithmetic and copies ran while one was open for 24% -> 9% of each run, Pallas kernels for 4% -> 14%
where the time goes in v2:
time: 459 us; the launch traced here: 458 us
  Pallas kernels  383 us (83%)
  local copies, waits for them, and re-layouts  54.4 us (12%)
  other arithmetic  18.3 us (4%)
    pallas_call x1, Pallas kernels, middle(): pl.pallas_call(functools.partial(middle_kernel, blocks), grid=(blocks + 5...  128 us
    pallas_call x1, Pallas kernels, back(): pl.pallas_call(functools.partial(back_kernel, seqs), grid=(seqs,), out_sh...  101 us
    pallas_call x1, Pallas kernels, front(): pl.pallas_call(functools.partial(front_kernel, seqs, count), grid=(seqs,)...  71 us
    pallas_call x1, Pallas kernels, scatter(): pl.pallas_call(functools.partial(scatter_kernel, count), out_shape=(jax.S...  63.3 us
    pallas_call x1, Pallas kernels, gather(): pl.pallas_call(functools.partial(gather_kernel, count), out_shape=jax.Sha...  19.7 us
  transfers between devices with their start and end apart: 1, of which 0 were waited for; matrix products, arithmetic and copies ran while one was open for 9% of the time, Pallas kernels for 14%

profile of v2, /device:TPU:8, one launch (start us, length us, event | category | flops | bytes accessed | tf_op | source)
XLA Modules:
  0.0 457.7 jit_solution(6480135055871773384)
XLA Ops:
  0.8 0.8 slice_bitcast_fusion.9
  2.7 0.8 copy.64
  3.5 1.5 fusion.28.own_ref
  5.0 19.7 %weight_gather.1 = bf16[16,144,384]{2,1,0:T(8,128)(2,1)} custom-call(bf16[1,144,384]{2,1,0:T(8,128)(2,1)} %fusion.28.own_ref), custom_call_target="tpu_custom_call" | custom-call | tf_op jit(solution)/shard_map/weight_gather/pallas_call | solution.py:91
  24.7 1.0 slice.303
  25.8 1.9 fusion.85
  28.1 0.6 pad.97.taps_ref
  28.7 0.8 copy.68
  29.5 0.8 pad.95.point_ref
  31.0 0.7 pad_maximum_fusion.1.marks_ref
  31.7 0.6 stack.276.vec_ref
  32.3 0.8 maximum_bitcast_fusion.second_ref
  33.1 1.4 pad_maximum_fusion.inputs_ref
  34.5 1.3 fusion.19.expand_ref
  35.7 0.7 broadcast_in_dim.30.bias_ref
  36.4 71.0 %front.1 = (bf16[3072,256]{1,0:T(8,128)(2,1)}, bf16[3072,256]{1,0:T(8,128)(2,1)}, bf16[3072,256]{1,0:T(8,128)(2,1)}, f32[3072,256]{1,0:T(8,128)}, bf16[3072,768]...) custom-call(bf16[3072,768]{1,0:T(8,128)(2,1)} %hidden_ref.5, ...), custom_call_target="tpu_custom_call" | custom-call | tf_op jit(solution)/shard_map/front/pallas_call | solution.py:571
  107.4 1.3 fusion.84
  108.8 3.3 fusion.83
  112.6 3.7 fusion.22.gather_ref
  116.2 0.9 pad.104.out1_ref
  117.1 0.8 pad.103.out0_ref
  117.9 0.7 stack.283.vec_ref
  118.6 128.1 %middle.1 = (bf16[3072,384]{1,0:T(8,128)(2,1)}, f32[3072,384]{1,0:T(8,128)}, bf16[3072,256]{1,0:T(8,128)(2,1)}, bf16[3072,256]{1,0:T(8,128)(2,1)}, bf16[1536,384...) custom-call(bf16[3072,256]{1,0:T(8,128)(2,1)} %get-tuple-element.55.context_ref.context_, ...), custom_call_target="tpu_custom_call" | custom-call | tf_op jit(solution)/shard_map/middle/pallas_call | solution.py:862
  246.7 100.8 %back.1 = (f32[3072,384]{1,0:T(8,128)}, bf16[3072,384]{1,0:T(8,128)(2,1)}, bf16[768,384]{1,0:T(8,128)(2,1)}, bf16[768,384]{1,0:T(8,128)(2,1)}, bf16[768,384]{1,0...) custom-call(bf16[3072,768]{1,0:T(8,128)(2,1)} %hidden_ref.5, ...), custom_call_target="tpu_custom_call" | custom-call | tf_op jit(solution)/shard_map/back/pallas_call | solution.py:1112
  347.5 0.8 collective-permute-start
  348.3 0.8 slice_reduce_fusion.1
  349.1 1.5 slice_reduce_fusion.5
  350.7 1.3 fusion.89
  352.0 0.8 reshape.272
  352.8 0.6 reshape.273
  353.4 0.8 slice.316
  354.3 0.6 reshape.270
  354.9 0.9 slice.313
  355.8 0.6 reverse_select_fusion
  356.4 1.6 reshape.267
  358.0 1.4 slice_bitcast_fusion.2
  359.5 1.6 copy.66
  361.0 1.6 reshape.268
  362.7 1.4 slice_reduce_fusion
  364.0 1.5 concatenate.101
  365.6 1.4 pad.112
  367.0 1.5 reshape.271
  368.5 1.5 pad_maximum_fusion.2.small_ref
  370.0 0.9 constant_dynamic-update-slice_fusion.5
  370.9 0.9 constant_dynamic-update-slice_fusion.4
  371.8 0.9 constant_dynamic-update-slice_fusion.3
  372.6 0.9 constant_dynamic-update-slice_fusion.2
  373.5 1.1 constant_dynamic-update-slice_fusion.1
  375.2 1.1 constant_dynamic-update-slice_fusion.in_ref
  376.3 63.3 %gradient_scatter.1 = (f32[384,384]{1,0:T(8,128)}, f32[64,384]{1,0:T(8,128)}) custom-call(bf16[16,384,384]{2,1,0:T(8,128)(2,1)} %constant_dynamic-update-slice_fusion.in_ref, f32[64,384]{1,0:T(8,128)} %pad_maximum_fusion.2.small_ref), custom_call_target="tpu_custom_call" | custom-call | tf_op jit(solution)/shard_map/gradient_scatter/pallas_call | solution.py:221
  439.6 0.8 slice.334
  440.5 0.8 slice.331
  442.1 0.8 fusion.86
  442.9 0.6 slice.348
  443.5 0.6 slice.346
  445.5 0.7 copy.67
  446.2 0.7 constant_dynamic-slice_fusion
  446.8 1.7 slice_bitcast_fusion.4
  448.5 0.6 pad_maximum_fusion.3
  449.2 0.6 fusion.88
  449.8 0.7 fusion.87
  450.5 0.7 slice_bitcast_fusion
  451.2 5.1 %convert_add_fusion = f32[3072,384]{1,0:T(8,128)} fusion(f32[3072,384]{1,0:T(8,128)} %get-tuple-element.71, bf16[3072,384]{1,0:T(8,128)(2,1)S(1)} %collective-permute-done), kind=kLoop, calls=%fused_computation | loop fusion | flops 2359296 | bytes 11796480 | tf_op jit(solution)/shard_map/add | solution.py:1261
  456.3 1.4 copy.75
  (132 shorter events, 5.1 us)
Async XLA Ops:
  25.8 2.0 copy-start.23
  25.8 2.0 copy-start.24
  25.8 2.0 copy-start.25
  25.8 2.0 copy-start.26
  25.8 2.0 copy-start.27
  25.8 2.2 copy-start.15
  25.8 2.9 copy-start.14
  30.4 2.7 copy-start
  30.5 2.6 copy-start.1
  30.5 1.8 copy-start.12
  30.5 1.8 copy-start.13
  30.6 3.9 copy-start.2
  30.7 3.8 copy-start.3
  108.7 3.4 copy-start.20
  108.8 3.5 copy-start.21
  108.8 3.5 copy-start.22
  108.8 3.7 copy-start.17
  108.8 3.7 copy-start.18
  108.8 3.7 copy-start.19
  108.8 3.7 copy-start.28
  112.4 5.5 %copy-start.16 = (f32[1,1536]{1,0:T(1,128)S(1)}, f32[1,1536]{1,0:T(1,128)}, u32[]{:S(2)}) copy-start(f32[1,1536]{1,0:T(1,128)} %param.44) | copy-start | bytes 18436
  347.5 22.5 %copy-start.11 = (bf16[768,384]{1,0:T(8,128)(2,1)S(1)}, bf16[768,384]{1,0:T(8,128)(2,1)}, u32[]{:S(2)}) copy-start(bf16[768,384]{1,0:T(8,128)(2,1)} %get-tuple-element.73) | copy-start | bytes 1769476
  347.5 103.7 %collective-permute-start = (bf16[3072,384]{1,0:T(8,128)(2,1)}, bf16[3072,384]{1,0:T(8,128)(2,1)S(1)}, u32[]{:S(2)}, u32[]{:S(2)}) collective-permute-start(bf16[3072,384]{1,0:T(8,128)(2,1)} %get-tuple-element.72), channel_id=1, source_target_pairs={{0,1},{1,0},{2,3},{3,2},{4,5},{5,4},{6,7},{7,6},{8,9},{9,8},{10,11... | collective-permute-start | bytes 7077896 | tf_op jit(solution)/shard_map/ppermute | solution.py:279
  356.4 14.5 %copy-start.10 = (bf16[768,384]{1,0:T(8,128)(2,1)S(1)}, bf16[768,384]{1,0:T(8,128)(2,1)}, u32[]{:S(2)}) copy-start(bf16[768,384]{1,0:T(8,128)(2,1)} %get-tuple-element.74) | copy-start | bytes 1769476
  370.0 1.8 copy-start.9
  370.9 1.8 copy-start.8
  371.8 1.8 copy-start.6
  373.5 1.7 copy-start.5
  439.6 10.8 %copy-start.7 = (f32[384,384]{1,0:T(8,128)S(1)}, f32[384,384]{1,0:T(8,128)}, u32[]{:S(2)}) copy-start(f32[384,384]{1,0:T(8,128)} %get-tuple-element.84) | copy-start | bytes 1769476
  451.2 5.1 %copy-start.4 = (bf16[3072,384]{1,0:T(8,128)(2,1)S(1)}, bf16[3072,384]{1,0:T(8,128)(2,1)}, u32[]{:S(2)}) copy-start(bf16[3072,384]{1,0:T(8,128)(2,1)} %get-tuple-element.275) | copy-start | bytes 7077892

commit v3 on v2

--- a/solution.py
+++ b/solution.py
@@ -8,6 +8,8 @@
 from jax.sharding import PartitionSpec as P
 
 MESH = pl.DeviceIdType.MESH
+BF16 = jnp.bfloat16
+F32 = jnp.float32
 
 
 def at(dp, mp):
@@ -103,11 +105,104 @@
     )(own)
 
 
-def scatter_kernel(
-    count, in_ref, small_ref, out_ref, total_ref,
-    twin_in, side_in, deep_in, twin_sum, side_sum,
-    small_in, small_out, send_sem, recv_sem, small_send, small_recv,
-):
+class Hops:
+    def __init__(self, count, in_ref, twin_in, side_in, deep_in, send_sem, recv_sem):
+        self.mp, self.core, self.side, self.deep, self.parts = places(count)
+        self.in_ref, self.twin_in, self.side_in, self.deep_in = in_ref, twin_in, side_in, deep_in
+        self.send_sem, self.recv_sem = send_sem, recv_sem
+        self.beside = index_of(self.deep, 1 - self.side, self.core)
+        self.twin = index_of(self.deep, self.side, 1 - self.core)
+        self.order = [(k, other) for k in list(range(1, self.parts)) + [0] for other in (1, 0)]
+        self.rows = in_ref.shape[1]
+        self.step = 48 if self.rows % 48 == 0 else 16
+
+    def depth(self, k):
+        return lax.rem(self.deep + k, self.parts)
+
+    def copy(self, source, target_ref, slot, target):
+        return pltpu.make_async_remote_copy(
+            src_ref=source,
+            dst_ref=target_ref,
+            send_sem=self.send_sem.at[slot],
+            recv_sem=self.recv_sem.at[slot],
+            device_id=at(target, self.mp),
+            device_id_type=MESH,
+        )
+
+    def block(self, slot, core):
+        k, other = self.order[slot]
+        return index_of(self.depth(k), 1 - self.side if other else self.side, core)
+
+    def first(self, slot):
+        return self.copy(self.in_ref.at[self.block(slot, 1 - self.core)], self.twin_in.at[slot], slot, self.twin)
+
+    def second(self, place):
+        return self.copy(
+            self.twin_in.at[2 * place], self.side_in.at[place], 2 * self.parts + place, self.beside
+        )
+
+    def third(self, place):
+        k = self.order[2 * place][0]
+        target = index_of(self.depth(k), self.side, self.core)
+        return self.copy(self.side_in.at[place], self.deep_in.at[place], 3 * self.parts + place, target)
+
+    def add(self, target, term):
+        @pl.loop(0, self.rows // self.step)
+        def _(i):
+            part = pl.ds(pl.multiple_of(i * self.step, 16), self.step)
+            total = target[part, :].astype(F32) + term[part, :].astype(F32)
+            target[part, :] = total.astype(target.dtype)
+
+    def start_first(self):
+        for slot in range(2 * self.parts):
+            self.first(slot).start()
+
+    def start_second(self):
+        for slot in range(2 * self.parts):
+            self.first(slot).wait_recv()
+            self.add(self.twin_in.at[slot], self.in_ref.at[self.block(slot, self.core)])
+            if self.order[slot][1]:
+                self.second(slot // 2).start()
+
+    def start_third(self):
+        for place in range(self.parts):
+            self.second(place).wait_recv()
+            self.add(self.side_in.at[place], self.twin_in.at[2 * place + 1])
+            if place < self.parts - 1:
+                self.third(place).start()
+
+    def finish(self, out_ref):
+        for place in range(self.parts - 1):
+            self.third(place).wait_recv()
+
+        @pl.loop(0, self.rows // self.step)
+        def _(i):
+            part = pl.ds(pl.multiple_of(i * self.step, 16), self.step)
+            total = self.side_in[self.parts - 1, part, :].astype(F32)
+            for place in range(self.parts - 1):
+                total = total + self.deep_in[place, part, :].astype(F32)
+            out_ref[part, :] = total
+
+        for slot in range(2 * self.parts):
+            self.first(slot).wait_send()
+        for place in range(self.parts):
+            self.second(place).wait_send()
+        for place in range(self.parts - 1):
+            self.third(place).wait_send()
+
+
+def hop_scratch(count, rows, columns):
+    parts = count // 4
+    return [
+        pltpu.VMEM((2 * parts, rows, columns), BF16),
+        pltpu.VMEM((parts, rows, columns), BF16),
+        pltpu.VMEM((max(parts - 1, 1), rows, columns), BF16),
+        pltpu.SemaphoreType.DMA((4 * parts - 1,)),
+        pltpu.SemaphoreType.DMA((4 * parts - 1,)),
+    ]
+
+
+def greet_all(count):
     mp, core, side, deep, parts = places(count)
     me = index_of(deep, side, core)
     barrier = pltpu.get_barrier_semaphore()
@@ -117,133 +212,207 @@
     for peer in peers:
         pl.semaphore_signal(barrier, inc=1, device_id=at(peer, mp), device_id_type=MESH)
     pl.semaphore_wait(barrier, len(peers) + 1)
+
+
+PIECES = 4
+
+
+def tail_kernel(
+    count, start,
+    in_ref, table_ref, own_ref, other_ref, rest_ref,
+    out_ref, total_ref, grad_ref,
+    twin_in, side_in, deep_in, send_sem, recv_sem,
+    table_in, table_out, table_send, table_recv, piece_in, piece_sum, piece_send, piece_recv, store_sem,
+):
+    mp, core, side, deep, parts = places(count)
+    me = index_of(deep, side, core)
+    greet_all(count)
     beside = index_of(deep, 1 - side, core)
     twin = index_of(deep, side, 1 - core)
-    started = []
-    rows = in_ref.shape[1]
-    step = rows // 4 if rows % 64 == 0 else rows
-
-    def push(source, target_ref, slot, target, sends=send_sem, recvs=recv_sem, plane=mp):
-        copy = pltpu.make_async_remote_copy(
+    hops = Hops(count, in_ref, twin_in, side_in, deep_in, send_sem, recv_sem)
+    rows = own_ref.shape[0] // PIECES
+
+    def table_hop(source, slot, target, plane):
+        return pltpu.make_async_remote_copy(
             src_ref=source,
-            dst_ref=target_ref,
-            send_sem=sends.at[slot],
-            recv_sem=recvs.at[slot],
+            dst_ref=table_in.at[slot],
+            send_sem=table_send.at[slot],
+            recv_sem=table_recv.at[slot],
             device_id=at(target, plane),
             device_id_type=MESH,
         )
+
+    def piece(i):
+        part = pl.ds(i * rows, rows)
+        return pltpu.make_async_remote_copy(
+            src_ref=other_ref.at[part],
+            dst_ref=piece_in.at[part],
+            send_sem=piece_send.at[i],
+            recv_sem=piece_recv.at[i],
+            device_id=at(me, 1 - mp),
+            device_id_type=MESH,
+        )
+
+    def store(i):
+        return pltpu.make_async_copy(
+            piece_sum.at[pl.ds(i * rows, rows)], grad_ref.at[pl.ds(start + i * rows, rows)], store_sem.at[i]
+        )
+
+    first = table_hop(table_ref, 0, me, 1 - mp)
+    first.start()
+    hops.start_first()
+    for i in range(PIECES):
+        piece(i).start()
+    first.wait_recv()
+    shared = pl.ds(TABLE_OWN, TABLE_ROWS - TABLE_OWN)
+    table_out[0, :TABLE_OWN, :] = table_ref[:TABLE_OWN, :]
+    table_out[0, shared, :] = table_ref[shared, :] + table_in[0, shared, :]
+    second = table_hop(table_out.at[0], 1, twin, mp)
+    second.start()
+    hops.start_second()
+    second.wait_recv()
+    table_out[1] = table_out[0] + table_in[1]
+    third = table_hop(table_out.at[1], 2, beside, mp)
+    third.start()
+    hops.start_third()
+    third.wait_recv()
+    table_out[2] = table_out[1] + table_in[2]
+    fourth = [
+        table_hop(table_out.at[2], 2 + j, index_of(lax.rem(deep + j, parts), side, core), mp) for j in range(1, parts)
+    ]
+    for copy in fourth:
         copy.start()
-        started.append(copy)
-        return copy
-
-    def add(target, first, second):
-        @pl.loop(0, rows // step)
-        def _(i):
-            part = pl.ds(pl.multiple_of(i * step, step), step)
-            total = first[part, :].astype(jnp.float32) + second[part, :].astype(jnp.float32)
-            target[part, :] = total.astype(target.dtype)
-
-    small_hop = push(small_ref, small_in.at[0], 0, me, small_send, small_recv, 1 - mp)
-    order = [(k, other) for k in list(range(1, parts)) + [0] for other in (1, 0)]
-    hop = {}
-    for slot, (k, other) in enumerate(order):
-        z = lax.rem(deep + k, parts)
-        s = 1 - side if other else side
-        hop[(k, other)] = push(
-            in_ref.at[index_of(z, s, 1 - core)], twin_in.at[slot], slot, twin
-        )
-    small_hop.wait_recv()
-    shared = small_ref.shape[0] - SHARED_ROWS
-    small_out[0, pl.ds(0, shared), :] = small_ref[pl.ds(0, shared), :]
-    small_out[0, pl.ds(shared, SHARED_ROWS), :] = (
-        small_ref[pl.ds(shared, SHARED_ROWS), :] + small_in[0, pl.ds(shared, SHARED_ROWS), :]
-    )
-    small_hop = push(small_out.at[0], small_in.at[1], 1, twin, small_send, small_recv)
-    base = len(order)
-    hop2 = {}
-    for slot, (k, other) in enumerate(order):
-        z = lax.rem(deep + k, parts)
-        s = 1 - side if other else side
-        hop[(k, other)].wait_recv()
-        add(twin_sum.at[slot], in_ref.at[index_of(z, s, core)], twin_in.at[slot])
-        if other:
-            place = slot // 2
-            hop2[k] = push(twin_sum.at[slot], side_in.at[place], base + place, beside)
-        if slot == 1:
-            small_hop.wait_recv()
-            small_out[1] = small_out[0] + small_in[1]
-            small_hop = push(small_out.at[1], small_in.at[2], 2, beside, small_send, small_recv)
-    base2 = base + parts
-    hop3 = []
-    small_hops = []
-    for place, k in enumerate(list(range(1, parts)) + [0]):
-        hop2[k].wait_recv()
-        add(side_sum.at[place], twin_sum.at[2 * place + 1], side_in.at[place])
-        if k:
-            z = lax.rem(deep + k, parts)
-            hop3.append(
-                push(side_sum.at[place], deep_in.at[place], base2 + place, index_of(z, side, core))
-            )
-        if place == 0:
-            small_hop.wait_recv()
-            small_out[2] = small_out[1] + small_in[2]
-            for j in range(1, parts):
-                z = lax.rem(deep + j, parts)
-                small_hops.append(
-                    push(small_out.at[2], small_in.at[2 + j], 2 + j, index_of(z, side, core), small_send, small_recv)
-                )
-    for copy in small_hops:
+    for i in range(PIECES):
+        piece(i).wait_recv()
+        part = pl.ds(i * rows, rows)
+        piece_sum[part, :] = own_ref[part, :] + piece_in[part, :].astype(F32)
+        store(i).start()
+    hops.finish(out_ref)
+    for copy in fourth:
         copy.wait_recv()
-    total = small_out[2]
+    total = table_out[2]
     for j in range(1, parts):
-        total = total + small_in[2 + j]
+        total = total + table_in[2 + j]
     total_ref[...] = total
-    for copy in hop3:
-        copy.wait_recv()
-
-    @pl.loop(0, rows // step)
-    def _(i):
-        part = pl.ds(pl.multiple_of(i * step, step), step)
-        total = side_sum[parts - 1, part, :].astype(jnp.float32)
-        for place in range(parts - 1):
-            total = total + deep_in[place, part, :].astype(jnp.float32)
-        out_ref[part, :] = total
-
-    for copy in started:
+    for copy in [first, second, third] + fourth:
         copy.wait_send()
-
-
-def scatter(blocks, small, count, ident):
+    for i in range(PIECES):
+        piece(i).wait_send()
+        store(i).wait()
+
+
+def tail(blocks, table, own, other, grad_rows, count, ident):
     parts = count // 4
     _, rows, columns = blocks.shape
-    sends = 4 * parts - 1
-    kind = blocks.dtype
+    start = grad_rows.shape[0] - own.shape[0]
+    vmem = pl.BlockSpec(memory_space=pltpu.VMEM)
+    place = pl.BlockSpec(memory_space=pl.ANY)
     return pl.pallas_call(
-        functools.partial(scatter_kernel, count),
+        functools.partial(tail_kernel, count, start),
         out_shape=(
-            jax.ShapeDtypeStruct((rows, columns), jnp.float32),
-            jax.ShapeDtypeStruct(small.shape, jnp.float32),
+            jax.ShapeDtypeStruct((rows, columns), F32),
+            jax.ShapeDtypeStruct(table.shape, F32),
+            jax.ShapeDtypeStruct(grad_rows.shape, F32),
         ),
-        in_specs=[pl.BlockSpec(memory_space=pltpu.VMEM)] * 2,
-        out_specs=(pl.BlockSpec(memory_space=pltpu.VMEM),) * 2,
-        scratch_shapes=[
-            pltpu.VMEM((2 * parts, rows, columns), kind),
-            pltpu.VMEM((parts, rows, columns), kind),
-            pltpu.VMEM((max(parts - 1, 1), rows, columns), kind),
-            pltpu.VMEM((2 * parts, rows, columns), kind),
-            pltpu.VMEM((parts, rows, columns), kind),
-            pltpu.VMEM((parts + 2,) + small.shape, jnp.float32),
-            pltpu.VMEM((3,) + small.shape, jnp.float32),
-            pltpu.SemaphoreType.DMA((sends,)),
-            pltpu.SemaphoreType.DMA((sends,)),
+        in_specs=[vmem, vmem, vmem, vmem, place],
+        out_specs=(vmem, vmem, place),
+        input_output_aliases={4: 2},
+        scratch_shapes=hop_scratch(count, rows, columns)
+        + [
+            pltpu.VMEM((parts + 2,) + table.shape, F32),
+            pltpu.VMEM((3,) + table.shape, F32),
             pltpu.SemaphoreType.DMA((parts + 2,)),
             pltpu.SemaphoreType.DMA((parts + 2,)),
+            pltpu.VMEM(other.shape, BF16),
+            pltpu.VMEM(own.shape, F32),
+            pltpu.SemaphoreType.DMA((PIECES,)),
+            pltpu.SemaphoreType.DMA((PIECES,)),
+            pltpu.SemaphoreType.DMA((PIECES,)),
         ],
         compiler_params=pltpu.CompilerParams(
             collective_id=ident, has_side_effects=True, vmem_limit_bytes=60 << 20
         ),
-        name="gradient_scatter",
-    )(blocks, small)
+        name="tail",
+    )(blocks, table, own, other, grad_rows)
+
+
+def wide_row(table, row, count):
+    return jnp.concatenate([table[row + k : row + k + 1, :] for k in range(count)], 1)
+
+
+def turned(tile, value):
+    rows, columns = value.shape
+    tile[...] = jnp.zeros_like(tile)
+    tile[:rows, :columns] = value
+    return jnp.transpose(tile[...])[:columns, :rows]
+
+
+def final_kernel(
+    count, first_ref, second_ref, table_ref,
+    q_ref, k_ref, v_ref, qb_ref, vb_ref, depth_ref, p_ref, pb_ref, kw_ref, kb_ref, c_ref, cb_ref, out_ref, ob_ref,
+    gain1_ref, bias1_ref, inner_ref, inb_ref, outer_ref, outb_ref, gain2_ref, bias2_ref,
+    tile_out, tile_inner, tile_taps, spread,
+):
+    share, width = q_ref.shape
+    share_ffn, group = outer_ref.shape
+    q_ref[...] = second_ref[:share, :width]
+    k_ref[...] = second_ref[:share, width : 2 * width]
+    v_ref[...] = second_ref[share : 2 * share, :width]
+    c_ref[...] = second_ref[share : 2 * share, width : 2 * width]
+    p_ref[...] = second_ref[2 * share : 3 * share, :width]
+    out_ref[0] = turned(tile_out, first_ref[:share, :width])
+    out_ref[1] = turned(tile_out, first_ref[:share, width : 2 * width])
+    inner_ref[...] = turned(tile_inner, first_ref[share : share + share_ffn, :])
+    outer_ref[...] = first_ref[share + share_ffn : share + 2 * share_ffn, :]
+    taps = kb_ref.shape[1]
+    rows = jnp.transpose(jnp.concatenate([table_ref[:64, :], jnp.zeros((64, WIDE), F32)], 0))
+    kw_ref[...] = rows[:width, :taps]
+    kb_ref[...] = rows[width : width + 1, :taps]
+    qb_ref[...] = table_ref[54:55, :width]
+    vb_ref[...] = table_ref[55:56, :width]
+    pb_ref[...] = table_ref[56:57, :width]
+    cb_ref[...] = table_ref[57:58, :width]
+    outb_ref[...] = wide_row(table_ref, 58, 2)[:, :group]
+    gain2_ref[...] = wide_row(table_ref, 60, 2)[:, :group]
+    bias2_ref[...] = wide_row(table_ref, 62, 2)[:, :group]
+    inb_ref[...] = wide_row(table_ref, 64, 6)
+    gain1_ref[...] = wide_row(table_ref, 99, 3)
+    bias1_ref[...] = wide_row(table_ref, 102, 3)
+    ob_ref[...] = wide_row(table_ref, 105, 3)
+    spread[...] = jnp.zeros_like(spread)
+    for k in range(3):
+        spread[:KERNEL, k * WIDE : (k + 1) * WIDE] = table_ref[72 + KERNEL * k : 72 + KERNEL * (k + 1), :]
+    model = spread.shape[1]
+    dp = lax.axis_index("dp")
+    moved = pltpu.roll(spread[...], lax.rem(model - dp * share, model), 1)
+    depth_ref[...] = moved[:KERNEL, :share]
+
+
+def final(first, second, table, share, share_ffn, width, group, taps, count):
+    def shape(*sizes):
+        return jax.ShapeDtypeStruct(sizes, F32)
+
+    model = 2 * group
+    return pl.pallas_call(
+        functools.partial(final_kernel, count),
+        out_shape=(
+            shape(share, width), shape(share, width), shape(share, width), shape(1, width), shape(1, width),
+            shape(KERNEL, share), shape(share, width), shape(1, width), shape(width, taps), shape(1, taps),
+            shape(share, width), shape(1, width), shape(2, width, share), shape(1, model), shape(1, model),
+            shape(1, model), shape(group, share_ffn), shape(1, 4 * group), shape(share_ffn, group), shape(1, group),
+            shape(1, group), shape(1, group),
+        ),
+        in_specs=[whole()] * 3,
+        out_specs=(whole(),) * 22,
+        scratch_shapes=[
+            pltpu.VMEM((WIDE, WIDE), F32),
+            pltpu.VMEM((512, 512), F32),
+            pltpu.VMEM((LANES, WIDE), F32),
+            pltpu.VMEM((TAP_ROWS, model), F32),
+        ],
+        name="final",
+    )(first, second, table)
+
 
 HEAD_DIM = 64
 KERNEL = 9
@@ -252,10 +421,10 @@
 MASK_FILL = -1e30
 INV_ROOT2 = 0.7071067811865476
 INV_ROOT_TWO_PI = 0.3989422804014327
-SHARED_ROWS = 24
+CUTS = 16
+TABLE_OWN = 72
+TABLE_ROWS = 112
 SWAP = [(0, 1), (1, 0)]
-BF16 = jnp.bfloat16
-F32 = jnp.float32
 
 
 class Group:
@@ -337,13 +506,11 @@
 EDGE = 8
 
 
-def spread_marks(marks_ref, columns_ref, masks_ref):
+def spread_marks(marks_ref, columns_ref):
     rows = marks_ref.shape[2]
     columns_ref[...] = jnp.transpose(
         jnp.concatenate([marks_ref[0], jnp.zeros((LANES - TAP_ROWS, rows), F32)], 0)
     )
-    for tap in range(KERNEL):
-        masks_ref[tap] = jnp.broadcast_to(columns_ref[:, tap : tap + 1], (rows, LANES))
 
 
 def head_lanes(head):
@@ -367,7 +534,7 @@
     hidden_ref, marks_ref, query_ref, key_ref, value_ref, conv_ref, point_ref, taps_ref, vec_ref, depth_ref, bias_ref,
     expand_ref, second_ref,
     q_ref, k_ref, v_ref, cv_ref, dl_ref, kc_ref, ca_ref, probs_ref, cc_ref, ctx_ref, lse_ref, second_all_ref,
-    rows_pad, conv_pad, masks, columns, weights, tops, tap_out, tap_in,
+    rows_pad, conv_pad, columns, weights, tops, tap_out, tap_in,
     send_sem, recv_sem, own_sem, gather_send, gather_recv,
 ):
     s = pl.program_id(0)
@@ -422,7 +589,7 @@
         conv_pad[:, :EDGE, :] = jnp.zeros((2, EDGE, LANES), F32)
         conv_pad[:, pl.ds(EDGE + rows, EDGE), :] = jnp.zeros((2, EDGE, LANES), F32)
 
-    spread_marks(marks_ref, columns, masks)
+    spread_marks(marks_ref, columns)
     hidden = hidden_ref[...]
     for c in range(chunks):
         rows_pad[c, pl.ds(EDGE, rows), :] = hidden[:, c * LANES : (c + 1) * LANES].astype(F32)
@@ -433,7 +600,7 @@
         base = pl.multiple_of(i * step, step)
         total = [jnp.zeros((step, LANES), F32)] * chunks
         for tap in range(KERNEL):
-            mask = masks[tap, pl.ds(base, step), :]
+            mask = jnp.broadcast_to(columns[pl.ds(base, step), tap : tap + 1], (step, LANES))
             for c in range(chunks):
                 moved = rows_pad[c, pl.ds(base + EDGE + tap - HALF, step), :]
                 total[c] = total[c] + (moved * mask) * depth_ref[tap : tap + 1, c * LANES : (c + 1) * LANES]
@@ -589,7 +756,6 @@
         scratch_shapes=[
             pltpu.VMEM((model // LANES, rows + 2 * EDGE, LANES), F32),
             pltpu.VMEM((2, rows + 2 * EDGE, LANES), F32),
-            pltpu.VMEM((KERNEL, rows, LANES), F32),
             pltpu.VMEM((rows, LANES), F32),
             pltpu.VMEM((rows, LANES), BF16),
             pltpu.VMEM((rows, LANES), F32),
@@ -638,7 +804,7 @@
 def middle_kernel(
     blocks,
     context_ref, conv_ref, context_late_ref, conv_late_ref, hidden_ref, grad_ref, grad_late_ref, out0_ref, out1_ref, inner_ref, outer_ref, vec_ref,
-    output_ref, residual_ref, grad_context_ref, grad_conv_ref, big_inner_ref, big_outer_ref, big_out_ref, small_ref,
+    output_ref, residual_ref, grad_context_ref, grad_conv_ref, pack_ref, small_ref,
     branch_ref, acc_out0, acc_out1, state, scale_ring, act_ring, slope_ring, low_ring, summed_ring, normed_ring, stat_ring,
     acc_inner, acc_outer, acc_small, acc_bias,
     branch_out, branch_in, stat1_out, stat1_in, stat2_out, stat2_in, stat3_out, stat3_in, back_out, back_in,
@@ -828,9 +994,13 @@
         for kind in range(5):
             for slot in range(SLOTS):
                 message(kind, *kinds[kind], slot).wait_send()
-        big_inner_ref[...] = acc_inner[...].astype(BF16)
-        big_outer_ref[...] = acc_outer[...].astype(BF16)
-        big_out_ref[...] = jnp.concatenate([acc_out0[:, : width // 2], acc_out1[:, : width // 2]], 1).astype(BF16)
+        cut, cut_ffn = 2 * width // CUTS, hidden_units // CUTS
+        for k in range(CUTS):
+            part, part_ffn = pl.ds(k * cut, cut), pl.ds(k * cut_ffn, cut_ffn)
+            both = jnp.concatenate([acc_out0[part, : width // 2], acc_out1[part, : width // 2]], 1)
+            pack_ref[k, pl.ds(0, cut), :] = both.astype(BF16)
+            pack_ref[k, pl.ds(cut, cut_ffn), :] = acc_inner[part_ffn, :].astype(BF16)
+            pack_ref[k, pl.ds(cut + cut_ffn, cut_ffn), :] = acc_outer[part_ffn, :].astype(BF16)
         small_ref[...] = jnp.zeros_like(small_ref)
         for row in range(6):
             small_ref[row : row + 1, :width] = jnp.sum(acc_small[row], axis=0, keepdims=True)
@@ -867,9 +1037,7 @@
             jax.ShapeDtypeStruct((tokens, width), F32),
             jax.ShapeDtypeStruct((tokens, local), BF16),
             jax.ShapeDtypeStruct((tokens, local), BF16),
-            jax.ShapeDtypeStruct((units, width), BF16),
-            jax.ShapeDtypeStruct((units, width), BF16),
-            jax.ShapeDtypeStruct((model, width), BF16),
+            jax.ShapeDtypeStruct((CUTS, (model + 2 * units) // CUTS, width), BF16),
             jax.ShapeDtypeStruct((8, units), F32),
         ),
         in_specs=[
@@ -877,7 +1045,7 @@
             block(width, 3),
             whole, whole, whole, whole, whole,
         ],
-        out_specs=(block(width, 3), block(width, 4), block(local, 5), block(local, 5), whole, whole, whole, whole),
+        out_specs=(block(width, 3), block(width, 4), block(local, 5), block(local, 5), whole, whole),
         scratch_shapes=[
             pltpu.VMEM((rows, model), BF16),
             pltpu.VMEM((model, local), F32),
@@ -906,12 +1074,15 @@
 
 
 def back_kernel(
-    seqs,
-    hidden_ref, grad_context, grad_conv_ref, residual_ref, marks_ref, q_ref, k_ref, v_ref, cv_ref, dl_ref, kc_ref, ca_ref, probs_ref,
-    lse_ref,
-    inputs_ref, point_ref, taps_ref, depth_ref, expand_ref, gather_ref,
-    own_ref, other_ref, big_qk_ref, big_vc_ref, big_point_ref, bias_ref, tap_grad_ref, tap_bias_ref, depth_grad_ref,
-    depth_pad, conv_pad, grad_pad, masks, columns, weights, shifted_weights, tap_terms, products,
+    seqs, count,
+    grad_context, grad_conv_ref, marks_ref, q_ref, k_ref, v_ref, cv_ref, ca_ref, probs_ref, lse_ref,
+    hidden_any, residual_any, dl_any, kc_any,
+    inputs_ref, point_ref, taps_ref, depth_ref, expand_ref, small_ref, pack_in_ref,
+    grad_ref, own_ref, other_ref, pack_ref, table_ref, reduced_ref,
+    hidden_ref, residual_ref, dl_ref, kc_ref, load_sem,
+    other_out, other_in, other_send, other_recv,
+    twin_in, side_in, deep_in, hop_send, hop_recv,
+    depth_pad, conv_pad, grad_pad, columns, weights, shifted_weights, tap_terms, products,
     grads, grad_q, grad_k, grad_v, rows_total, tap_all,
     acc_in, acc_point, acc_bias, acc_tap, acc_tap_bias, acc_depth,
     tap_out, tap_in, send_sem, recv_sem,
@@ -925,19 +1096,38 @@
     tap_rows = heads * TAP_ROWS
     half = chunks // 2
     slot = lax.rem(s, 2)
+    hops = Hops(count, pack_in_ref, twin_in, side_in, deep_in, hop_send, hop_recv)
+    here_rows = pl.ds(pl.multiple_of(s * rows, rows), rows)
+    loads = [
+        pltpu.make_async_copy(source.at[here_rows], target, load_sem.at[k])
+        for k, (source, target) in enumerate(
+            [(hidden_any, hidden_ref), (residual_any, residual_ref), (dl_any, dl_ref), (kc_any, kc_ref)]
+        )
+    ]
+    for load in loads:
+        load.start()
+
+    def swap_rows(which):
+        return pltpu.make_async_remote_copy(
+            src_ref=other_out.at[which],
+            dst_ref=other_in.at[which],
+            send_sem=other_send.at[which],
+            recv_sem=other_recv.at[which],
+            device_id=(dp, 1 - mp),
+            device_id_type=MESH,
+        )
 
     @pl.when(s == 0)
     def _():
-        barrier = pltpu.get_barrier_semaphore()
-        pl.semaphore_signal(barrier, inc=1, device_id=(dp, 1 - mp), device_id_type=MESH)
-        pl.semaphore_wait(barrier, 1)
+        greet_all(count)
+        hops.start_first()
         for pad in (depth_pad, conv_pad, grad_pad):
             for start in (0, EDGE + rows):
                 pad[:, pl.ds(start, EDGE), :] = jnp.zeros((pad.shape[0], EDGE, LANES), F32)
         for acc in (acc_in, acc_point, acc_bias, acc_tap, acc_tap_bias, acc_depth):
             acc[...] = jnp.zeros_like(acc)
 
-    spread_marks(marks_ref, columns, masks)
+    spread_marks(marks_ref, columns)
     block = 256
 
     for c in range(2):
@@ -974,7 +1164,7 @@
                     c, pl.ds(base + EDGE + HALF - j, conv_block), :
                 ]
             grads[part, 3 * WIDE + c * LANES : 3 * WIDE + (c + 1) * LANES] = total.astype(BF16)
-        tap_terms[part, :] = nn(products[...], gather_ref[...])
+        tap_terms[part, :] = nt(products[...], expand_ref[...])
         return carry
 
     lax.fori_loop(0, rows // conv_block, conv_step, 0)
@@ -1017,6 +1207,8 @@
 
     lax.fori_loop(0, rows // block, attention_step, 0)
 
+    for load in loads:
+        load.wait()
     swap_taps.wait()
     tap_all[...] = jnp.zeros_like(tap_all)
     tap_all[:tap_rows, :] = tap_out[slot].astype(F32)
@@ -1049,84 +1241,144 @@
     lax.fori_loop(0, rows // block, key_step, 0)
     acc_point[...] += tn(dl_ref[...], grads[:, 4 * WIDE : 5 * WIDE])
     acc_in[...] += tn(hidden_ref[...], grads[:, : 4 * WIDE])
-    step = 64
-
-    for c in range(chunks):
-        lanes = slice(c * LANES, (c + 1) * LANES)
-
-        def depth_step(i, carry, c=c, lanes=lanes):
-            base = pl.multiple_of(i * step, step)
-            part = pl.ds(base, step)
-            here = hidden_ref[part, lanes].astype(F32)
-            total = rows_total[c, part, :]
-            sums = []
-            for j in range(KERNEL):
-                mirror = KERNEL - 1 - j
-                near = depth_pad[c, pl.ds(base + EDGE + j - HALF, step), :] * masks[j, part, :]
-                total = total + near * depth_ref[mirror : mirror + 1, lanes]
-                sums.append(carry[j] + jnp.sum((near * here).reshape(step // 8, 8, LANES), axis=0))
-            rows_total[c, part, :] = total
-            return tuple(sums)
-
-        sums = lax.fori_loop(0, rows // step, depth_step, tuple(jnp.zeros((8, LANES), F32) for _ in range(KERNEL)))
+    step = 32
+
+    def depth_step(i, carry):
+        base = pl.multiple_of(i * step, step)
+        part = pl.ds(base, step)
+        total = [rows_total[c, part, :] for c in range(chunks)]
         for j in range(KERNEL):
-            acc_depth[KERNEL - 1 - j, :, lanes] += sums[j]
+            mirror = KERNEL - 1 - j
+            mask = jnp.broadcast_to(columns[part, j : j + 1], (step, LANES))
+            for c in range(chunks):
+                lanes = slice(c * LANES, (c + 1) * LANES)
+                near = depth_pad[c, pl.ds(base + EDGE + j - HALF, step), :] * mask
+                total[c] = total[c] + near * depth_ref[mirror : mirror + 1, lanes]
+                acc_depth[mirror, :, lanes] += row_sums(near * hidden_ref[part, lanes].astype(F32))
+        for c in range(chunks):
+            rows_total[c, part, :] = total[c]
+        return carry
+
+    lax.fori_loop(0, rows // step, depth_step, 0)
+
+    @pl.when(s >= 1)
+    def _():
+        which = s - 1
+        swap_rows(which).wait_recv()
+        grad_ref[...] = own_ref[...] + other_in[which].astype(F32)
+
     for c in range(half):
         lanes = slice(c * LANES, (c + 1) * LANES)
         own_ref[:, lanes] = rows_total[mp * half + c] + residual_ref[:, lanes]
-        other_ref[:, lanes] = rows_total[(1 - mp) * half + c].astype(BF16)
+
+    @pl.when(s < seqs - 1)
+    def _():
+        for c in range(half):
+            lanes = slice(c * LANES, (c + 1) * LANES)
+            other_out[s, :, lanes] = rows_total[(1 - mp) * half + c].astype(BF16)
+        swap_rows(s).start()
+
+    @pl.when(s == 0)
+    def _():
+        hops.start_second()
+
+    @pl.when(s == min(1, seqs - 1))
+    def _():
+        hops.start_third()
 
     @pl.when(s == seqs - 1)
     def _():
+        for c in range(half):
+            lanes = slice(c * LANES, (c + 1) * LANES)
+            other_ref[:, lanes] = rows_total[(1 - mp) * half + c].astype(BF16)
+        hops.finish(reduced_ref)
+        for which in range(seqs - 1):
+            swap_rows(which).wait_send()
         width = heads * HEAD_DIM
-
-        def pair(first, second):
-            return jnp.concatenate([first[:, :width], second[:, :width]], 1).astype(BF16)
-
-        big_qk_ref[...] = pair(acc_in[:, :WIDE], acc_in[:, WIDE : 2 * WIDE])
-        big_vc_ref[...] = pair(acc_in[:, 2 * WIDE : 3 * WIDE], acc_in[:, 3 * WIDE :])
-        big_point_ref[...] = pair(acc_point[...], jnp.zeros_like(acc_point))
-        bias_ref[...] = jnp.sum(acc_bias[...], axis=0, keepdims=True) + jnp.zeros_like(bias_ref)
-        tap_grad_ref[...] = acc_tap[...]
-        tap_bias_ref[...] = jnp.sum(acc_tap_bias[...], axis=1, keepdims=True) + jnp.zeros_like(tap_bias_ref)
+        group = model // 2
+        cut = model // CUTS
+        empty = jnp.zeros((cut, width), F32)
+        for k in range(CUTS):
+            part = pl.ds(k * cut, cut)
+            for place in range(2):
+                first = acc_in[part, 2 * place * WIDE : 2 * place * WIDE + width]
+                second = acc_in[part, (2 * place + 1) * WIDE : (2 * place + 1) * WIDE + width]
+                pack_ref[k, pl.ds(place * cut, cut), :] = jnp.concatenate([first, second], 1).astype(BF16)
+            pack_ref[k, pl.ds(2 * cut, cut), :] = jnp.concatenate([acc_point[part, :width], empty], 1).astype(BF16)
+        table_ref[...] = jnp.zeros_like(table_ref)
+        lane = lax.broadcasted_iota(jnp.int32, (LANES, WIDE), 1)
+        taps = jnp.where(lane == width, jnp.sum(acc_tap_bias[...], axis=1, keepdims=True), acc_tap[...])
+        own_taps = [taps[h * TAP_ROWS : h * TAP_ROWS + KERNEL] for h in range(heads)]
+        other_taps = [taps[tap_rows + h * TAP_ROWS : tap_rows + h * TAP_ROWS + KERNEL] for h in range(heads)]
+        for h in range(heads):
+            table_ref[KERNEL * h : KERNEL * (h + 1), :] = jnp.where(mp == 0, own_taps[h], other_taps[h])
+            later = KERNEL * (heads + h)
+            table_ref[later : later + KERNEL, :] = jnp.where(mp == 0, other_taps[h], own_taps[h])
+        for row, place in ((54, 0), (55, 2), (56, 4), (57, 3)):
+            table_ref[row : row + 1, :] = jnp.sum(acc_bias[:, place * WIDE : (place + 1) * WIDE], axis=0, keepdims=True)
+
+        def lay(row, value):
+            for k in range(-(-value.shape[1] // WIDE)):
+                piece = value[:, k * WIDE : (k + 1) * WIDE]
+                table_ref[row + k : row + k + 1, : piece.shape[1]] = piece
+
+        for row, source in ((58, 0), (60, 1), (62, 2)):
+            lay(row, small_ref[source : source + 1, :group])
+        lay(64, small_ref[6:7, :])
+        for row, source in ((99, 3), (102, 4), (105, 5)):
+            value = small_ref[source : source + 1, :group]
+            blank = jnp.zeros_like(value)
+            lay(row, jnp.where(mp == 0, jnp.concatenate([value, blank], 1), jnp.concatenate([blank, value], 1)))
         for j in range(KERNEL):
-            depth_grad_ref[j : j + 1, :] = jnp.sum(acc_depth[j], axis=0, keepdims=True)
-        depth_grad_ref[KERNEL:, :] = jnp.zeros((TAP_ROWS - KERNEL, model), F32)
-
-
-def back(hidden, grad_context, grad_conv, residual, marks, kept, w, taps, depth, expand, ident):
+            total = jnp.sum(acc_depth[j], axis=0, keepdims=True)
+            for k in range(model // WIDE):
+                row = TABLE_OWN + KERNEL * k + j
+                table_ref[row : row + 1, :] = total[:, k * WIDE : (k + 1) * WIDE]
+
+
+def back(hidden, grad_context, grad_conv, residual, marks, kept, w, taps, depth, expand, small, pack, count, ident):
     q, k, v, cv, dl, kc, ca, probs, lse = kept
     seqs, _, rows = marks.shape
     tokens, model = hidden.shape
     width = model // 2
     tap_rows = probs.shape[1]
-
-    def seq(columns):
-        return by_seq(rows, columns)
-
-    def shape(columns, kind, count=tokens):
-        return jax.ShapeDtypeStruct((count, columns), kind)
-
+    wide = by_seq(rows, WIDE)
+    place = pl.BlockSpec(memory_space=pl.ANY)
     padded_rows = rows + 2 * EDGE
     vmem = pltpu.VMEM
+    swaps = max(seqs - 1, 1)
     return pl.pallas_call(
-        functools.partial(back_kernel, seqs),
+        functools.partial(back_kernel, seqs, count),
         grid=(seqs,),
         out_shape=(
-            shape(width, F32), shape(width, BF16),
-            shape(width, BF16, model), shape(width, BF16, model), shape(width, BF16, model),
-            shape(5 * WIDE, F32, 8), shape(WIDE, F32, LANES), shape(LANES, F32, LANES), shape(model, F32, TAP_ROWS),
+            jax.ShapeDtypeStruct((tokens, width), F32),
+            jax.ShapeDtypeStruct((rows, width), F32),
+            jax.ShapeDtypeStruct((rows, width), BF16),
+            jax.ShapeDtypeStruct((CUTS, 3 * model // CUTS, width), BF16),
+            jax.ShapeDtypeStruct((TABLE_ROWS, WIDE), F32),
+            jax.ShapeDtypeStruct(pack.shape[1:], F32),
         ),
-        in_specs=[
-            seq(model), seq(WIDE), seq(WIDE), seq(width), by_seq_row(TAP_ROWS, rows), seq(WIDE), seq(WIDE), seq(WIDE), seq(WIDE),
-            seq(model), seq(WIDE), seq(WIDE), by_seq_row(tap_rows, rows), by_seq_row(8, rows),
-        ] + [whole()] * 6,
-        out_specs=(seq(width), seq(width)) + (whole(),) * 7,
+        in_specs=[wide, wide, by_seq_row(TAP_ROWS, rows), wide, wide, wide, wide, wide]
+        + [by_seq_row(tap_rows, rows), by_seq_row(8, rows)]
+        + [place] * 4
+        + [whole()] * 7,
+        out_specs=(pl.BlockSpec((rows, width), lambda s: (jnp.maximum(s - 1, 0), 0)),) + (whole(),) * 5,
         scratch_shapes=[
+            vmem((rows, model), BF16),
+            vmem((rows, width), F32),
+            vmem((rows, model), BF16),
+            vmem((rows, WIDE), F32),
+            pltpu.SemaphoreType.DMA((4,)),
+            vmem((swaps, rows, width), BF16),
+            vmem((swaps, rows, width), BF16),
+            pltpu.SemaphoreType.DMA((swaps,)),
+            pltpu.SemaphoreType.DMA((swaps,)),
+        ]
+        + hop_scratch(count, pack.shape[1], pack.shape[2])
+        + [
             vmem((model // LANES, padded_rows, LANES), F32),
             vmem((2, padded_rows, LANES), F32),
             vmem((2, padded_rows, LANES), F32),
-            vmem((KERNEL, rows, LANES), F32),
             vmem((rows, LANES), F32),
             vmem((rows, LANES), BF16),
             vmem((rows, LANES), BF16),
@@ -1150,13 +1402,12 @@
             pltpu.SemaphoreType.DMA((2,)),
         ],
         compiler_params=pltpu.CompilerParams(
-            collective_id=ident, has_side_effects=True, vmem_limit_bytes=62 << 20
+            collective_id=ident, has_side_effects=True, vmem_limit_bytes=63 << 20
         ),
         name="back",
     )(
-        hidden, grad_context, grad_conv, residual, marks, q, k, v, cv, dl, kc, ca, probs, lse,
-        jnp.concatenate([w.query, w.key, w.value, w.conv], 1), w.point, taps, depth, expand,
-        jnp.pad(expand[:tap_rows], ((0, LANES - tap_rows), (0, 0))).T,
+        grad_context, grad_conv, marks, q, k, v, cv, ca, probs, lse, hidden, residual, dl, kc,
+        jnp.concatenate([w.query, w.key, w.value, w.conv], 1), w.point, taps, depth, expand, small, pack,
     )
 
 
@@ -1179,6 +1430,34 @@
     rows = value.shape[-2]
     extra = -rows % multiple
     return jnp.pad(value, [(0, 0)] * (value.ndim - 2) + [(0, extra), (0, 0)])
+
+
+def recut(pack, sizes, count):
+    if count == CUTS:
+        return pack
+    unit, parts, start = pack.shape[1] // sum(sizes), [], 0
+    for size in sizes:
+        rows = pack[:, start : start + size * unit].reshape(-1, pack.shape[2])
+        parts.append(rows.reshape(count, -1, pack.shape[2]))
+        start += size * unit
+    return padded(jnp.concatenate(parts, 1), 16)
+
+
+def final_plain(first, second, table, share, share_ffn, width, group, taps):
+    model = 2 * group
+    depth = jnp.concatenate([table[72 + KERNEL * k : 72 + KERNEL * (k + 1)] for k in range(model // WIDE)], 1)
+    row = lambda at_row, size: table[at_row : at_row + 6].reshape(1, -1)[:, :size]
+    out = first[:share]
+    return (
+        second[:share, :width], second[:share, width:], second[share : 2 * share, :width],
+        row(54, width), row(55, width),
+        lax.dynamic_slice_in_dim(depth, lax.axis_index("dp") * share, share, 1),
+        second[2 * share : 3 * share, :width], row(56, width),
+        table[:taps, :width].T, table[None, :taps, width], second[share : 2 * share, width:], row(57, width),
+        jnp.stack([out[:, :width].T, out[:, width:].T]), row(105, model), row(99, model), row(102, model),
+        first[share : share + share_ffn].T, row(64, 4 * group), first[share + share_ffn : share + 2 * share_ffn],
+        row(58, group), row(60, group), row(62, group),
+    )
 
 
 def on_device(
@@ -1250,95 +1529,26 @@
     w.out1 = cut_wide(second_all, 0, width)
     w.inner = cut(second_all, share, share_ffn, 0, group)
     w.outer = cut(second_all, share + share_ffn, share_ffn, 0, group)
-    output, grad_residual, grad_context, grad_conv, big_inner, big_outer, big_out, sums_mid = middle(
+    output, grad_residual, grad_context, grad_conv, pack_mid, sums_mid = middle(
         ctx, cc, hidden, out_grad, w, p, me, 4
     )
-    depth = w.depth.astype(F32)
-    part_own, part_other, big_qk, big_vc, big_point, bias_sums, tap_grads, tap_bias, depth_grads = back(
+    grad_input, own_last, other_last, pack_back, table, first_sum = back(
         hidden, grad_context, grad_conv, grad_residual, marks, (q, k, v, cv, dl, kc, ca, probs, lse),
-        w, taps, depth, expand, 5,
-    )
-    grad_input = part_own + swap(part_other).astype(F32)
-
-    def both(value):
-        value = value[: 2 * heads * TAP_ROWS].reshape(2, heads, TAP_ROWS, -1)[:, :, :KERNEL]
-        return jnp.where(me == 0, value, value[::-1]).reshape(2 * heads * KERNEL, -1)
-
-    kernel_weight_grad = both(tap_grads)[:, :width].T
-    kernel_bias_grad = both(tap_bias)[:, 0]
-
-    def bias_of(place):
-        return bias_sums[0, place * WIDE : place * WIDE + width]
-
-    def widened(value):
-        empty = jnp.zeros_like(value)
-        return jnp.where(me == 0, jnp.concatenate([value, empty]), jnp.concatenate([empty, value]))
-
-
-    def blocks(value):
-        return value.reshape(count, value.shape[0] // count, value.shape[1])
-
-    pieces = [blocks(value) for value in (big_qk, big_vc, big_point, big_out, big_inner, big_outer)]
-    pieces = jnp.concatenate(pieces, 1)
-    own_parts = [
-        bias_of(0), bias_of(2), bias_of(4), kernel_weight_grad, kernel_bias_grad,
-        bias_of(3), sums_mid[6], sums_mid[0, :group], sums_mid[1, :group], sums_mid[2, :group],
-    ]
-    columns = group
-
-    def table(parts, rows):
-        flat = jnp.concatenate([part.reshape(-1) for part in parts])
-        return jnp.pad(flat, (0, rows * columns - flat.shape[0])).reshape(rows, columns)
-
-    own_size = sum(part.size for part in own_parts)
-    own_rows = -(-own_size // columns)
-    own_rows += -own_rows % 8
-    shared_parts = [depth_grads[:KERNEL]] + [widened(sums_mid[k, :group]) for k in (3, 4, 5)]
-    smalls = jnp.concatenate([table(own_parts, own_rows), table(shared_parts, SHARED_ROWS)], 0)
-    sums, totals = scatter(padded(pieces, 16), smalls, count, 3)
-
-    def untable(value, parts):
-        flat, result, start = value.reshape(-1), [], 0
-        for part in parts:
-            result.append(flat[start : start + part.size].reshape(part.shape))
-            start += part.size
-        return result
-
-    query_b, value_b, point_b, kernel_w, kernel_b, conv_b, in_b, outer_b, gain2, bias2 = untable(
-        totals[:own_rows], own_parts
-    )
-    depth_g, gain1, bias1, out_b = untable(totals[own_rows:], shared_parts)
-    place = lax.axis_index("dp")
-    depth_own = lax.dynamic_slice_in_dim(depth_g, place * share, share, 1)
-    at_rows = lambda k: sums[k * share : (k + 1) * share]
-    qk, vc, po, oo = at_rows(0), at_rows(1), at_rows(2), at_rows(3)
-    inner_own = sums[4 * share : 4 * share + share_ffn]
-    outer_own = sums[4 * share + share_ffn : 4 * share + 2 * share_ffn]
+        w, taps, w.depth.astype(F32), expand, sums_mid, recut(pack_mid, (1, 2, 2), count), count, 5,
+    )
+    second_sum, totals, grad_input = tail(
+        recut(pack_back, (1, 1, 1), count), table, own_last, other_last, grad_input, count, 3
+    )
+    small_cuts = (share, share_ffn, width, group, 2 * heads * KERNEL)
+    if share % TAP_ROWS == 0:
+        results = final(first_sum, second_sum, totals, *small_cuts, count)
+    else:
+        results = final_plain(first_sum, second_sum, totals, *small_cuts)
+    q_g, k_g, v_g, q_b, v_b, depth_g, p_g, p_b, kw_g, kb_g, c_g, c_b, out_g, out_b, gain1, bias1 = results[:16]
+    inner_g, inner_b, outer_g, outer_b, gain2, bias2 = results[16:]
     return (
-        output,
-        grad_input,
-        qk[:, :width],
-        qk[:, width:],
-        vc[:, :width],
-        query_b,
-        value_b,
-        depth_own,
-        po[:, :width],
-        point_b,
-        kernel_w,
-        kernel_b,
-        vc[:, width:],
-        conv_b,
-        jnp.stack([oo[:, :width].T, oo[:, width:].T]),
-        out_b,
-        gain1,
-        bias1,
-        inner_own.T[None],
-        in_b[None],
-        outer_own[None],
-        outer_b,
-        gain2,
-        bias2,
+        output, grad_input, q_g, k_g, v_g, q_b[0], v_b[0], depth_g, p_g, p_b[0], kw_g, kb_g[0], c_g, c_b[0], out_g,
+        out_b[0], gain1[0], bias1[0], inner_g[None], inner_b, outer_g[None], outer_b[0], gain2[0], bias2[0],
     )
 
 

time: 459 us -> 412 us (0.90)
  local copies, waits for them, and re-layouts: 54.4 us -> 28 us
  Pallas kernels: 383 us -> 367 us
    pallas_call x2 -> x3, Pallas kernels: 164 us -> 147 us  [the longest x1 110 us: back(): pl.pallas_call(functools.partial(back_kernel, seqs, count), grid=(seqs,),...]
    slice x17 -> x0, local copies, waits for them, and re-layouts: 13.1 us -> none  [the longest x10 5.49 us: untable(): result.append(flat[start:start + part.size].reshape(part.shape))]
    pallas_call x0 -> x6, other arithmetic: none -> 7.59 us  [final(): pl.pallas_call(functools.partial(final_kernel, count), out_shape=(shape(s...]
    reshape x9 -> x0, local copies, waits for them, and re-layouts: 6.92 us -> none  [the longest x2 2.45 us: table(): flat = jnp.concatenate([part.reshape(-1) for part in parts])]
    add x2 -> x0, other arithmetic: 5.06 us -> none  [the longest x1 5.05 us: on_device(): grad_input = part_own + swap(part_other).astype(F32)]
    unnamed x66 -> x52, local copies, waits for them, and re-layouts: 8.25 us -> 11.2 us
  transfers between devices with their start and end apart: 1 -> 0, of which waited for: 0 -> 0; matrix products, arithmetic and copies ran while one was open for 9% -> 0% of each run, Pallas kernels for 14% -> 0%
where the time goes in v3:
time: 412 us; the launch traced here: 410 us
  Pallas kernels  367 us (89%)
  local copies, waits for them, and re-layouts  28 us (7%)
  other arithmetic  14.3 us (3%)
    pallas_call x1, Pallas kernels, middle(): pl.pallas_call(functools.partial(middle_kernel, blocks), grid=(blocks + 5...  128 us
    pallas_call x1, Pallas kernels, back(): pl.pallas_call(functools.partial(back_kernel, seqs, count), grid=(seqs,),...  110 us
    pallas_call x1, Pallas kernels, front(): pl.pallas_call(functools.partial(front_kernel, seqs, count), grid=(seqs,)...  71.9 us
    pallas_call x1, Pallas kernels, tail(): pl.pallas_call(functools.partial(tail_kernel, count, start), out_shape=(j...  34.4 us
    pallas_call x1, Pallas kernels, gather(): pl.pallas_call(functools.partial(gather_kernel, count), out_shape=jax.Sha...  19.7 us
    unnamed x52, local copies, waits for them, and re-layouts  11.2 us

profile of v3, /device:TPU:8, one launch (start us, length us, event | category | flops | bytes accessed | tf_op | source)
XLA Modules:
  0.0 410.2 jit_solution(8222603182358797603)
XLA Ops:
  0.7 0.8 slice_bitcast_fusion.4
  1.5 0.2 reduce-window.26
  1.6 0.1 convert_reduce_fusion
  1.7 0.1 fusion.47
  1.9 0.1 stack.260
  2.0 0.2 reduce-window.25
  2.1 0.1 convert_reduce_fusion.1
  2.2 0.1 fusion.55
  2.3 0.1 stack.242
  2.4 0.2 reduce-window.24
  2.6 0.1 convert_reduce_fusion.2
  2.7 0.1 fusion.63
  2.8 0.1 stack.224
  2.9 0.7 pad_maximum_fusion.1.marks_ref
  3.6 0.8 copy.65
  4.3 1.5 fusion.16.own_ref
  5.9 19.7 %weight_gather.1 = bf16[16,144,384]{2,1,0:T(8,128)(2,1)} custom-call(bf16[1,144,384]{2,1,0:T(8,128)(2,1)} %fusion.16.own_ref), custom_call_target="tpu_custom_call" | custom-call | tf_op jit(solution)/shard_map/weight_gather/pallas_call | solution.py:93
  25.6 1.8 fusion.73
  27.4 0.8 pad.77.query_ref
  28.3 0.8 pad.78.key_ref
  29.1 0.8 pad.79.value_ref
  29.9 0.8 pad.80.conv_ref
  30.8 0.8 pad.81.point_ref
  31.6 0.6 pad.83.taps_ref
  32.3 0.0 copy-done.21
  32.3 0.6 stack.267.vec_ref
  33.0 1.0 slice.149
  34.1 0.8 copy.70
  34.8 0.0 copy-done.22
  34.8 0.1 reshape.198
  34.9 0.1 broadcast_in_dim.26
  35.0 0.7 broadcast_in_dim.27.bias_ref
  35.7 1.2 fusion.9.expand_ref
  37.0 0.8 maximum_bitcast_fusion.second_ref
  37.7 71.9 %front.1 = (bf16[3072,256]{1,0:T(8,128)(2,1)}, bf16[3072,256]{1,0:T(8,128)(2,1)}, bf16[3072,256]{1,0:T(8,128)(2,1)}, f32[3072,256]{1,0:T(8,128)}, bf16[3072,768]...) custom-call(bf16[3072,768]{1,0:T(8,128)(2,1)} %hidden_any.1, ...), custom_call_target="tpu_custom_call" | custom-call | tf_op jit(solution)/shard_map/front/pallas_call | solution.py:738
  109.7 1.4 fusion.72
  111.1 0.8 pad.89.out0_ref
  112.0 0.8 pad.90.out1_ref
  112.8 0.0 copy-start.12
  112.8 0.0 copy-start.13
  112.8 0.0 copy-start.14
  112.8 0.0 copy-start.11
  112.8 1.7 fusion.71
  114.5 0.1 dynamic_slice.13
  114.6 0.1 dynamic_slice.14
  114.7 0.1 dynamic_slice.15
  114.9 0.7 stack.274.vec_ref
  115.6 128.3 %middle.1 = (bf16[3072,384]{1,0:T(8,128)(2,1)}, f32[3072,384]{1,0:T(8,128)}, bf16[3072,256]{1,0:T(8,128)(2,1)}, bf16[3072,256]{1,0:T(8,128)(2,1)}, bf16[16,240,384]{2,1,0:T(8,128)(2,1)}, /*index=5*/f32[8,1536]{1,0:T(8,128)}) custom-call(bf16[3072,256]{1,0:T(8,128)(2,1)} %get-tuple-element.73.context_ref.context_late_ref, ...), custom_call_target="tpu_custom_call" | custom-call | tf_op jit(solution)/shard_map/middle/pallas_call | solution.py:1032
  243.9 1.4 pad_maximum_fusion.inputs_ref
  245.3 110.2 %back.1 = (f32[3072,384]{1,0:T(8,128)}, f32[1024,384]{1,0:T(8,128)}, bf16[1024,384]{1,0:T(8,128)(2,1)}, bf16[16,144,384]{2,1,0:T(8,128)(2,1)}, f32[112,256]{1,0:T(8,128)}, /*index=5*/f32[240,384]{1,0:T(8,128)}) custom-call(bf16[3072,256]{1,0:T(8,128)(2,1)} %get-tuple-element.77.grad_context, bf16[3072,256]{1,0:T(8,128)(2,1)} %get-tuple-element.78.grad_conv_ref, ...), custom_call_target="tpu_custom_call" | custom-call | tf_op jit(solution)/shard_map/back/pallas_call | solution.py:1350
  355.5 34.4 %tail.1 = (f32[144,384]{1,0:T(8,128)}, f32[112,256]{1,0:T(8,128)}, f32[3072,384]{1,0:T(8,128)}) custom-call(bf16[16,144,384]{2,1,0:T(8,128)(2,1)} %get-tuple-element.91.in_ref, f32[112,256]{1,0:T(8,128)} %get-tuple-element.92.table_ref, f32[1024,384]{1,0:T(8,128)} %get-tuple-element.93.own_ref, ...), custom_call_target="tpu_custom_call", output_to_operand_aliasing={{2}: (4, {})} | custom-call | tf_op jit(solution)/shard_map/tail/pallas_call | solution.py:310
  389.9 2.3 final.1
  392.2 1.6 copy.67
  393.8 1.7 copy.68
  395.5 1.3 reduce
  396.8 1.3 reduce.1
  398.1 1.3 reduce.2
  399.3 1.7 copy.69
  401.0 1.3 reduce.3
  402.3 1.2 reduce.4
  403.5 1.3 reduce.5
  404.8 1.4 copy.74
  406.2 1.8 copy-done
  408.0 2.2 copy.75
  (74 shorter events, 0.3 us)
Async XLA Ops:
  28.3 3.3 copy-start.10
  29.1 3.2 copy-start.18
  29.1 3.2 copy-start.19
  29.1 3.2 copy-start.20
  29.1 3.2 copy-start.21
  29.9 4.9 %copy-start.22 = (f32[54]{0:T(128)S(1)}, f32[54]{0:T(128)}, u32[]{:S(2)}) copy-start(f32[54]{0:T(128)} %param.36) | copy-start | bytes 652
  30.7 6.2 %copy-start.9 = (bf16[2,192,48]{1,2,0:T(8,128)(2,1)S(1)}, bf16[2,192,48]{1,2,0:T(8,128)(2,1)}, u32[]{:S(2)}) copy-start(bf16[2,192,48]{1,2,0:T(8,128)(2,1)} %param.39) | copy-start | bytes 110596
  30.7 6.2 %copy-start.7 = (bf16[1,96,384]{2,1,0:T(8,128)(2,1)S(1)}, bf16[1,96,384]{2,1,0:T(8,128)(2,1)}, u32[]{:S(2)}) copy-start(bf16[1,96,384]{2,1,0:T(8,128)(2,1)} %param.45) | copy-start | bytes 221188
  30.8 6.2 %copy-start.8 = (bf16[1,384,96]{1,2,0:T(8,128)(2,1)S(1)}, bf16[1,384,96]{1,2,0:T(8,128)(2,1)}, u32[]{:S(2)}) copy-start(bf16[1,384,96]{1,2,0:T(8,128)(2,1)} %param.43) | copy-start | bytes 221188
  109.7 3.1 copy-start.5
  112.8 1.7 copy-start.15
  112.8 1.8 copy-start.16
  112.8 1.9 copy-start.17
  112.8 2.0 copy-start.12
  112.8 2.0 copy-start.13
  112.8 2.1 copy-start.14
  112.8 2.1 copy-start.11
  115.6 128.3 %copy-start.1 = (bf16[768,256]{1,0:T(8,128)(2,1)S(1)}, bf16[768,256]{1,0:T(8,128)(2,1)}, u32[]{:S(2)}) copy-start(bf16[768,256]{1,0:T(8,128)(2,1)} %pad.77.query_ref) | copy-start | bytes 1179652
  115.6 128.3 %copy-start.2 = (bf16[768,256]{1,0:T(8,128)(2,1)S(1)}, bf16[768,256]{1,0:T(8,128)(2,1)}, u32[]{:S(2)}) copy-start(bf16[768,256]{1,0:T(8,128)(2,1)} %pad.78.key_ref) | copy-start | bytes 1179652
  115.6 128.3 %copy-start.3 = (bf16[768,256]{1,0:T(8,128)(2,1)S(1)}, bf16[768,256]{1,0:T(8,128)(2,1)}, u32[]{:S(2)}) copy-start(bf16[768,256]{1,0:T(8,128)(2,1)} %pad.79.value_ref) | copy-start | bytes 1179652
  115.6 128.3 %copy-start.4 = (bf16[768,256]{1,0:T(8,128)(2,1)S(1)}, bf16[768,256]{1,0:T(8,128)(2,1)}, u32[]{:S(2)}) copy-start(bf16[768,256]{1,0:T(8,128)(2,1)} %pad.80.conv_ref) | copy-start | bytes 1179652
  355.5 49.3 %copy-start.6 = (bf16[3072,384]{1,0:T(8,128)(2,1)S(1)}, bf16[3072,384]{1,0:T(8,128)(2,1)}, u32[]{:S(2)}) copy-start(bf16[3072,384]{1,0:T(8,128)(2,1)} %get-tuple-element.290) | copy-start | bytes 7077892
  404.8 3.2 copy-start

commit v4 on v3

--- a/solution.py
+++ b/solution.py
@@ -10,6 +10,17 @@
 MESH = pl.DeviceIdType.MESH
 BF16 = jnp.bfloat16
 F32 = jnp.float32
+HEAD_DIM = 64
+KERNEL = 9
+HALF = KERNEL // 2
+CUTS = 16
+TABLE_OWN = 72
+TABLE_ROWS = 112
+TAP_ROWS = 16
+WIDE = 256
+LANES = 128
+EDGE = 8
+MOST_DOC = 512
 
 
 def at(dp, mp):
@@ -38,10 +49,20 @@
     pl.semaphore_wait(barrier, len(peers))
 
 
-def gather_kernel(count, own_ref, out_ref, own_sem, send_sem, recv_sem):
+def turned(tile, value):
+    rows, columns = value.shape
+    tile[...] = jnp.zeros_like(tile)
+    tile[:rows, :columns] = value.astype(F32)
+    return jnp.transpose(tile[...])[:columns, :rows]
+
+
+def beside_each(first, second):
+    return jnp.concatenate([first.astype(F32), second.astype(F32)], 1).astype(BF16)
+
+
+def gather_body(count, own_ref, out_ref, own_sem, send_sem, recv_sem):
     mp, core, side, deep, parts = places(count)
     me = index_of(deep, side, core)
-    greet(count)
     local = pltpu.make_async_copy(own_ref.at[0], out_ref.at[me], own_sem)
     local.start()
     started = []
@@ -67,6 +88,7 @@
         push(own_ref.at[0], me, index_of(lax.rem(deep + k, parts), side, core))
     push(own_ref.at[0], me, beside)
     push(own_ref.at[0], me, twin)
+    yield
     arrive(beside)
     push(out_ref.at[beside], beside, twin)
     for k in range(1, parts):
@@ -84,20 +106,72 @@
     for copy in started:
         copy.wait_send()
     local.wait()
+    yield
+
+
+def gather_kernel(count, own_ref, out_ref, own_sem, send_sem, recv_sem):
+    greet(count)
+    for _ in gather_body(count, own_ref, out_ref, own_sem, send_sem, recv_sem):
+        pass
+
+
+def pack_kernel(
+    count, q_ref, k_ref, v_ref, c_ref, p_ref, depth_ref, out_w_ref, in_w_ref, outer_w_ref,
+    out_ref, second_ref,
+    own_ref, tile_depth, own_sem, send_sem, recv_sem,
+):
+    share, width = q_ref.shape
+    share_ffn = outer_w_ref.shape[1]
+    own_ref[0, :share, :] = beside_each(q_ref[...], k_ref[...])
+    own_ref[0, share : 2 * share, :] = beside_each(v_ref[...], c_ref[...])
+    depth = turned(tile_depth, depth_ref[...])
+    depth = jnp.concatenate([depth, jnp.zeros((share, width - KERNEL), F32)], 1)
+    own_ref[0, 2 * share : 3 * share, :] = beside_each(p_ref[...], depth)
+    greet(count)
+    moves = gather_body(count, own_ref, out_ref, own_sem, send_sem, recv_sem)
+    next(moves)
+    second_ref[0, :share, :] = beside_each(out_w_ref[0], out_w_ref[1])
+    second_ref[0, share : share + share_ffn, :] = in_w_ref[0]
+    second_ref[0, share + share_ffn :, :] = outer_w_ref[0]
+    next(moves)
+
+
+def gather_first(weights, count, ident):
+    q, depth, out_w, in_w, outer_w = weights[0], weights[5], weights[6], weights[7], weights[8]
+    share, width = q.shape
+    share_ffn, group = outer_w.shape[1:]
+    parts = count // 4
+    vmem = pl.BlockSpec(memory_space=pltpu.VMEM)
+    return pl.pallas_call(
+        functools.partial(pack_kernel, count),
+        out_shape=(
+            jax.ShapeDtypeStruct((count, 3 * share, 2 * width), BF16),
+            jax.ShapeDtypeStruct((1, share + 2 * share_ffn, group), BF16),
+        ),
+        in_specs=[vmem] * 9,
+        out_specs=(pl.BlockSpec(memory_space=pl.ANY), vmem),
+        scratch_shapes=[
+            pltpu.VMEM((1, 3 * share, 2 * width), BF16),
+            pltpu.VMEM((LANES, LANES), F32),
+            pltpu.SemaphoreType.DMA,
+            pltpu.SemaphoreType.DMA((4 * parts - 1,)),
+            pltpu.SemaphoreType.DMA((count,)),
+        ],
+        compiler_params=pltpu.CompilerParams(collective_id=ident, has_side_effects=True),
+        name="weight_gather",
+    )(*weights)
 
 
 def gather(own, count, ident):
     parts = count // 4
-    sends = (parts - 1) * 4 + 3
-    shape = (count,) + own.shape[1:]
     return pl.pallas_call(
         functools.partial(gather_kernel, count),
-        out_shape=jax.ShapeDtypeStruct(shape, own.dtype),
+        out_shape=jax.ShapeDtypeStruct((count,) + own.shape[1:], own.dtype),
         in_specs=[pl.BlockSpec(memory_space=pl.ANY)],
         out_specs=pl.BlockSpec(memory_space=pl.ANY),
         scratch_shapes=[
             pltpu.SemaphoreType.DMA,
-            pltpu.SemaphoreType.DMA((sends,)),
+            pltpu.SemaphoreType.DMA((4 * parts - 1,)),
             pltpu.SemaphoreType.DMA((count,)),
         ],
         compiler_params=pltpu.CompilerParams(collective_id=ident, has_side_effects=True),
@@ -340,18 +414,11 @@
     return jnp.concatenate([table[row + k : row + k + 1, :] for k in range(count)], 1)
 
 
-def turned(tile, value):
-    rows, columns = value.shape
-    tile[...] = jnp.zeros_like(tile)
-    tile[:rows, :columns] = value
-    return jnp.transpose(tile[...])[:columns, :rows]
-
-
 def final_kernel(
     count, first_ref, second_ref, table_ref,
     q_ref, k_ref, v_ref, qb_ref, vb_ref, depth_ref, p_ref, pb_ref, kw_ref, kb_ref, c_ref, cb_ref, out_ref, ob_ref,
     gain1_ref, bias1_ref, inner_ref, inb_ref, outer_ref, outb_ref, gain2_ref, bias2_ref,
-    tile_out, tile_inner, tile_taps, spread,
+    spread,
 ):
     share, width = q_ref.shape
     share_ffn, group = outer_ref.shape
@@ -360,25 +427,21 @@
     v_ref[...] = second_ref[share : 2 * share, :width]
     c_ref[...] = second_ref[share : 2 * share, width : 2 * width]
     p_ref[...] = second_ref[2 * share : 3 * share, :width]
-    out_ref[0] = turned(tile_out, first_ref[:share, :width])
-    out_ref[1] = turned(tile_out, first_ref[:share, width : 2 * width])
-    inner_ref[...] = turned(tile_inner, first_ref[share : share + share_ffn, :])
+    out_ref[0] = first_ref[:share, :width]
+    out_ref[1] = first_ref[:share, width : 2 * width]
+    inner_ref[...] = first_ref[share : share + share_ffn, :]
     outer_ref[...] = first_ref[share + share_ffn : share + 2 * share_ffn, :]
-    taps = kb_ref.shape[1]
-    rows = jnp.transpose(jnp.concatenate([table_ref[:64, :], jnp.zeros((64, WIDE), F32)], 0))
-    kw_ref[...] = rows[:width, :taps]
-    kb_ref[...] = rows[width : width + 1, :taps]
-    qb_ref[...] = table_ref[54:55, :width]
-    vb_ref[...] = table_ref[55:56, :width]
-    pb_ref[...] = table_ref[56:57, :width]
-    cb_ref[...] = table_ref[57:58, :width]
-    outb_ref[...] = wide_row(table_ref, 58, 2)[:, :group]
-    gain2_ref[...] = wide_row(table_ref, 60, 2)[:, :group]
-    bias2_ref[...] = wide_row(table_ref, 62, 2)[:, :group]
+    taps = kb_ref.shape[0]
+    kw_ref[...] = table_ref[:taps, :width]
+    rows = jnp.transpose(jnp.concatenate([table_ref[:64, LANES:], jnp.zeros((64, LANES), F32)], 0))
+    kb_ref[...] = rows[width - LANES : width - LANES + 1, :taps].reshape(taps)
+    for target, row in ((qb_ref, 54), (vb_ref, 55), (pb_ref, 56), (cb_ref, 57)):
+        target[...] = table_ref[row : row + 1, :width].reshape(width)
+    for target, row in ((outb_ref, 58), (gain2_ref, 60), (bias2_ref, 62)):
+        target[...] = wide_row(table_ref, row, 2)[:, :group].reshape(group)
     inb_ref[...] = wide_row(table_ref, 64, 6)
-    gain1_ref[...] = wide_row(table_ref, 99, 3)
-    bias1_ref[...] = wide_row(table_ref, 102, 3)
-    ob_ref[...] = wide_row(table_ref, 105, 3)
+    for target, row in ((gain1_ref, 99), (bias1_ref, 102), (ob_ref, 105)):
+        target[...] = wide_row(table_ref, row, 3).reshape(2 * group)
     spread[...] = jnp.zeros_like(spread)
     for k in range(3):
         spread[:KERNEL, k * WIDE : (k + 1) * WIDE] = table_ref[72 + KERNEL * k : 72 + KERNEL * (k + 1), :]
@@ -396,40 +459,25 @@
     return pl.pallas_call(
         functools.partial(final_kernel, count),
         out_shape=(
-            shape(share, width), shape(share, width), shape(share, width), shape(1, width), shape(1, width),
-            shape(KERNEL, share), shape(share, width), shape(1, width), shape(width, taps), shape(1, taps),
-            shape(share, width), shape(1, width), shape(2, width, share), shape(1, model), shape(1, model),
-            shape(1, model), shape(group, share_ffn), shape(1, 4 * group), shape(share_ffn, group), shape(1, group),
-            shape(1, group), shape(1, group),
+            shape(share, width), shape(share, width), shape(share, width), shape(width), shape(width),
+            shape(KERNEL, share), shape(share, width), shape(width), shape(taps, width), shape(taps),
+            shape(share, width), shape(width), shape(2, share, width), shape(model), shape(model),
+            shape(model), shape(share_ffn, group), shape(1, 4 * group), shape(share_ffn, group), shape(group),
+            shape(group), shape(group),
         ),
         in_specs=[whole()] * 3,
         out_specs=(whole(),) * 22,
         scratch_shapes=[
-            pltpu.VMEM((WIDE, WIDE), F32),
-            pltpu.VMEM((512, 512), F32),
-            pltpu.VMEM((LANES, WIDE), F32),
             pltpu.VMEM((TAP_ROWS, model), F32),
         ],
         name="final",
     )(first, second, table)
 
 
-HEAD_DIM = 64
-KERNEL = 9
-HALF = KERNEL // 2
 EPSILON = 1e-06
 MASK_FILL = -1e30
 INV_ROOT2 = 0.7071067811865476
 INV_ROOT_TWO_PI = 0.3989422804014327
-CUTS = 16
-TABLE_OWN = 72
-TABLE_ROWS = 112
-SWAP = [(0, 1), (1, 0)]
-
-
-class Group:
-    def __init__(self, **parts):
-        self.__dict__.update(parts)
 
 
 def nn(left, right):
@@ -442,55 +490,6 @@
 
 def nt(left, right):
     return lax.dot_general(left, right, (((1,), (1,)), ((), ())), preferred_element_type=F32)
-
-
-def swap(value):
-    return lax.ppermute(value, "mp", SWAP)
-
-
-def shifted(tensor, offset, half_width):
-    filler = jnp.zeros((half_width,) + tensor.shape[1:], tensor.dtype)
-    padded = jnp.concatenate([filler, tensor, filler], axis=0)
-    return padded[half_width + offset : half_width + offset + tensor.shape[0]]
-
-
-def same_segment(segment, offset, half_width):
-    filler = jnp.full((half_width,), -1, dtype=jnp.int32)
-    padded = jnp.concatenate([filler, segment, filler])
-    return padded[half_width + offset : half_width + offset + segment.shape[0]] == segment
-
-
-def segment_ids(lengths_row, seq_rows):
-    doc_ends = jnp.cumsum(lengths_row)
-    positions = jnp.arange(seq_rows, dtype=jnp.int32)
-    return jnp.sum((positions[:, None] >= doc_ends[None, :]).astype(jnp.int32), axis=1)
-
-
-def tap_mask_list(segment):
-    return [
-        same_segment(segment, tap - HALF, HALF).astype(F32)[:, None] for tap in range(KERNEL)
-    ]
-
-
-def gelu(tensor):
-    return 0.5 * tensor * (1.0 + lax.erf(tensor * INV_ROOT2))
-
-
-def gelu_slope(tensor):
-    normal_cdf = 0.5 * (1.0 + lax.erf(tensor * INV_ROOT2))
-    return normal_cdf + tensor * jnp.exp(-0.5 * tensor * tensor) * INV_ROOT_TWO_PI
-
-
-def halves(value, me):
-    width = value.shape[1] // 2
-    return (
-        lax.dynamic_slice_in_dim(value, me * width, width, 1),
-        lax.dynamic_slice_in_dim(value, (1 - me) * width, width, 1),
-    )
-
-
-def joined(own, other, me):
-    return jnp.where(me == 0, jnp.concatenate([own, other], 1), jnp.concatenate([other, own], 1))
 
 
 def moments(sum_own, square_own, sum_other, square_other, width):
@@ -500,10 +499,8 @@
     return mean, lax.rsqrt(spread + EPSILON)
 
 
-TAP_ROWS = 16
-WIDE = 256
-LANES = 128
-EDGE = 8
+def as_row(value):
+    return value.reshape(1, -1)
 
 
 def spread_marks(marks_ref, columns_ref):
@@ -513,6 +510,67 @@
     )
 
 
+def write_marks(lengths_ref, s, marks_ref):
+    rows = marks_ref.shape[2]
+    place = lax.broadcasted_iota(jnp.int32, (1, rows), 1)
+    segment = jnp.zeros((1, rows), jnp.int32)
+    end = 0
+    for document in range(lengths_ref.shape[1]):
+        end = end + lengths_ref[s, document]
+        segment = segment + (place >= end).astype(jnp.int32)
+    segment = segment.astype(F32)
+    for tap in range(KERNEL):
+        offset = tap - HALF
+        there = pltpu.roll(segment, -offset % rows, 1) if offset else segment
+        inside = jnp.logical_and(place + offset >= 0, place + offset < rows)
+        marks_ref[0, tap : tap + 1, :] = jnp.where(jnp.logical_and(there == segment, inside), 1.0, 0.0)
+    marks_ref[0, KERNEL : KERNEL + 1, :] = segment
+    marks_ref[0, KERNEL + 1 :, :] = jnp.zeros((TAP_ROWS - KERNEL - 1, rows), F32)
+
+
+def unpack_wide(target, source_ref, start, low, width):
+    cut = target.shape[0] // CUTS
+    for k in range(CUTS):
+        rows = source_ref[k, pl.ds(start, cut), :].astype(F32)[:, low : low + width]
+        rows = jnp.concatenate([rows, jnp.zeros((cut, WIDE - width), F32)], 1)
+        target[pl.ds(k * cut, cut), :] = rows.astype(target.dtype)
+
+
+def tap_places(heads, mp):
+    row = lax.broadcasted_iota(jnp.int32, (LANES, LANES), 0)
+    column = lax.broadcasted_iota(jnp.int32, (LANES, LANES), 1)
+    tap_rows = heads * TAP_ROWS
+    far = row >= tap_rows
+    inner = jnp.where(far, row - tap_rows, row)
+    head, tap = lax.shift_right_logical(inner, 4), jnp.bitwise_and(inner, TAP_ROWS - 1)
+    half = jnp.where(far, 1 - mp, mp)
+    valid = jnp.logical_and(tap < KERNEL, row < 2 * tap_rows)
+    return jnp.logical_and(valid, column == (half * heads + head) * KERNEL + tap)
+
+
+def write_expansion(target, heads):
+    row = lax.broadcasted_iota(jnp.int32, (LANES, WIDE), 0)
+    lane = lax.broadcasted_iota(jnp.int32, (LANES, WIDE), 1)
+    tap_rows = heads * TAP_ROWS
+    inner = jnp.where(row >= tap_rows, row - tap_rows, row)
+    inside = jnp.logical_and(lane < heads * HEAD_DIM, row < 2 * tap_rows)
+    head = lax.shift_right_logical(lane, 6) * TAP_ROWS
+    for tap in range(KERNEL):
+        chosen = jnp.logical_and(inside, inner == head + tap)
+        target[:, tap * WIDE : (tap + 1) * WIDE] = jnp.where(chosen, 1.0, 0.0).astype(BF16)
+
+
+def key_window(start, size, rows):
+    low = max(0, start - (MOST_DOC - 1)) // size * size
+    high = min(rows, -(-(start + size - 1 + MOST_DOC) // size) * size)
+    return slice(low, high)
+
+
+def only_rows(value, head):
+    row = lax.broadcasted_iota(jnp.int32, (WIDE, 1), 0)
+    return jnp.where(jnp.logical_and(row >= head * HEAD_DIM, row < (head + 1) * HEAD_DIM), value.astype(F32), 0.0)
+
+
 def head_lanes(head):
     lane = lax.broadcasted_iota(jnp.int32, (1, WIDE), 1)
     return jnp.logical_and(lane >= head * HEAD_DIM, lane < (head + 1) * HEAD_DIM)
@@ -530,11 +588,13 @@
 
 
 def front_kernel(
-    seqs, count,
-    hidden_ref, marks_ref, query_ref, key_ref, value_ref, conv_ref, point_ref, taps_ref, vec_ref, depth_ref, bias_ref,
-    expand_ref, second_ref,
+    seqs, count, early,
+    hidden_ref, lengths_ref, first_ref, kw_ref, kb_ref, qb_ref, vb_ref, pb_ref, cb_ref, second_ref,
     q_ref, k_ref, v_ref, cv_ref, dl_ref, kc_ref, ca_ref, probs_ref, cc_ref, ctx_ref, lse_ref, second_all_ref,
-    rows_pad, conv_pad, columns, weights, tops, tap_out, tap_in,
+    marks_ref, taps_ref, depth_ref, expand_ref, inputs_turned_ref, point_turned_ref, early_ref,
+    lead_ref, out0_nat, out1_nat, part_out, part_send, part_recv,
+    query_ref, key_ref, value_ref, conv_ref, point_ref, vec_ref, bias_ref, depth_wide, tile,
+    rows_pad, conv_pad, columns, weights, query_turned, value_turned, context_turned, tap_out, tap_in,
     send_sem, recv_sem, own_sem, gather_send, gather_recv,
 ):
     s = pl.program_id(0)
@@ -547,31 +607,66 @@
     beside = index_of(deep, 1 - side, core)
     twin = index_of(deep, side, 1 - core)
 
-    def push(source, block, target, slot):
+    split = lead_ref.shape[1]
+    spans = [pl.ds(0, split), pl.ds(split, second_ref.shape[1] - split)]
+
+    def push(group, source, block, target, slot):
         return pltpu.make_async_remote_copy(
-            src_ref=source,
-            dst_ref=second_all_ref.at[block],
-            send_sem=gather_send.at[slot],
-            recv_sem=gather_recv.at[block],
+            src_ref=source.at[spans[group]],
+            dst_ref=second_all_ref.at[block, spans[group]],
+            send_sem=gather_send.at[group, slot],
+            recv_sem=gather_recv.at[group, block],
             device_id=at(target, mp),
             device_id_type=MESH,
         )
 
-    def arrive(block):
-        pltpu.make_async_copy(second_ref.at[0], second_all_ref.at[block], gather_recv.at[block]).wait()
-
-    own_copy = pltpu.make_async_copy(second_ref.at[0], second_all_ref.at[me], own_sem)
-    first_hops = [
-        push(second_ref.at[0], me, index_of(lax.rem(deep + k, parts), side, core), k - 1) for k in range(1, parts)
-    ]
-    first_hops += [push(second_ref.at[0], me, beside, parts - 1), push(second_ref.at[0], me, twin, parts)]
-    second_hops = [(beside, twin, parts + 1)]
+    def arrive(group, block):
+        pltpu.make_async_copy(
+            second_ref.at[0, spans[group]], second_all_ref.at[block, spans[group]], gather_recv.at[group, block]
+        ).wait()
+
+    own_copy = pltpu.make_async_copy(second_ref.at[0], second_all_ref.at[me], own_sem.at[0])
+    lead_copy = pltpu.make_async_copy(second_all_ref.at[:, spans[0]], lead_ref, own_sem.at[1])
+    first_hops = [(me, index_of(lax.rem(deep + k, parts), side, core), k - 1) for k in range(1, parts)]
+    first_hops += [(me, beside, parts - 1), (me, twin, parts)]
+    second_hops = [(beside, [(twin, parts + 1)])]
     for k in range(1, parts):
         block = index_of(lax.rem(deep + parts - k, parts), side, core)
-        second_hops += [(block, beside, parts + 2 * k), (block, twin, parts + 2 * k + 1)]
+        second_hops.append((block, [(beside, parts + 2 * k), (twin, parts + 2 * k + 1)]))
     third_hops = [
-        (index_of(lax.rem(deep + parts - k, parts), 1 - side, core), twin, 3 * parts + k - 1) for k in range(1, parts)
+        (index_of(lax.rem(deep + parts - k, parts), 1 - side, core), [(twin, 3 * parts + k - 1)]) for k in range(1, parts)
     ]
+
+    def start_hops(group):
+        for block, target, place in first_hops:
+            push(group, second_ref.at[0], block, target, place).start()
+
+    def pass_on(group, hops):
+        for block, targets in hops:
+            arrive(group, block)
+            for target, place in targets:
+                push(group, second_all_ref.at[block], block, target, place).start()
+
+    def end_hops(group):
+        for k in range(parts):
+            for other in range(2):
+                arrive(group, index_of(lax.rem(deep + parts - k, parts), other, 1 - core))
+        for block, target, place in first_hops:
+            push(group, second_ref.at[0], block, target, place).wait_send()
+        for block, targets in second_hops + third_hops:
+            for target, place in targets:
+                push(group, second_all_ref.at[block], block, target, place).wait_send()
+
+    def swap_part(which, piece):
+        size = rows // PIECES
+        return pltpu.make_async_remote_copy(
+            src_ref=part_out.at[which, pl.ds(piece * size, size)],
+            dst_ref=early_ref.at[pl.ds(which * rows + piece * size, size)],
+            send_sem=part_send.at[which, piece],
+            recv_sem=part_recv.at[which, piece],
+            device_id=at(me, 1 - mp),
+            device_id_type=MESH,
+        )
 
     @pl.when(s == 0)
     def _():
@@ -582,13 +677,37 @@
             pl.semaphore_signal(barrier, inc=1, device_id=at(peer, mp), device_id_type=MESH)
         pl.semaphore_wait(barrier, len(peers) + 1)
         own_copy.start()
-        for copy in first_hops:
-            copy.start()
+        start_hops(0)
+        start_hops(1)
+        width = heads * HEAD_DIM
+        cut = model // CUTS
+        for target, place, low in (
+            (query_ref, 0, 0), (key_ref, 0, width), (value_ref, 1, 0), (conv_ref, 1, width), (point_ref, 2, 0),
+            (depth_wide, 2, width),
+        ):
+            unpack_wide(target, first_ref, place * cut, low, width)
+        depth_ref[...] = jnp.transpose(depth_wide[:, :LANES])[:TAP_ROWS]
+        vec_ref[...] = jnp.zeros_like(vec_ref)
+        for row, source in enumerate((qb_ref, vb_ref, pb_ref, cb_ref)):
+            vec_ref[row : row + 1, :width] = as_row(source[...])
+        write_expansion(expand_ref, heads)
+        chosen = tap_places(heads, mp)
+        tile[...] = jnp.zeros_like(tile)
+        tile[:1, : kb_ref.shape[0]] = as_row(kb_ref[...])
+        bias = jnp.sum(jnp.where(chosen, tile[:1, :LANES], 0.0), axis=1, keepdims=True)
+        bias_ref[...] = jnp.broadcast_to(bias[:tap_rows], bias_ref.shape)
+        tile[: kw_ref.shape[0], :width] = kw_ref[...].astype(F32)
+        turned_weight = tile[:LANES, :].astype(BF16)
+        taps_ref[...] = nn(jnp.where(chosen, 1.0, 0.0).astype(BF16), turned_weight).astype(BF16)
+        for place, source in enumerate((query_ref, key_ref, value_ref, conv_ref)):
+            inputs_turned_ref[place * WIDE : (place + 1) * WIDE, :] = jnp.transpose(source[...])
+        point_turned_ref[...] = jnp.transpose(point_ref[...])
         rows_pad[:, :EDGE, :] = jnp.zeros((chunks, EDGE, LANES), F32)
         rows_pad[:, pl.ds(EDGE + rows, EDGE), :] = jnp.zeros((chunks, EDGE, LANES), F32)
         conv_pad[:, :EDGE, :] = jnp.zeros((2, EDGE, LANES), F32)
         conv_pad[:, pl.ds(EDGE + rows, EDGE), :] = jnp.zeros((2, EDGE, LANES), F32)
 
+    write_marks(lengths_ref, s, marks_ref)
     spread_marks(marks_ref, columns)
     hidden = hidden_ref[...]
     for c in range(chunks):
@@ -609,6 +728,11 @@
         return carry
 
     lax.fori_loop(0, rows // step, depth_step, 0)
+
+    @pl.when(s == 0)
+    def _():
+        pass_on(0, second_hops)
+
     queries = (nn(hidden, query_ref[...]) + vec_ref[0:1, :]).astype(BF16)
     q_ref[...] = queries
     key_conv = nn(dl_ref[...], point_ref[...]) + vec_ref[2:3, :]
@@ -627,6 +751,12 @@
         device_id_type=MESH,
     )
     swap_taps.start()
+
+    @pl.when(jnp.logical_and(s >= 1, s < early + 1))
+    def _():
+        for piece in range(PIECES // 2, PIECES):
+            swap_part(s - 1, piece).start()
+
     own_terms = tap_terms[:tap_rows]
     k_ref[...] = nn(hidden, key_ref[...]).astype(BF16)
     v_ref[...] = (nn(hidden, value_ref[...]) + vec_ref[1:2, :]).astype(BF16)
@@ -636,30 +766,29 @@
         conv_pad[c, pl.ds(EDGE, rows), :] = conv_values[:, c * LANES : (c + 1) * LANES]
 
     block = 256
-    seg_row = marks_ref[0, KERNEL : KERNEL + 1, :]
-    lane = lax.broadcasted_iota(jnp.int32, (block, LANES), 1)
-
-    def attention_step(i, carry):
-        part = pl.ds(pl.multiple_of(i * block, block), block)
-        allowed = columns[part, KERNEL : KERNEL + 1] == seg_row
-        query = q_ref[part, :]
-        total = jnp.zeros((block, WIDE), F32)
-        packed = jnp.zeros((block, LANES), F32)
+    query_turned[...] = jnp.transpose(q_ref[...])
+    value_turned[...] = jnp.transpose(v_ref[...])
+    for start in range(0, rows, block):
+        part = slice(start, start + block)
+        keys = key_window(start, block, rows)
+        allowed = columns[keys, KERNEL : KERNEL + 1] == marks_ref[0, KERNEL : KERNEL + 1, part]
         for head in range(heads):
-            mine = (only(query, head) * (HEAD_DIM**-0.5)).astype(BF16)
-            scores = jnp.where(allowed, nt(mine, k_ref[...]), MASK_FILL)
-            top = jnp.max(scores, axis=1, keepdims=True)
+            lanes = slice(head * HEAD_DIM, (head + 1) * HEAD_DIM)
+            mine = (only_rows(query_turned[:, part], head) * (HEAD_DIM**-0.5)).astype(BF16)
+            scores = jnp.where(allowed, nn(k_ref[keys, :], mine), MASK_FILL)
+            top = jnp.max(scores, axis=0, keepdims=True)
             exponent = jnp.exp(scores - top)
-            amount = jnp.sum(exponent, axis=1, keepdims=True)
-            probs = (exponent * (1.0 / amount)).astype(BF16)
-            total = total + nn(probs, only(v_ref[...], head).astype(BF16))
-            packed = jnp.where(lane == head, top + jnp.log(amount), packed)
-        ctx_ref[part, :] = total.astype(BF16)
-        tops[part, :] = packed
-        return carry
-
-    lax.fori_loop(0, rows // block, attention_step, 0)
-    lse_ref[0] = jnp.transpose(tops[...])[:8]
+            amount = jnp.sum(exponent, axis=0, keepdims=True)
+            context_turned[lanes, part] = nn(value_turned[lanes, keys], exponent.astype(BF16)) * (1.0 / amount)
+            lse_ref[0, head : head + 1, part] = top + jnp.log(amount)
+    lse_ref[0, heads:, :] = jnp.zeros((8 - heads, rows), F32)
+    context_turned[heads * HEAD_DIM :, :] = jnp.zeros((WIDE - heads * HEAD_DIM, rows), F32)
+    ctx_ref[...] = jnp.transpose(context_turned[...]).astype(BF16)
+
+    @pl.when(s == 0)
+    def _():
+        pass_on(0, third_hops)
+
 
     swap_taps.wait()
     logits = (own_terms + tap_in[slot] + bias_ref[:, :1]).reshape(heads, TAP_ROWS, rows)
@@ -689,29 +818,42 @@
 
     @pl.when(s == 0)
     def _():
-        for block, target, place in second_hops:
-            if target is twin and place == parts + 1:
-                arrive(block)
-            elif target is beside:
-                arrive(block)
-            push(second_all_ref.at[block], block, target, place).start()
+        own_copy.wait()
+        end_hops(0)
+        pass_on(1, second_hops)
+        if early:
+            lead_copy.start()
+            lead_copy.wait()
+            width = heads * HEAD_DIM
+            for target, low in ((out0_nat, 0), (out1_nat, width)):
+                unpack_wide(depth_wide, lead_ref, 0, low, width)
+                target[...] = jnp.transpose(depth_wide[...].astype(BF16))
+
+    @pl.when(s < early)
+    def _():
+        half = model // 2
+        theirs = pl.ds(pl.multiple_of((1 - mp) * half, half), half)
+
+        def part_step(i, carry):
+            part = pl.ds(pl.multiple_of(i * block, block), block)
+            other = nn(ctx_ref[part, :], out0_nat[:, theirs]) + nn(cc_ref[part, :], out1_nat[:, theirs])
+            part_out[s, part, :] = other.astype(BF16)
+            return carry
+
+        lax.fori_loop(0, rows // block, part_step, 0)
+        for piece in range(PIECES // 2):
+            swap_part(s, piece).start()
 
     @pl.when(s == min(1, seqs - 1))
     def _():
-        for block, target, place in third_hops:
-            arrive(block)
-            push(second_all_ref.at[block], block, target, place).start()
+        pass_on(1, third_hops)
 
     @pl.when(s == seqs - 1)
     def _():
-        for k in range(parts):
-            for other in range(2):
-                arrive(index_of(lax.rem(deep + parts - k, parts), other, 1 - core))
-        for copy in first_hops:
-            copy.wait_send()
-        for block, target, place in second_hops + third_hops:
-            push(second_all_ref.at[block], block, target, place).wait_send()
-        own_copy.wait()
+        end_hops(1)
+        for which in range(early):
+            for piece in range(PIECES):
+                swap_part(which, piece).wait()
 
 
 def whole():
@@ -726,17 +868,21 @@
     return pl.BlockSpec((1, rows, columns), lambda s: (s, 0, 0))
 
 
-def front(hidden, marks, w, vectors, depth, bias, expand, taps, second, count, ident):
-    seqs, _, rows = marks.shape
+def front(hidden, lengths, first, kernel_weight, biases, second, count, early, ident):
+    seqs = lengths.shape[0]
     tokens, model = hidden.shape
-    tap_rows = bias.shape[0]
+    rows = tokens // seqs
+    tap_rows = kernel_weight.shape[1] // HEAD_DIM * TAP_ROWS
     parts = count // 4
+    place = pl.BlockSpec(memory_space=pl.ANY)
+    share = model // count
+    split = share + -share % TAP_ROWS
 
     def wide(kind):
         return jax.ShapeDtypeStruct((tokens, WIDE), kind)
 
     return pl.pallas_call(
-        functools.partial(front_kernel, seqs, count),
+        functools.partial(front_kernel, seqs, count, early),
         grid=(seqs,),
         out_shape=(
             wide(BF16), wide(BF16), wide(BF16), wide(F32),
@@ -746,50 +892,70 @@
             wide(BF16), wide(BF16),
             jax.ShapeDtypeStruct((seqs, 8, rows), F32),
             jax.ShapeDtypeStruct((count,) + second.shape[1:], BF16),
+            jax.ShapeDtypeStruct((seqs, TAP_ROWS, rows), F32),
+            jax.ShapeDtypeStruct((LANES, WIDE), BF16),
+            jax.ShapeDtypeStruct((TAP_ROWS, model), F32),
+            jax.ShapeDtypeStruct((LANES, KERNEL * WIDE), BF16),
+            jax.ShapeDtypeStruct((4 * WIDE, model), BF16),
+            jax.ShapeDtypeStruct((WIDE, model), BF16),
+            jax.ShapeDtypeStruct((tokens, model // 2), BF16),
         ),
-        in_specs=[by_seq(rows, model), by_seq_row(TAP_ROWS, rows)] + [whole()] * 10 + [pl.BlockSpec(memory_space=pl.ANY)],
+        in_specs=[by_seq(rows, model), pl.BlockSpec(memory_space=pltpu.SMEM)] + [whole()] * 7 + [place],
         out_specs=(
             by_seq(rows, WIDE), by_seq(rows, WIDE), by_seq(rows, WIDE), by_seq(rows, WIDE), by_seq(rows, model),
             by_seq(rows, WIDE), by_seq(rows, WIDE), by_seq_row(tap_rows, rows), by_seq(rows, WIDE), by_seq(rows, WIDE),
-            by_seq_row(8, rows), pl.BlockSpec(memory_space=pl.ANY),
-        ),
+            by_seq_row(8, rows), place, by_seq_row(TAP_ROWS, rows),
+        )
+        + (whole(),) * 5
+        + (place,),
         scratch_shapes=[
+            pltpu.VMEM((count, split, second.shape[2]), BF16),
+            pltpu.VMEM((WIDE, model), BF16),
+            pltpu.VMEM((WIDE, model), BF16),
+            pltpu.VMEM((max(early, 1), rows, model // 2), BF16),
+            pltpu.SemaphoreType.DMA((max(early, 1), PIECES)),
+            pltpu.SemaphoreType.DMA((max(early, 1), PIECES)),
+        ]
+        + [pltpu.VMEM((model, WIDE), BF16)] * 5
+        + [
+            pltpu.VMEM((8, WIDE), F32),
+            pltpu.VMEM((tap_rows, LANES), F32),
+            pltpu.VMEM((model, WIDE), F32),
+            pltpu.VMEM((WIDE, WIDE), F32),
             pltpu.VMEM((model // LANES, rows + 2 * EDGE, LANES), F32),
             pltpu.VMEM((2, rows + 2 * EDGE, LANES), F32),
             pltpu.VMEM((rows, LANES), F32),
             pltpu.VMEM((rows, LANES), BF16),
-            pltpu.VMEM((rows, LANES), F32),
+            pltpu.VMEM((WIDE, rows), BF16),
+            pltpu.VMEM((WIDE, rows), BF16),
+            pltpu.VMEM((WIDE, rows), F32),
             pltpu.VMEM((2, tap_rows, rows), F32),
             pltpu.VMEM((2, tap_rows, rows), F32),
             pltpu.SemaphoreType.DMA((2,)),
             pltpu.SemaphoreType.DMA((2,)),
-            pltpu.SemaphoreType.DMA,
-            pltpu.SemaphoreType.DMA((4 * parts - 1,)),
-            pltpu.SemaphoreType.DMA((count,)),
+            pltpu.SemaphoreType.DMA((2,)),
+            pltpu.SemaphoreType.DMA((2, 4 * parts - 1)),
+            pltpu.SemaphoreType.DMA((2, count)),
         ],
         compiler_params=pltpu.CompilerParams(
-            collective_id=ident, has_side_effects=True, vmem_limit_bytes=60 << 20
+            collective_id=ident, has_side_effects=True, vmem_limit_bytes=62 << 20
         ),
         name="front",
-    )(
-        hidden, marks, w.query, w.key, w.value, w.conv, w.point, taps, vectors, depth, bias, expand, second,
-    )
-
-
-def transposed_stats(columns):
+    )(hidden, lengths, first, kernel_weight, *biases, second)
+
+
+def stat_rows(columns):
     rows = columns[0].shape[0]
-    lane = lax.broadcasted_iota(jnp.int32, (rows, 128), 1)
-    packed = jnp.zeros((rows, 128), F32)
-    for place, column in enumerate(columns):
-        packed = jnp.where(lane == place, column, packed)
-    return jnp.transpose(packed)[:8]
-
-
-def stat_columns(message, amount):
-    rows = message.shape[1]
-    wide = jnp.concatenate([message, jnp.zeros((120, rows), F32)], 0)
+    diagonal = lax.broadcasted_iota(jnp.int32, (rows, rows), 0) == lax.broadcasted_iota(jnp.int32, (rows, rows), 1)
+    lines = [jnp.sum(jnp.where(diagonal, column, 0.0), axis=0, keepdims=True) for column in columns]
+    return jnp.concatenate(lines + [jnp.zeros((8 - len(lines), rows), F32)], 0)
+
+
+def stat_columns(lines):
+    rows = lines[0].shape[1]
+    wide = jnp.concatenate(lines + [jnp.zeros((LANES - len(lines), rows), F32)], 0)
     tall = jnp.transpose(wide)
-    return [tall[:, k : k + 1] for k in range(amount)]
+    return [tall[:, k : k + 1] for k in range(len(lines))]
 
 
 def row_sums(value):
@@ -802,10 +968,11 @@
 
 
 def middle_kernel(
-    blocks,
-    context_ref, conv_ref, context_late_ref, conv_late_ref, hidden_ref, grad_ref, grad_late_ref, out0_ref, out1_ref, inner_ref, outer_ref, vec_ref,
+    blocks, early,
+    early_ref, context_ref, conv_ref, context_late_ref, conv_late_ref, hidden_ref, grad_ref, grad_late_ref, second_ref,
+    ob_ref, gain1_ref, bias1_ref, outb_ref, gain2_ref, bias2_ref, inb_ref,
     output_ref, residual_ref, grad_context_ref, grad_conv_ref, pack_ref, small_ref,
-    branch_ref, acc_out0, acc_out1, state, scale_ring, act_ring, slope_ring, low_ring, summed_ring, normed_ring, stat_ring,
+    out0_ref, out1_ref, inner_ref, outer_ref, vec_ref, inner_nat, outer_turned, out0_nat, out1_nat, low_units, branch_ref, acc_out0, acc_out1, state, scale_ring, act_ring, slope_ring, low_ring, summed_ring, normed_ring, stat_ring,
     acc_inner, acc_outer, acc_small, acc_bias,
     branch_out, branch_in, stat1_out, stat1_in, stat2_out, stat2_in, stat3_out, stat3_in, back_out, back_in,
     send_sem, recv_sem,
@@ -844,6 +1011,22 @@
         barrier = pltpu.get_barrier_semaphore()
         pl.semaphore_signal(barrier, inc=1, device_id=(dp, 1 - me), device_id_type=MESH)
         pl.semaphore_wait(barrier, 1)
+        cut, cut_ffn = 2 * width // CUTS, hidden_units // CUTS
+        unpack_wide(out0_ref, second_ref, 0, 0, width // 2)
+        unpack_wide(out1_ref, second_ref, 0, width // 2, width // 2)
+        for k in range(CUTS):
+            inner_ref[pl.ds(k * cut_ffn, cut_ffn), :] = second_ref[k, pl.ds(cut, cut_ffn), :]
+            outer_ref[pl.ds(k * cut_ffn, cut_ffn), :] = second_ref[k, pl.ds(cut + cut_ffn, cut_ffn), :]
+        for row, source in enumerate((ob_ref, gain1_ref, bias1_ref)):
+            value = as_row(source[...])
+            vec_ref[row : row + 1, :width] = jnp.where(me == 0, value[:, :width], value[:, width:])
+        for row, source in enumerate((outb_ref, gain2_ref, bias2_ref)):
+            vec_ref[3 + row : 4 + row, :width] = as_row(source[...])
+        vec_ref[7:8, :] = inb_ref[...]
+        inner_nat[...] = jnp.transpose(inner_ref[...])
+        outer_turned[...] = jnp.transpose(outer_ref[...])
+        out0_nat[...] = jnp.transpose(out0_ref[...])
+        out1_nat[...] = jnp.transpose(out1_ref[...])
         acc_inner[...] = jnp.zeros_like(acc_inner)
         acc_outer[...] = jnp.zeros_like(acc_outer)
         acc_out0[...] = jnp.zeros_like(acc_out0)
@@ -855,26 +1038,38 @@
     def _():
         b = i
         slot = lax.rem(b, SLOTS)
-        fresh(0, b, slot)
         theirs = pl.ds(pl.multiple_of((1 - me) * width, width), width)
         ours = pl.ds(pl.multiple_of(me * width, width), width)
-        other = nt(context_ref[...], out0_ref[theirs, :]) + nt(conv_ref[...], out1_ref[theirs, :])
-        branch_out[slot] = other.astype(BF16)
-        message(0, *kinds[0], slot).start()
-        own = nt(context_ref[...], out0_ref[ours, :]) + nt(conv_ref[...], out1_ref[ours, :])
+
+        @pl.when(b >= early)
+        def _():
+            fresh(0, b - early, slot)
+            other = nn(context_ref[...], out0_nat[:, theirs]) + nn(conv_ref[...], out1_nat[:, theirs])
+            branch_out[slot] = other.astype(BF16)
+            message(0, *kinds[0], slot).start()
+
+        own = nn(context_ref[...], out0_nat[:, ours]) + nn(conv_ref[...], out1_nat[:, ours])
         state[lax.rem(b, 8)] = hidden_ref[:, ours].astype(F32) + (own + vec(0))
+
+        @pl.when(b < early)
+        def _():
+            state[lax.rem(b, 8)] += early_ref[...].astype(F32)
 
     @pl.when(jnp.logical_and(i >= 1, i < blocks + 1))
     def _():
         b = i - 1
         slot = lax.rem(b, SLOTS)
-        message(0, *kinds[0], slot).wait_recv()
         fresh(1, b, slot)
-        residual = state[lax.rem(b, 8)] + branch_in[slot].astype(F32)
-        state[lax.rem(b, 8)] = residual
+
+        @pl.when(b >= early)
+        def _():
+            message(0, *kinds[0], slot).wait_recv()
+            state[lax.rem(b, 8)] += branch_in[slot].astype(F32)
+
+        residual = state[lax.rem(b, 8)]
         total = jnp.sum(residual, axis=1, keepdims=True)
         apart = residual - total * (1.0 / width)
-        stat1_out[slot] = transposed_stats([total, jnp.sum(apart * apart, axis=1, keepdims=True)])
+        stat1_out[slot] = stat_rows([total, jnp.sum(apart * apart, axis=1, keepdims=True)])
         message(1, *kinds[1], slot).start()
 
     @pl.when(jnp.logical_and(i >= 2, i < blocks + 2))
@@ -884,9 +1079,9 @@
         two = lax.rem(b, 2)
         message(1, *kinds[1], slot).wait_recv()
         fresh(2, b, slot)
-        total, square = stat_columns(stat1_out[slot], 2)
-        total_o, square_o = stat_columns(stat1_in[slot], 2)
-        mean, scale = moments(total, square, total_o, square_o, width)
+        ours, theirs = stat1_out[slot], stat1_in[slot]
+        mean, scale = moments(ours[0:1], ours[1:2], theirs[0:1], theirs[1:2], width)
+        mean, scale = stat_columns([mean, scale])
         standard = (state[lax.rem(b, 8)] - mean) * scale
         state[lax.rem(b, 8)] = standard
         scale_ring[lax.rem(b, 4)] = jnp.broadcast_to(scale, scale_ring.shape[1:])
@@ -896,17 +1091,17 @@
         summed = normed + vec(3)
         for start in range(0, hidden_units, FFN_STEP):
             part = pl.ds(start, FFN_STEP)
-            inner = nt(low, inner_ref[part, :]) + vec_ref[7:8, start : start + FFN_STEP]
+            inner = nn(low, inner_nat[:, part]) + vec_ref[7:8, start : start + FFN_STEP]
             cdf = 0.5 * (1.0 + lax.erf(inner * INV_ROOT2))
             act = (inner * cdf).astype(BF16)
             act_ring[two, :, part] = act
             slope_ring[two, :, part] = cdf + inner * jnp.exp(-0.5 * inner * inner) * INV_ROOT_TWO_PI
-            summed = summed + nn(act, outer_ref[part, :])
+        summed = summed + nn(act_ring[two], outer_ref[...])
         summed_ring[two] = summed
         scaled = grad_ref[...].astype(F32) * vec(4)
         total = jnp.sum(summed, axis=1, keepdims=True)
         apart = summed - total * (1.0 / width)
-        stat2_out[slot] = transposed_stats(
+        stat2_out[slot] = stat_rows(
             [
                 total,
                 jnp.sum(apart * apart, axis=1, keepdims=True),
@@ -923,12 +1118,13 @@
         two = lax.rem(b, 2)
         message(2, *kinds[2], slot).wait_recv()
         fresh(3, b, slot)
-        total, square, grads, cross = stat_columns(stat2_out[slot], 4)
-        total_o, square_o, grads_o, cross_o = stat_columns(stat2_in[slot], 4)
+        total, square, grads, cross = [stat2_out[slot][k : k + 1] for k in range(4)]
+        total_o, square_o, grads_o, cross_o = [stat2_in[slot][k : k + 1] for k in range(4)]
         mean, scale = moments(total, square, total_o, square_o, width)
         mean_grad = (grads + grads_o) * inverse
         product = cross + cross_o + (total * (1.0 / width) - mean) * grads + (total_o * (1.0 / width) - mean) * grads_o
         mean_product = product * scale * inverse
+        mean, scale, mean_grad, mean_product = stat_columns([mean, scale, mean_grad, mean_product])
         standard = (summed_ring[two] - mean) * scale
         output_ref[...] = (standard * vec(4) + vec(5)).astype(BF16)
         gradient = grad_late_ref[...].astype(F32)
@@ -941,18 +1137,18 @@
         grad_normed = grad_summed
         for start in range(0, hidden_units, FFN_STEP):
             part = pl.ds(start, FFN_STEP)
-            grad_inner = nt(low, outer_ref[part, :]) * slope_ring[two, :, part]
-            inner_low = grad_inner.astype(BF16)
+            inner_low = (nn(low, outer_turned[:, part]) * slope_ring[two, :, part]).astype(BF16)
+            low_units[:, part] = inner_low
             acc_bias[:, part] += row_sums(inner_low.astype(F32))
-            grad_normed = grad_normed + nn(inner_low, inner_ref[part, :])
-            acc_outer[part, :] += tn(act_ring[two, :, part], low)
-            acc_inner[part, :] += tn(inner_low, normed_low)
+            acc_outer[:, part] += tn(low, act_ring[two, :, part])
+            acc_inner[:, part] += tn(normed_low, inner_low)
+        grad_normed = grad_normed + nn(low_units[...], inner_ref[...])
         normed_ring[two] = grad_normed
         standard1 = state[lax.rem(b, 8)]
         scaled = grad_normed * vec(1)
         acc_small[3] += row_sums(grad_normed * standard1)
         acc_small[4] += row_sums(grad_normed)
-        sums = transposed_stats(
+        sums = stat_rows(
             [jnp.sum(scaled, axis=1, keepdims=True), jnp.sum(scaled * standard1, axis=1, keepdims=True)]
         )
         stat3_out[slot] = sums
@@ -964,7 +1160,8 @@
         slot = lax.rem(b, SLOTS)
         message(3, *kinds[3], slot).wait_recv()
         fresh(4, b, slot)
-        first, second = stat_columns(stat3_out[slot] + stat3_in[slot], 2)
+        both = stat3_out[slot] + stat3_in[slot]
+        first, second = stat_columns([both[0:1], both[1:2]])
         standard = state[lax.rem(b, 8)]
         scaled = normed_ring[lax.rem(b, 2)] * vec(1)
         residual = scale_ring[lax.rem(b, 4)][:, :1] * (scaled - first * inverse - standard * (second * inverse))
@@ -986,8 +1183,8 @@
         branch = branch_ref[...]
         grad_context_ref[...] = nn(branch, out0_ref[...]).astype(BF16)
         grad_conv_ref[...] = nn(branch, out1_ref[...]).astype(BF16)
-        acc_out0[...] += tn(branch, context_late_ref[...])
-        acc_out1[...] += tn(branch, conv_late_ref[...])
+        acc_out0[...] += tn(context_late_ref[...], branch)
+        acc_out1[...] += tn(conv_late_ref[...], branch)
 
     @pl.when(i == blocks + 4)
     def _():
@@ -995,33 +1192,27 @@
             for slot in range(SLOTS):
                 message(kind, *kinds[kind], slot).wait_send()
         cut, cut_ffn = 2 * width // CUTS, hidden_units // CUTS
+        out_grads = jnp.transpose(jnp.concatenate([acc_out0[: width // 2], acc_out1[: width // 2]], 0)).astype(BF16)
+        inner_grads = jnp.transpose(acc_inner[...]).astype(BF16)
+        outer_grads = jnp.transpose(acc_outer[...]).astype(BF16)
         for k in range(CUTS):
-            part, part_ffn = pl.ds(k * cut, cut), pl.ds(k * cut_ffn, cut_ffn)
-            both = jnp.concatenate([acc_out0[part, : width // 2], acc_out1[part, : width // 2]], 1)
-            pack_ref[k, pl.ds(0, cut), :] = both.astype(BF16)
-            pack_ref[k, pl.ds(cut, cut_ffn), :] = acc_inner[part_ffn, :].astype(BF16)
-            pack_ref[k, pl.ds(cut + cut_ffn, cut_ffn), :] = acc_outer[part_ffn, :].astype(BF16)
+            part_ffn = slice(k * cut_ffn, (k + 1) * cut_ffn)
+            pack_ref[k, pl.ds(0, cut), :] = out_grads[k * cut : (k + 1) * cut]
+            pack_ref[k, pl.ds(cut, cut_ffn), :] = inner_grads[part_ffn]
+            pack_ref[k, pl.ds(cut + cut_ffn, cut_ffn), :] = outer_grads[part_ffn]
         small_ref[...] = jnp.zeros_like(small_ref)
         for row in range(6):
             small_ref[row : row + 1, :width] = jnp.sum(acc_small[row], axis=0, keepdims=True)
         small_ref[6:7, :] = jnp.sum(acc_bias[...], axis=0, keepdims=True)
 
 
-def middle(context, conv_context, hidden, out_grad, w, p, me, ident):
+def middle(early, early_rows, context, conv_context, hidden, out_grad, second, vectors, ident):
     tokens, model = hidden.shape
     width = model // 2
     local = context.shape[1]
-    units = w.inner.shape[0]
+    units = vectors[-1].shape[1]
     rows = 256
     blocks = tokens // rows
-
-    def mine(value):
-        return lax.dynamic_slice_in_dim(value, me * width, width, 0)
-
-    vectors = [
-        mine(p.out_bias), mine(p.norm1_gain), mine(p.norm1_bias), p.ffn_out_bias, p.norm2_gain, p.norm2_bias,
-    ]
-    table = jnp.stack([jnp.pad(v, (0, units - width)) for v in vectors] + [jnp.zeros((units,), F32), p.ffn_in_bias])
 
     def block(columns, lag):
         return pl.BlockSpec((rows, columns), lambda i: (jnp.clip(i - lag, 0, blocks - 1), 0))
@@ -1030,7 +1221,7 @@
     stat = pltpu.VMEM((SLOTS, 8, rows), F32)
     half = pltpu.VMEM((SLOTS, rows, width), BF16)
     return pl.pallas_call(
-        functools.partial(middle_kernel, blocks),
+        functools.partial(middle_kernel, blocks, early // rows),
         grid=(blocks + 5,),
         out_shape=(
             jax.ShapeDtypeStruct((tokens, width), BF16),
@@ -1041,15 +1232,25 @@
             jax.ShapeDtypeStruct((8, units), F32),
         ),
         in_specs=[
-            block(local, 0), block(local, 0), block(local, 5), block(local, 5), block(model, 0), block(width, 2),
+            block(width, 0), block(local, 0), block(local, 0), block(local, 5), block(local, 5), block(model, 0), block(width, 2),
             block(width, 3),
-            whole, whole, whole, whole, whole,
-        ],
+        ]
+        + [whole] * 8,
         out_specs=(block(width, 3), block(width, 4), block(local, 5), block(local, 5), whole, whole),
         scratch_shapes=[
+            pltpu.VMEM((model, local), BF16),
+            pltpu.VMEM((model, local), BF16),
+            pltpu.VMEM((units, width), BF16),
+            pltpu.VMEM((units, width), BF16),
+            pltpu.VMEM((8, units), F32),
+            pltpu.VMEM((width, units), BF16),
+            pltpu.VMEM((width, units), BF16),
+            pltpu.VMEM((local, model), BF16),
+            pltpu.VMEM((local, model), BF16),
+            pltpu.VMEM((rows, units), BF16),
             pltpu.VMEM((rows, model), BF16),
-            pltpu.VMEM((model, local), F32),
-            pltpu.VMEM((model, local), F32),
+            pltpu.VMEM((local, model), F32),
+            pltpu.VMEM((local, model), F32),
             pltpu.VMEM((8, rows, width), F32),
             pltpu.VMEM((4, rows, 128), F32),
             pltpu.VMEM((2, rows, units), BF16),
@@ -1058,8 +1259,8 @@
             pltpu.VMEM((2, rows, width), F32),
             pltpu.VMEM((2, rows, width), F32),
             pltpu.VMEM((8, 128), F32),
-            pltpu.VMEM((units, width), F32),
-            pltpu.VMEM((units, width), F32),
+            pltpu.VMEM((width, units), F32),
+            pltpu.VMEM((width, units), F32),
             pltpu.VMEM((6, 8, width), F32),
             pltpu.VMEM((8, units), F32),
             half, half, stat, stat, stat, stat, stat, stat, half, half,
@@ -1070,7 +1271,7 @@
             collective_id=ident, has_side_effects=True, vmem_limit_bytes=60 << 20
         ),
         name="middle",
-    )(context, conv_context, context, conv_context, hidden, out_grad, out_grad, w.out0, w.out1, w.inner, w.outer, table)
+    )(early_rows, context, conv_context, context, conv_context, hidden, out_grad, out_grad, second, *vectors)
 
 
 def back_kernel(
@@ -1083,7 +1284,7 @@
     other_out, other_in, other_send, other_recv,
     twin_in, side_in, deep_in, hop_send, hop_recv,
     depth_pad, conv_pad, grad_pad, columns, weights, shifted_weights, tap_terms, products,
-    grads, grad_q, grad_k, grad_v, rows_total, tap_all,
+    grads, grad_q, grad_k, grad_v, key_turned, probs_all, scores_all, turned_query, rows_total, tap_all,
     acc_in, acc_point, acc_bias, acc_tap, acc_tap_bias, acc_depth,
     tap_out, tap_in, send_sem, recv_sem,
 ):
@@ -1185,27 +1386,30 @@
     grad_k[...] = jnp.zeros_like(grad_k)
     grad_v[...] = jnp.zeros_like(grad_v)
 
-    def attention_step(i, carry):
-        part = pl.ds(pl.multiple_of(i * block, block), block)
-        allowed = columns[:, KERNEL : KERNEL + 1] == marks_ref[0, KERNEL : KERNEL + 1, part]
-        query = q_ref[part, :]
-        context = grad_context[part, :]
-        total = jnp.zeros((block, WIDE), F32)
+    key_turned[...] = jnp.transpose(k_ref[...])
+    for start in range(0, rows, block):
+        part = slice(start, start + block)
+        keys = key_window(start, block, rows)
+        allowed = columns[keys, KERNEL : KERNEL + 1] == marks_ref[0, KERNEL : KERNEL + 1, part]
+        query, context = q_ref[part, :], grad_context[part, :]
+        query_turned, context_turned = jnp.transpose(query), jnp.transpose(context)
         for head in range(heads):
-            mine = (only(query, head) * (HEAD_DIM**-0.5)).astype(BF16)
-            grad_mine = only(context, head).astype(BF16)
-            scores = jnp.where(allowed, nt(k_ref[...], mine), MASK_FILL)
+            lanes = slice(head * HEAD_DIM, (head + 1) * HEAD_DIM)
+            place = slice(head * block, (head + 1) * block)
+            mine = (only_rows(query_turned, head) * (HEAD_DIM**-0.5)).astype(BF16)
+            scores = jnp.where(allowed, nn(k_ref[keys, :], mine), MASK_FILL)
             probs = jnp.exp(scores - lse_ref[0, head : head + 1, part])
-            grad_v[...] += nn(probs.astype(BF16), grad_mine)
-            grad_probs = nt(v_ref[...], grad_mine)
-            mixed = probs * grad_probs
+            probs_all[keys, place] = probs.astype(BF16)
+            mixed = probs * nn(v_ref[keys, :], only_rows(context_turned, head).astype(BF16))
             grad_scores = (mixed - probs * jnp.sum(mixed, axis=0, keepdims=True)).astype(BF16)
-            grad_k[...] += nn(grad_scores, mine)
-            total = total + tn(grad_scores, only(k_ref[...], head).astype(BF16))
-        grad_q[part, :] = total
-        return carry
-
-    lax.fori_loop(0, rows // block, attention_step, 0)
+            scores_all[keys, place] = grad_scores
+            turned_query[lanes, :] = nn(key_turned[lanes, keys], grad_scores)
+        turned_query[heads * HEAD_DIM :, :] = jnp.zeros((WIDE - heads * HEAD_DIM, block), F32)
+        grad_q[part, :] = jnp.transpose(turned_query[...])
+        contexts = jnp.concatenate([only(context, head).astype(BF16) for head in range(heads)], 0)
+        queries = jnp.concatenate([(only(query, head) * (HEAD_DIM**-0.5)).astype(BF16) for head in range(heads)], 0)
+        grad_v[keys, :] += nn(probs_all[keys, :], contexts)
+        grad_k[keys, :] += nn(scores_all[keys, :], queries)
 
     for load in loads:
         load.wait()
@@ -1230,8 +1434,8 @@
         grads[part, WIDE : 2 * WIDE] = grad_k[part, :].astype(BF16)
         grads[part, 2 * WIDE : 3 * WIDE] = grad_v[part, :].astype(BF16)
         acc_bias[...] += row_sums(grads[part, :].astype(F32))
-        grad_depth = nt(key_low, point_ref[...])
-        total = nt(grads[part, : 4 * WIDE], inputs_ref[...])
+        grad_depth = nn(key_low, point_ref[...])
+        total = nn(grads[part, : 4 * WIDE], inputs_ref[...])
         for c in range(chunks):
             lanes = slice(c * LANES, (c + 1) * LANES)
             depth_pad[c, pl.ds(base + EDGE, block), :] = grad_depth[:, lanes]
@@ -1239,7 +1443,7 @@
         return carry
 
     lax.fori_loop(0, rows // block, key_step, 0)
-    acc_point[...] += tn(dl_ref[...], grads[:, 4 * WIDE : 5 * WIDE])
+    acc_point[...] += tn(grads[:, 4 * WIDE : 5 * WIDE], dl_ref[...])
     acc_in[...] += tn(hidden_ref[...], grads[:, : 4 * WIDE])
     step = 32
 
@@ -1298,13 +1502,14 @@
         group = model // 2
         cut = model // CUTS
         empty = jnp.zeros((cut, width), F32)
+        point_grad = jnp.transpose(acc_point[...])
         for k in range(CUTS):
             part = pl.ds(k * cut, cut)
             for place in range(2):
                 first = acc_in[part, 2 * place * WIDE : 2 * place * WIDE + width]
                 second = acc_in[part, (2 * place + 1) * WIDE : (2 * place + 1) * WIDE + width]
                 pack_ref[k, pl.ds(place * cut, cut), :] = jnp.concatenate([first, second], 1).astype(BF16)
-            pack_ref[k, pl.ds(2 * cut, cut), :] = jnp.concatenate([acc_point[part, :width], empty], 1).astype(BF16)
+            pack_ref[k, pl.ds(2 * cut, cut), :] = jnp.concatenate([point_grad[k * cut : (k + 1) * cut, :width], empty], 1).astype(BF16)
         table_ref[...] = jnp.zeros_like(table_ref)
         lane = lax.broadcasted_iota(jnp.int32, (LANES, WIDE), 1)
         taps = jnp.where(lane == width, jnp.sum(acc_tap_bias[...], axis=1, keepdims=True), acc_tap[...])
@@ -1336,7 +1541,7 @@
                 table_ref[row : row + 1, :] = total[:, k * WIDE : (k + 1) * WIDE]
 
 
-def back(hidden, grad_context, grad_conv, residual, marks, kept, w, taps, depth, expand, small, pack, count, ident):
+def back(hidden, grad_context, grad_conv, residual, marks, kept, turned_weights, taps, depth, expand, small, pack, count, ident):
     q, k, v, cv, dl, kc, ca, probs, lse = kept
     seqs, _, rows = marks.shape
     tokens, model = hidden.shape
@@ -1388,10 +1593,14 @@
             vmem((rows, WIDE), F32),
             vmem((rows, WIDE), F32),
             vmem((rows, WIDE), F32),
+            vmem((WIDE, rows), BF16),
+            vmem((rows, tap_rows // TAP_ROWS * 256), BF16),
+            vmem((rows, tap_rows // TAP_ROWS * 256), BF16),
+            vmem((WIDE, 256), F32),
             vmem((model // LANES, rows, LANES), F32),
             vmem((LANES, rows), F32),
             vmem((model, 4 * WIDE), F32),
-            vmem((model, WIDE), F32),
+            vmem((WIDE, model), F32),
             vmem((8, 5 * WIDE), F32),
             vmem((LANES, WIDE), F32),
             vmem((LANES, LANES), F32),
@@ -1407,23 +1616,8 @@
         name="back",
     )(
         grad_context, grad_conv, marks, q, k, v, cv, ca, probs, lse, hidden, residual, dl, kc,
-        jnp.concatenate([w.query, w.key, w.value, w.conv], 1), w.point, taps, depth, expand, small, pack,
+        *turned_weights, taps, depth, expand, small, pack,
     )
-
-
-def marks_of(segment):
-    masks = [same_segment(segment, tap - HALF, HALF) for tap in range(KERNEL)]
-    blank = jnp.zeros_like(segment)
-    return jnp.stack([m.astype(F32) for m in masks] + [segment.astype(F32)] + [blank.astype(F32)] * (TAP_ROWS - KERNEL - 1))
-
-
-def expansion(heads):
-    row = lax.broadcasted_iota(jnp.int32, (LANES, KERNEL * WIDE), 0)
-    column = lax.broadcasted_iota(jnp.int32, (LANES, KERNEL * WIDE), 1)
-    tap, lane = column // WIDE, column % WIDE
-    wanted = (lane // HEAD_DIM) * TAP_ROWS + tap
-    inside = jnp.logical_and(lane < heads * HEAD_DIM, row < 2 * heads * TAP_ROWS)
-    return jnp.logical_and(inside, row % (heads * TAP_ROWS) == wanted).astype(BF16)
 
 
 def padded(value, multiple):
@@ -1432,30 +1626,39 @@
     return jnp.pad(value, [(0, 0)] * (value.ndim - 2) + [(0, extra), (0, 0)])
 
 
-def recut(pack, sizes, count):
-    if count == CUTS:
+def recut(pack, sizes, unit, start, count):
+    if count == start:
         return pack
-    unit, parts, start = pack.shape[1] // sum(sizes), [], 0
+    parts, low = [], 0
     for size in sizes:
-        rows = pack[:, start : start + size * unit].reshape(-1, pack.shape[2])
+        rows = pack[:, low : low + size * unit].reshape(-1, pack.shape[2])
         parts.append(rows.reshape(count, -1, pack.shape[2]))
-        start += size * unit
-    return padded(jnp.concatenate(parts, 1), 16)
+        low += size * unit
+    return padded(jnp.concatenate(parts, 1), TAP_ROWS)
+
+
+def gather_plain(weights, count, ident):
+    q, k, v, c, p, depth, out_w, in_w, outer_w = weights
+    depth = jnp.pad(depth.T, ((0, 0), (0, q.shape[1] - KERNEL)))
+    pairs = [jnp.concatenate(pair, 1) for pair in ((q, k), (v, c), (p, depth), (out_w[0], out_w[1]))]
+    first = padded(jnp.concatenate(pairs[:3], 0), TAP_ROWS)[None]
+    second = padded(jnp.concatenate([pairs[3], in_w[0], outer_w[0]], 0), TAP_ROWS)[None]
+    return recut(gather(first, count, ident), (1, 1, 1), q.shape[0], count, CUTS), second
 
 
 def final_plain(first, second, table, share, share_ffn, width, group, taps):
     model = 2 * group
     depth = jnp.concatenate([table[72 + KERNEL * k : 72 + KERNEL * (k + 1)] for k in range(model // WIDE)], 1)
-    row = lambda at_row, size: table[at_row : at_row + 6].reshape(1, -1)[:, :size]
+    row = lambda at_row, size: table[at_row : at_row + 6].reshape(-1)[:size]
     out = first[:share]
     return (
         second[:share, :width], second[:share, width:], second[share : 2 * share, :width],
         row(54, width), row(55, width),
         lax.dynamic_slice_in_dim(depth, lax.axis_index("dp") * share, share, 1),
         second[2 * share : 3 * share, :width], row(56, width),
-        table[:taps, :width].T, table[None, :taps, width], second[share : 2 * share, width:], row(57, width),
-        jnp.stack([out[:, :width].T, out[:, width:].T]), row(105, model), row(99, model), row(102, model),
-        first[share : share + share_ffn].T, row(64, 4 * group), first[share + share_ffn : share + 2 * share_ffn],
+        table[:taps, :width], table[:taps, width], second[share : 2 * share, width:], row(57, width),
+        jnp.stack([out[:, :width], out[:, width:]]), row(105, model), row(99, model), row(102, model),
+        first[share : share + share_ffn], row(64, 4 * group)[None], first[share + share_ffn : share + 2 * share_ffn],
         row(58, group), row(60, group), row(62, group),
     )
 
@@ -1467,77 +1670,33 @@
     out_weight, out_bias, norm1_gain, norm1_bias, ffn_in_weight, ffn_in_bias, ffn_out_weight,
     ffn_out_bias, norm2_gain, norm2_bias, out_grad,
 ):
-    me = lax.axis_index("mp")
     share, width = query_weight.shape
     model = hidden.shape[1]
     group = ffn_out_bias.shape[0]
     share_ffn = ffn_out_weight.shape[1]
-    depth_wide = jnp.pad(depth_weight.T, ((0, 0), (0, width - KERNEL)))
-    first = jnp.concatenate(
-        [
-            jnp.concatenate([query_weight, key_weight], 1),
-            jnp.concatenate([value_weight, conv_weight], 1),
-            jnp.concatenate([point_weight, depth_wide], 1),
-        ],
-        0,
+    heads = width // HEAD_DIM
+    weights = (
+        query_weight, key_weight, value_weight, conv_weight, point_weight, depth_weight,
+        out_weight.transpose(0, 2, 1), ffn_in_weight.transpose(0, 2, 1), ffn_out_weight,
     )
-    out_cut = jnp.concatenate([out_weight[0].T, out_weight[1].T], 1)
-    second = jnp.concatenate([out_cut, ffn_in_weight[0].T, ffn_out_weight[0]], 0)
-    first_all = gather(padded(first, 16)[None], count, 1)
-
-    def cut(source, start, size, low, high):
-        return source[:, start : start + size, low:high].reshape(count * size, high - low)
-
-    def cut_wide(source, start, low):
-        return jnp.pad(cut(source, start, share, low, low + width), ((0, 0), (0, WIDE - width)))
-
-    w = Group(
-        query=cut_wide(first_all, 0, 0),
-        key=cut_wide(first_all, 0, width),
-        value=cut_wide(first_all, share, 0),
-        conv=cut_wide(first_all, share, width),
-        point=cut_wide(first_all, 2 * share, 0),
-        depth=cut(first_all, 2 * share, share, width, width + TAP_ROWS).T,
+    first, second = (gather_first if share % TAP_ROWS == 0 else gather_plain)(weights, count, 1)
+    seqs = doc_lengths.shape[0]
+    early = seqs - 1 if count == CUTS else 0
+    biases = [kernel_bias, query_bias, value_bias, point_bias, conv_bias]
+    q, k, v, cv, dl, kc, ca, probs, cc, ctx, lse, second_all, marks, taps, depth, expand, *rest = front(
+        hidden, doc_lengths, first, kernel_weight.T, biases, second, count, early, 2
     )
-    p = Group(
-        query_bias=query_bias, value_bias=value_bias, point_bias=point_bias, kernel_weight=kernel_weight,
-        kernel_bias=kernel_bias, conv_bias=conv_bias, out_bias=out_bias, norm1_gain=norm1_gain,
-        norm1_bias=norm1_bias, ffn_in_bias=ffn_in_bias[0], ffn_out_bias=ffn_out_bias,
-        norm2_gain=norm2_gain, norm2_bias=norm2_bias,
-    )
-    seqs = doc_lengths.shape[0]
-    seq_rows = hidden.shape[0] // seqs
-    spans = [slice(s * seq_rows, (s + 1) * seq_rows) for s in range(seqs)]
-    segments = [segment_ids(doc_lengths[q], seq_rows) for q in range(seqs)]
-    marks = jnp.stack([marks_of(segment) for segment in segments])
-    heads = width // HEAD_DIM
-    vectors = jnp.stack(
-        [jnp.pad(b, (0, WIDE - width)) for b in (query_bias, value_bias, point_bias, conv_bias)] * 2
-    )
-    order = kernel_weight.T.reshape(2, heads, KERNEL, width)
-    order = jnp.where(me == 0, order, order[::-1])
-    taps = jnp.pad(order, ((0, 0), (0, 0), (0, TAP_ROWS - KERNEL), (0, WIDE - width))).reshape(-1, WIDE)
-    taps = jnp.pad(taps, ((0, LANES - taps.shape[0]), (0, 0)))
-    bias = lax.dynamic_slice_in_dim(kernel_bias.reshape(2, heads, KERNEL), me, 1, 0)[0]
-    bias = jnp.pad(bias, ((0, 0), (0, TAP_ROWS - KERNEL))).reshape(-1, 1)
-    bias = jnp.broadcast_to(bias, (bias.shape[0], LANES))
-    expand = expansion(heads)
-    q, k, v, cv, dl, kc, ca, probs, cc, ctx, lse, second_all = front(
-        hidden, marks, w, vectors, w.depth.astype(F32), bias, expand, taps, padded(second, 16)[None], count, 2
-    )
-    w.out0 = cut_wide(second_all, 0, 0)
-    w.out1 = cut_wide(second_all, 0, width)
-    w.inner = cut(second_all, share, share_ffn, 0, group)
-    w.outer = cut(second_all, share + share_ffn, share_ffn, 0, group)
+    turned_weights, early_rows = rest[:2], rest[2]
+    vectors = [out_bias, norm1_gain, norm1_bias, ffn_out_bias, norm2_gain, norm2_bias, ffn_in_bias]
     output, grad_residual, grad_context, grad_conv, pack_mid, sums_mid = middle(
-        ctx, cc, hidden, out_grad, w, p, me, 4
+        early * (hidden.shape[0] // seqs), early_rows, ctx, cc, hidden, out_grad, recut(second_all, (1, 2, 2), share, count, CUTS), vectors, 4
     )
     grad_input, own_last, other_last, pack_back, table, first_sum = back(
         hidden, grad_context, grad_conv, grad_residual, marks, (q, k, v, cv, dl, kc, ca, probs, lse),
-        w, taps, w.depth.astype(F32), expand, sums_mid, recut(pack_mid, (1, 2, 2), count), count, 5,
+        turned_weights, taps, depth, expand, sums_mid, recut(pack_mid, (1, 2, 2), model // CUTS, CUTS, count), count, 5,
     )
     second_sum, totals, grad_input = tail(
-        recut(pack_back, (1, 1, 1), count), table, own_last, other_last, grad_input, count, 3
+        recut(pack_back, (1, 1, 1), model // CUTS, CUTS, count), table, own_last, other_last, grad_input, count, 3
     )
     small_cuts = (share, share_ffn, width, group, 2 * heads * KERNEL)
     if share % TAP_ROWS == 0:
@@ -1547,8 +1706,8 @@
     q_g, k_g, v_g, q_b, v_b, depth_g, p_g, p_b, kw_g, kb_g, c_g, c_b, out_g, out_b, gain1, bias1 = results[:16]
     inner_g, inner_b, outer_g, outer_b, gain2, bias2 = results[16:]
     return (
-        output, grad_input, q_g, k_g, v_g, q_b[0], v_b[0], depth_g, p_g, p_b[0], kw_g, kb_g[0], c_g, c_b[0], out_g,
-        out_b[0], gain1[0], bias1[0], inner_g[None], inner_b, outer_g[None], outer_b[0], gain2[0], bias2[0],
+        output, grad_input, q_g, k_g, v_g, q_b, v_b, depth_g, p_g, p_b, kw_g.T, kb_g, c_g, c_b, out_g.transpose(0, 2, 1),
+        out_b, gain1, bias1, inner_g.T[None], inner_b, outer_g[None], outer_b, gain2, bias2,
     )
 
 

time: 412 us -> 357 us (0.87)
  local copies, waits for them, and re-layouts: 28 us -> 5.37 us
  Pallas kernels: 367 us -> 350 us
  other arithmetic: 14.3 us -> 0 us
    pallas_call x3, Pallas kernels: 220 us -> 206 us  [the longest x1 103 us: middle(): pl.pallas_call(functools.partial(middle_kernel, blocks, early // rows), g...]
    pallas_call x6 -> x0, other arithmetic: 7.59 us -> none  [final(): pl.pallas_call(functools.partial(final_kernel, count), out_shape=(shape(s...]
    pad x20 -> x0, local copies, waits for them, and re-layouts: 6.44 us -> none  [the longest x7 5.73 us: cut_wide(): jnp.pad(cut(source, start, share, low, low + width), ((0, 0), (0, WIDE -...]
    slice x4 -> x0, local copies, waits for them, and re-layouts: 6 us -> none  [cut(): source[:, start:start + size, low:high].reshape(count * size, high - low)]
    unnamed x52 -> x6, local copies, waits for them, and re-layouts: 11.2 us -> 5.37 us
where the time goes in v4:
time: 357 us; the launch traced here: 356 us
  Pallas kernels  350 us (98%)
  local copies, waits for them, and re-layouts  5.37 us (2%)
    pallas_call x1, Pallas kernels, back(): pl.pallas_call(functools.partial(back_kernel, seqs, count), grid=(seqs,),...  108 us
    pallas_call x1, Pallas kernels, middle(): pl.pallas_call(functools.partial(middle_kernel, blocks, early // rows), g...  103 us
    pallas_call x1, Pallas kernels, front(): pl.pallas_call(functools.partial(front_kernel, seqs, count, early), grid=...  81.7 us
    pallas_call x1, Pallas kernels, tail(): pl.pallas_call(functools.partial(tail_kernel, count, start), out_shape=(j...  33.8 us
    pallas_call x1, Pallas kernels, gather_first(): pl.pallas_call(functools.partial(pack_kernel, count), out_shape=(jax.Shap...  21.3 us

profile of v4, /device:TPU:8, one launch (start us, length us, event | category | flops | bytes accessed | tf_op | source)
XLA Modules:
  0.0 355.7 jit_solution(5279912761050931495)
XLA Ops:
  0.7 21.3 %weight_gather.1 = (bf16[16,144,384]{2,1,0:T(8,128)(2,1)}, bf16[1,240,384]{2,1,0:T(8,128)(2,1)}) custom-call(bf16[48,192]{1,0:T(8,128)(2,1)} %q_ref.1, bf16[48,192]{1,0:T(8,128)(2,1)} %k_ref.1, bf16[48,192]{1,0:T(8,128)(2,1)} %v_ref.1, bf16[48,192]{1,0:T(8,128)(2,1)} %c_ref.1, bf16[48,192]{1,0:T(8,128)(2,1)} %p_ref.1, bf16[9,48]{1,0:T(8,128)(2,1)} %depth_ref.1, ...), custom_call_target="tpu_custom_call" | custom-call | tf_op jit(solution)/shard_map/weight_gather/pallas_call | solution.py:145
  22.0 81.7 %front.1 = (bf16[3072,256]{1,0:T(8,128)(2,1)}, bf16[3072,256]{1,0:T(8,128)(2,1)}, bf16[3072,256]{1,0:T(8,128)(2,1)}, f32[3072,256]{1,0:T(8,128)}, bf16[3072,768]...) custom-call(bf16[3072,768]{1,0:T(8,128)(2,1)} %hidden_any.1, ...), custom_call_target="tpu_custom_call" | custom-call | tf_op jit(solution)/shard_map/front/pallas_call | solution.py:884
  103.6 102.9 %middle.1 = (bf16[3072,384]{1,0:T(8,128)(2,1)}, f32[3072,384]{1,0:T(8,128)}, bf16[3072,256]{1,0:T(8,128)(2,1)}, bf16[3072,256]{1,0:T(8,128)(2,1)}, bf16[16,240,384]{2,1,0:T(8,128)(2,1)}, /*index=5*/f32[8,1536]{1,0:T(8,128)}) custom-call(bf16[3072,384]{1,0:T(8,128)(2,1)} %get-tuple-element.84.early_ref, ...), custom_call_target="tpu_custom_call" | custom-call | tf_op jit(solution)/shard_map/middle/pallas_call | solution.py:1223
  206.6 107.7 %back.1 = (f32[3072,384]{1,0:T(8,128)}, f32[1024,384]{1,0:T(8,128)}, bf16[1024,384]{1,0:T(8,128)(2,1)}, bf16[16,144,384]{2,1,0:T(8,128)(2,1)}, f32[112,256]{1,0:T(8,128)}, /*index=5*/f32[240,384]{1,0:T(8,128)}) custom-call(bf16[3072,256]{1,0:T(8,128)(2,1)} %get-tuple-element.89.grad_context, bf16[3072,256]{1,0:T(8,128)(2,1)} %get-tuple-element.90.grad_conv_ref, ...), custom_call_target="tpu_custom_call" | custom-call | tf_op jit(solution)/shard_map/back/pallas_call | solution.py:1555
  314.3 0.0 copy-start.1
  314.3 33.8 %tail.1 = (f32[144,384]{1,0:T(8,128)}, f32[112,256]{1,0:T(8,128)}, f32[3072,384]{1,0:T(8,128)}) custom-call(bf16[16,144,384]{2,1,0:T(8,128)(2,1)} %get-tuple-element.109.in_ref, f32[112,256]{1,0:T(8,128)} %get-tuple-element.110.table_ref, f32[1024,384]{1,0:T(8,128)} %get-tuple-element.111.own_ref, ...), custom_call_target="tpu_custom_call", output_to_operand_aliasing={{2}: (4, {})} | custom-call | tf_op jit(solution)/shard_map/tail/pallas_call | solution.py:384
  348.2 2.1 final.1
  350.3 0.0 copy-done.1
  350.3 0.0 copy-start
  350.3 1.4 copy.53
  351.7 1.8 copy-done
  353.5 2.2 copy.54
Async XLA Ops:
  314.3 35.9 %copy-start.1 = (bf16[3072,384]{1,0:T(8,128)(2,1)S(1)}, bf16[3072,384]{1,0:T(8,128)(2,1)}, u32[]{:S(2)}) copy-start(bf16[3072,384]{1,0:T(8,128)(2,1)} %get-tuple-element.164) | copy-start | bytes 7077892
  350.3 3.2 copy-start

commit v5 on v4

--- a/solution.py
+++ b/solution.py
@@ -594,7 +594,7 @@
     marks_ref, taps_ref, depth_ref, expand_ref, inputs_turned_ref, point_turned_ref, early_ref,
     lead_ref, out0_nat, out1_nat, part_out, part_send, part_recv,
     query_ref, key_ref, value_ref, conv_ref, point_ref, vec_ref, bias_ref, depth_wide, tile,
-    rows_pad, conv_pad, columns, weights, query_turned, value_turned, context_turned, tap_out, tap_in,
+    masks, rows_pad, conv_pad, columns, weights, query_turned, value_turned, context_turned, tap_out, tap_in,
     send_sem, recv_sem, own_sem, gather_send, gather_recv,
 ):
     s = pl.program_id(0)
@@ -713,18 +713,23 @@
     for c in range(chunks):
         rows_pad[c, pl.ds(EDGE, rows), :] = hidden[:, c * LANES : (c + 1) * LANES].astype(F32)
 
-    step = 32
+    step = masks.shape[1]
 
     def depth_step(i, carry):
         base = pl.multiple_of(i * step, step)
-        total = [jnp.zeros((step, LANES), F32)] * chunks
+        part = pl.ds(base, step)
         for tap in range(KERNEL):
-            mask = jnp.broadcast_to(columns[pl.ds(base, step), tap : tap + 1], (step, LANES))
-            for c in range(chunks):
-                moved = rows_pad[c, pl.ds(base + EDGE + tap - HALF, step), :]
-                total[c] = total[c] + (moved * mask) * depth_ref[tap : tap + 1, c * LANES : (c + 1) * LANES]
-        for c in range(chunks):
-            dl_ref[pl.ds(base, step), c * LANES : (c + 1) * LANES] = total[c].astype(BF16)
+            masks[tap] = jnp.broadcast_to(columns[part, tap : tap + 1], (step, LANES))
+        for first in range(0, chunks, 2):
+            total = [jnp.zeros((step, LANES), F32)] * 2
+            for tap in range(KERNEL):
+                mask = masks[tap]
+                for k in range(2):
+                    c = first + k
+                    moved = rows_pad[c, pl.ds(base + EDGE + tap - HALF, step), :]
+                    total[k] = total[k] + (moved * mask) * depth_ref[tap : tap + 1, c * LANES : (c + 1) * LANES]
+            for k in range(2):
+                dl_ref[part, (first + k) * LANES : (first + k + 1) * LANES] = total[k].astype(BF16)
         return carry
 
     lax.fori_loop(0, rows // step, depth_step, 0)
@@ -752,7 +757,7 @@
     )
     swap_taps.start()
 
-    @pl.when(jnp.logical_and(s >= 1, s < early + 1))
+    @pl.when(jnp.logical_and(s >= 1, s < early))
     def _():
         for piece in range(PIECES // 2, PIECES):
             swap_part(s - 1, piece).start()
@@ -840,7 +845,7 @@
             part_out[s, part, :] = other.astype(BF16)
             return carry
 
-        lax.fori_loop(0, rows // block, part_step, 0)
+        lax.fori_loop(0, jnp.where(s == early - 1, rows // 2 // block, rows // block), part_step, 0)
         for piece in range(PIECES // 2):
             swap_part(s, piece).start()
 
@@ -852,7 +857,7 @@
     def _():
         end_hops(1)
         for which in range(early):
-            for piece in range(PIECES):
+            for piece in range(PIECES if which < early - 1 else PIECES // 2):
                 swap_part(which, piece).wait()
 
 
@@ -922,6 +927,7 @@
             pltpu.VMEM((tap_rows, LANES), F32),
             pltpu.VMEM((model, WIDE), F32),
             pltpu.VMEM((WIDE, WIDE), F32),
+            pltpu.VMEM((KERNEL, 64, LANES), F32),
             pltpu.VMEM((model // LANES, rows + 2 * EDGE, LANES), F32),
             pltpu.VMEM((2, rows + 2 * EDGE, LANES), F32),
             pltpu.VMEM((rows, LANES), F32),
@@ -964,17 +970,18 @@
 
 
 SLOTS = 4
+LAST_LAG = 6
 FFN_STEP = 256
 
 
 def middle_kernel(
     blocks, early,
-    early_ref, context_ref, conv_ref, context_late_ref, conv_late_ref, hidden_ref, grad_ref, grad_late_ref, second_ref,
+    early_ref, context_ahead_ref, conv_ahead_ref, context_ref, conv_ref, context_late_ref, conv_late_ref, hidden_ref, grad_ref, grad_late_ref, second_ref,
     ob_ref, gain1_ref, bias1_ref, outb_ref, gain2_ref, bias2_ref, inb_ref,
     output_ref, residual_ref, grad_context_ref, grad_conv_ref, pack_ref, small_ref,
     out0_ref, out1_ref, inner_ref, outer_ref, vec_ref, inner_nat, outer_turned, out0_nat, out1_nat, low_units, branch_ref, acc_out0, acc_out1, state, scale_ring, act_ring, slope_ring, low_ring, summed_ring, normed_ring, stat_ring,
     acc_inner, acc_outer, acc_small, acc_bias,
-    branch_out, branch_in, stat1_out, stat1_in, stat2_out, stat2_in, stat3_out, stat3_in, back_out, back_in,
+    branch_send, branch_recv, branch_out, branch_in, stat1_out, stat1_in, stat2_out, stat2_in, stat3_out, stat3_in, back_out, back_in,
     send_sem, recv_sem,
 ):
     i = pl.program_id(0)
@@ -994,8 +1001,18 @@
             device_id_type=MESH,
         )
 
+    def ahead(slot):
+        return pltpu.make_async_remote_copy(
+            src_ref=branch_out.at[slot],
+            dst_ref=branch_in.at[slot],
+            send_sem=branch_send.at[slot],
+            recv_sem=branch_recv.at[slot],
+            device_id=(dp, 1 - me),
+            device_id_type=MESH,
+        )
+
     kinds = [
-        (branch_out, branch_in), (stat1_out, stat1_in), (stat2_out, stat2_in), (stat3_out, stat3_in), (back_out, back_in),
+        None, (stat1_out, stat1_in), (stat2_out, stat2_in), (stat3_out, stat3_in), (back_out, back_in),
     ]
 
     def fresh(kind, b, slot):
@@ -1034,20 +1051,19 @@
         acc_small[...] = jnp.zeros_like(acc_small)
         acc_bias[...] = jnp.zeros_like(acc_bias)
 
+    cuts = branch_in.shape[0] // (blocks - early)
+
+    @pl.when(i < cuts * (blocks - early))
+    def _():
+        theirs = pl.ds(pl.multiple_of((1 - me) * width, width), width)
+        other = nn(context_ahead_ref[...], out0_nat[:, theirs]) + nn(conv_ahead_ref[...], out1_nat[:, theirs])
+        branch_out[i] = other.astype(BF16)
+        ahead(i).start()
+
     @pl.when(i < blocks)
     def _():
         b = i
-        slot = lax.rem(b, SLOTS)
-        theirs = pl.ds(pl.multiple_of((1 - me) * width, width), width)
         ours = pl.ds(pl.multiple_of(me * width, width), width)
-
-        @pl.when(b >= early)
-        def _():
-            fresh(0, b - early, slot)
-            other = nn(context_ref[...], out0_nat[:, theirs]) + nn(conv_ref[...], out1_nat[:, theirs])
-            branch_out[slot] = other.astype(BF16)
-            message(0, *kinds[0], slot).start()
-
         own = nn(context_ref[...], out0_nat[:, ours]) + nn(conv_ref[...], out1_nat[:, ours])
         state[lax.rem(b, 8)] = hidden_ref[:, ours].astype(F32) + (own + vec(0))
 
@@ -1063,8 +1079,11 @@
 
         @pl.when(b >= early)
         def _():
-            message(0, *kinds[0], slot).wait_recv()
-            state[lax.rem(b, 8)] += branch_in[slot].astype(F32)
+            size = branch_in.shape[1]
+            for k in range(cuts):
+                piece = cuts * (b - early) + k
+                ahead(piece).wait_recv()
+                state[lax.rem(b, 8), pl.ds(k * size, size), :] += branch_in[piece].astype(F32)
 
         residual = state[lax.rem(b, 8)]
         total = jnp.sum(residual, axis=1, keepdims=True)
@@ -1171,9 +1190,9 @@
         back_out[slot] = low
         message(4, *kinds[4], slot).start()
 
-    @pl.when(i >= 5)
-    def _():
-        b = i - 5
+    @pl.when(i >= LAST_LAG)
+    def _():
+        b = i - LAST_LAG
         slot = lax.rem(b, SLOTS)
         message(4, *kinds[4], slot).wait_recv()
         theirs = pl.ds(pl.multiple_of((1 - me) * width, width), width)
@@ -1186,9 +1205,11 @@
         acc_out0[...] += tn(context_late_ref[...], branch)
         acc_out1[...] += tn(conv_late_ref[...], branch)
 
-    @pl.when(i == blocks + 4)
-    def _():
-        for kind in range(5):
+    @pl.when(i == blocks + LAST_LAG - 1)
+    def _():
+        for slot in range(cuts * (blocks - early)):
+            ahead(slot).wait_send()
+        for kind in range(1, 5):
             for slot in range(SLOTS):
                 message(kind, *kinds[kind], slot).wait_send()
         cut, cut_ffn = 2 * width // CUTS, hidden_units // CUTS
@@ -1213,16 +1234,19 @@
     units = vectors[-1].shape[1]
     rows = 256
     blocks = tokens // rows
+    early = early // rows
 
     def block(columns, lag):
         return pl.BlockSpec((rows, columns), lambda i: (jnp.clip(i - lag, 0, blocks - 1), 0))
 
+    cuts = 2 if 2 * early >= blocks else 1
+    ahead = pl.BlockSpec((rows // cuts, local), lambda i: (jnp.minimum(cuts * early + i, cuts * blocks - 1), 0))
     whole = pl.BlockSpec(memory_space=pltpu.VMEM)
     stat = pltpu.VMEM((SLOTS, 8, rows), F32)
     half = pltpu.VMEM((SLOTS, rows, width), BF16)
     return pl.pallas_call(
-        functools.partial(middle_kernel, blocks, early // rows),
-        grid=(blocks + 5,),
+        functools.partial(middle_kernel, blocks, early),
+        grid=(blocks + LAST_LAG,),
         out_shape=(
             jax.ShapeDtypeStruct((tokens, width), BF16),
             jax.ShapeDtypeStruct((tokens, width), F32),
@@ -1232,11 +1256,11 @@
             jax.ShapeDtypeStruct((8, units), F32),
         ),
         in_specs=[
-            block(width, 0), block(local, 0), block(local, 0), block(local, 5), block(local, 5), block(model, 0), block(width, 2),
+            block(width, 0), ahead, ahead, block(local, 0), block(local, 0), block(local, LAST_LAG), block(local, LAST_LAG), block(model, 0), block(width, 2),
             block(width, 3),
         ]
         + [whole] * 8,
-        out_specs=(block(width, 3), block(width, 4), block(local, 5), block(local, 5), whole, whole),
+        out_specs=(block(width, 3), block(width, 4), block(local, LAST_LAG), block(local, LAST_LAG), whole, whole),
         scratch_shapes=[
             pltpu.VMEM((model, local), BF16),
             pltpu.VMEM((model, local), BF16),
@@ -1263,7 +1287,11 @@
             pltpu.VMEM((width, units), F32),
             pltpu.VMEM((6, 8, width), F32),
             pltpu.VMEM((8, units), F32),
-            half, half, stat, stat, stat, stat, stat, stat, half, half,
+            pltpu.SemaphoreType.DMA((cuts * (blocks - early),)),
+            pltpu.SemaphoreType.DMA((cuts * (blocks - early),)),
+            pltpu.VMEM((cuts * (blocks - early), rows // cuts, width), BF16),
+            pltpu.VMEM((cuts * (blocks - early), rows // cuts, width), BF16),
+            stat, stat, stat, stat, stat, stat, half, half,
             pltpu.SemaphoreType.DMA((5, SLOTS)),
             pltpu.SemaphoreType.DMA((5, SLOTS)),
         ],
@@ -1271,7 +1299,7 @@
             collective_id=ident, has_side_effects=True, vmem_limit_bytes=60 << 20
         ),
         name="middle",
-    )(early_rows, context, conv_context, context, conv_context, hidden, out_grad, out_grad, second, *vectors)
+    )(early_rows, context, conv_context, context, conv_context, context, conv_context, hidden, out_grad, out_grad, second, *vectors)
 
 
 def back_kernel(
@@ -1283,7 +1311,7 @@
     hidden_ref, residual_ref, dl_ref, kc_ref, load_sem,
     other_out, other_in, other_send, other_recv,
     twin_in, side_in, deep_in, hop_send, hop_recv,
-    depth_pad, conv_pad, grad_pad, columns, weights, shifted_weights, tap_terms, products,
+    masks, depth_pad, conv_pad, grad_pad, columns, weights, shifted_weights, tap_terms, products,
     grads, grad_q, grad_k, grad_v, key_turned, probs_all, scores_all, turned_query, rows_total, tap_all,
     acc_in, acc_point, acc_bias, acc_tap, acc_tap_bias, acc_depth,
     tap_out, tap_in, send_sem, recv_sem,
@@ -1445,22 +1473,26 @@
     lax.fori_loop(0, rows // block, key_step, 0)
     acc_point[...] += tn(grads[:, 4 * WIDE : 5 * WIDE], dl_ref[...])
     acc_in[...] += tn(hidden_ref[...], grads[:, : 4 * WIDE])
-    step = 32
+    step = masks.shape[1]
 
     def depth_step(i, carry):
         base = pl.multiple_of(i * step, step)
         part = pl.ds(base, step)
-        total = [rows_total[c, part, :] for c in range(chunks)]
         for j in range(KERNEL):
-            mirror = KERNEL - 1 - j
-            mask = jnp.broadcast_to(columns[part, j : j + 1], (step, LANES))
-            for c in range(chunks):
-                lanes = slice(c * LANES, (c + 1) * LANES)
-                near = depth_pad[c, pl.ds(base + EDGE + j - HALF, step), :] * mask
-                total[c] = total[c] + near * depth_ref[mirror : mirror + 1, lanes]
-                acc_depth[mirror, :, lanes] += row_sums(near * hidden_ref[part, lanes].astype(F32))
-        for c in range(chunks):
-            rows_total[c, part, :] = total[c]
+            masks[j] = jnp.broadcast_to(columns[part, j : j + 1], (step, LANES))
+        for first in range(0, chunks, 2):
+            total = [rows_total[first + k, part, :] for k in range(2)]
+            lanes = [slice((first + k) * LANES, (first + k + 1) * LANES) for k in range(2)]
+            here = [hidden_ref[part, lanes[k]].astype(F32) for k in range(2)]
+            for j in range(KERNEL):
+                mirror = KERNEL - 1 - j
+                mask = masks[j]
+                for k in range(2):
+                    near = depth_pad[first + k, pl.ds(base + EDGE + j - HALF, step), :] * mask
+                    total[k] = total[k] + near * depth_ref[mirror : mirror + 1, lanes[k]]
+                    acc_depth[mirror, :, lanes[k]] += row_sums(near * here[k])
+            for k in range(2):
+                rows_total[first + k, part, :] = total[k]
         return carry
 
     lax.fori_loop(0, rows // step, depth_step, 0)
@@ -1581,6 +1613,7 @@
         ]
         + hop_scratch(count, pack.shape[1], pack.shape[2])
         + [
+            vmem((KERNEL, 64, LANES), F32),
             vmem((model // LANES, padded_rows, LANES), F32),
             vmem((2, padded_rows, LANES), F32),
             vmem((2, padded_rows, LANES), F32),
@@ -1689,7 +1722,7 @@
     turned_weights, early_rows = rest[:2], rest[2]
     vectors = [out_bias, norm1_gain, norm1_bias, ffn_out_bias, norm2_gain, norm2_bias, ffn_in_bias]
     output, grad_residual, grad_context, grad_conv, pack_mid, sums_mid = middle(
-        early * (hidden.shape[0] // seqs), early_rows, ctx, cc, hidden, out_grad, recut(second_all, (1, 2, 2), share, count, CUTS), vectors, 4
+        max(2 * early - 1, 0) * (hidden.shape[0] // seqs) // 2, early_rows, ctx, cc, hidden, out_grad, recut(second_all, (1, 2, 2), share, count, CUTS), vectors, 4
     )
     grad_input, own_last, other_last, pack_back, table, first_sum = back(
         hidden, grad_context, grad_conv, grad_residual, marks, (q, k, v, cv, dl, kc, ca, probs, lse),

time: 357 us -> 344 us (0.964)
  Pallas kernels: 350 us -> 336 us
    pallas_call x1, Pallas kernels: 81.7 us -> 76 us  [front(): pl.pallas_call(functools.partial(front_kernel, seqs, count, early), grid=...]
where the time goes in v5:
time: 344 us; the launch traced here: 342 us
  Pallas kernels  336 us (98%)
  local copies, waits for them, and re-layouts  5.37 us (2%)
    pallas_call x1, Pallas kernels, back(): pl.pallas_call(functools.partial(back_kernel, seqs, count), grid=(seqs,),...  106 us
    pallas_call x1, Pallas kernels, middle(): pl.pallas_call(functools.partial(middle_kernel, blocks, early), grid=(blo...  100 us
    pallas_call x1, Pallas kernels, front(): pl.pallas_call(functools.partial(front_kernel, seqs, count, early), grid=...  76 us
    pallas_call x1, Pallas kernels, tail(): pl.pallas_call(functools.partial(tail_kernel, count, start), out_shape=(j...  31 us
    pallas_call x1, Pallas kernels, gather_first(): pl.pallas_call(functools.partial(pack_kernel, count), out_shape=(jax.Shap...  21.3 us

profile of v5, /device:TPU:8, one launch (start us, length us, event | category | flops | bytes accessed | tf_op | source)
XLA Modules:
  0.0 342.5 jit_solution(15702132886975581697)
XLA Ops:
  0.7 21.3 %weight_gather.1 = (bf16[16,144,384]{2,1,0:T(8,128)(2,1)}, bf16[1,240,384]{2,1,0:T(8,128)(2,1)}) custom-call(bf16[48,192]{1,0:T(8,128)(2,1)} %q_ref.1, bf16[48,192]{1,0:T(8,128)(2,1)} %k_ref.1, bf16[48,192]{1,0:T(8,128)(2,1)} %v_ref.1, bf16[48,192]{1,0:T(8,128)(2,1)} %c_ref.1, bf16[48,192]{1,0:T(8,128)(2,1)} %p_ref.1, bf16[9,48]{1,0:T(8,128)(2,1)} %depth_ref.1, ...), custom_call_target="tpu_custom_call" | custom-call | tf_op jit(solution)/shard_map/weight_gather/pallas_call | solution.py:145
  22.0 76.0 %front.1 = (bf16[3072,256]{1,0:T(8,128)(2,1)}, bf16[3072,256]{1,0:T(8,128)(2,1)}, bf16[3072,256]{1,0:T(8,128)(2,1)}, f32[3072,256]{1,0:T(8,128)}, bf16[3072,768]...) custom-call(bf16[3072,768]{1,0:T(8,128)(2,1)} %hidden_any.1, ...), custom_call_target="tpu_custom_call" | custom-call | tf_op jit(solution)/shard_map/front/pallas_call | solution.py:889
  98.0 100.4 %middle.1 = (bf16[3072,384]{1,0:T(8,128)(2,1)}, f32[3072,384]{1,0:T(8,128)}, bf16[3072,256]{1,0:T(8,128)(2,1)}, bf16[3072,256]{1,0:T(8,128)(2,1)}, bf16[16,240,384]{2,1,0:T(8,128)(2,1)}, /*index=5*/f32[8,1536]{1,0:T(8,128)}) custom-call(bf16[3072,384]{1,0:T(8,128)(2,1)} %get-tuple-element.84.early_ref, ...), custom_call_target="tpu_custom_call" | custom-call | tf_op jit(solution)/shard_map/middle/pallas_call | solution.py:1247
  198.4 105.6 %back.1 = (f32[3072,384]{1,0:T(8,128)}, f32[1024,384]{1,0:T(8,128)}, bf16[1024,384]{1,0:T(8,128)(2,1)}, bf16[16,144,384]{2,1,0:T(8,128)(2,1)}, f32[112,256]{1,0:T(8,128)}, /*index=5*/f32[240,384]{1,0:T(8,128)}) custom-call(bf16[3072,256]{1,0:T(8,128)(2,1)} %get-tuple-element.89.grad_context, bf16[3072,256]{1,0:T(8,128)(2,1)} %get-tuple-element.90.grad_conv_ref, ...), custom_call_target="tpu_custom_call" | custom-call | tf_op jit(solution)/shard_map/back/pallas_call | solution.py:1587
  304.0 0.0 copy-start.1
  304.0 31.0 %tail.1 = (f32[144,384]{1,0:T(8,128)}, f32[112,256]{1,0:T(8,128)}, f32[3072,384]{1,0:T(8,128)}) custom-call(bf16[16,144,384]{2,1,0:T(8,128)(2,1)} %get-tuple-element.109.in_ref, f32[112,256]{1,0:T(8,128)} %get-tuple-element.110.table_ref, f32[1024,384]{1,0:T(8,128)} %get-tuple-element.111.own_ref, ...), custom_call_target="tpu_custom_call", output_to_operand_aliasing={{2}: (4, {})} | custom-call | tf_op jit(solution)/shard_map/tail/pallas_call | solution.py:384
  335.0 2.1 final.1
  337.1 0.0 copy-done.1
  337.1 0.0 copy-start
  337.1 1.4 copy.53
  338.5 1.8 copy-done
  340.3 2.2 copy.54
Async XLA Ops:
  304.0 33.1 %copy-start.1 = (bf16[3072,384]{1,0:T(8,128)(2,1)S(1)}, bf16[3072,384]{1,0:T(8,128)(2,1)}, u32[]{:S(2)}) copy-start(bf16[3072,384]{1,0:T(8,128)(2,1)} %get-tuple-element.164) | copy-start | bytes 7077892
  337.1 3.2 copy-start

commit v6 on v5

--- a/solution.py
+++ b/solution.py
@@ -332,23 +332,29 @@
             piece_sum.at[pl.ds(i * rows, rows)], grad_ref.at[pl.ds(start + i * rows, rows)], store_sem.at[i]
         )
 
-    first = table_hop(table_ref, 0, me, 1 - mp)
+    shared = pl.ds(TABLE_OWN, TABLE_ROWS - TABLE_OWN)
+    first = pltpu.make_async_remote_copy(
+        src_ref=table_ref.at[shared],
+        dst_ref=table_in.at[0, shared],
+        send_sem=table_send.at[0],
+        recv_sem=table_recv.at[0],
+        device_id=at(me, 1 - mp),
+        device_id_type=MESH,
+    )
     first.start()
     hops.start_first()
     for i in range(PIECES):
         piece(i).start()
     first.wait_recv()
-    shared = pl.ds(TABLE_OWN, TABLE_ROWS - TABLE_OWN)
     table_out[0, :TABLE_OWN, :] = table_ref[:TABLE_OWN, :]
     table_out[0, shared, :] = table_ref[shared, :] + table_in[0, shared, :]
     second = table_hop(table_out.at[0], 1, twin, mp)
     second.start()
-    hops.start_second()
     second.wait_recv()
     table_out[1] = table_out[0] + table_in[1]
     third = table_hop(table_out.at[1], 2, beside, mp)
     third.start()
-    hops.start_third()
+    hops.start_second()
     third.wait_recv()
     table_out[2] = table_out[1] + table_in[2]
     fourth = [
@@ -356,6 +362,7 @@
     ]
     for copy in fourth:
         copy.start()
+    hops.start_third()
     for i in range(PIECES):
         piece(i).wait_recv()
         part = pl.ds(i * rows, rows)
@@ -505,9 +512,8 @@
 
 def spread_marks(marks_ref, columns_ref):
     rows = marks_ref.shape[2]
-    columns_ref[...] = jnp.transpose(
-        jnp.concatenate([marks_ref[0], jnp.zeros((LANES - TAP_ROWS, rows), F32)], 0)
-    )
+    wide = jnp.concatenate([marks_ref[0], jnp.zeros((LANES - TAP_ROWS, rows), F32)], 0)
+    columns_ref[...] = jnp.transpose(wide.astype(BF16)).astype(F32)
 
 
 def write_marks(lengths_ref, s, marks_ref):
@@ -584,7 +590,7 @@
     high = weights.astype(BF16).astype(F32)
     low = weights - high
     rest = jnp.zeros((LANES - 2 * heads * TAP_ROWS, weights.shape[1]), F32)
-    return jnp.transpose(jnp.concatenate([high, low, rest], 0)).astype(BF16)
+    return jnp.transpose(jnp.concatenate([high, low, rest], 0).astype(BF16))
 
 
 def front_kernel(
@@ -762,6 +768,10 @@
         for piece in range(PIECES // 2, PIECES):
             swap_part(s - 1, piece).start()
 
+    @pl.when(jnp.logical_and(s >= 1, s == early))
+    def _():
+        swap_part(s - 1, 1).start()
+
     own_terms = tap_terms[:tap_rows]
     k_ref[...] = nn(hidden, key_ref[...]).astype(BF16)
     v_ref[...] = (nn(hidden, value_ref[...]) + vec_ref[1:2, :]).astype(BF16)
@@ -788,7 +798,7 @@
             lse_ref[0, head : head + 1, part] = top + jnp.log(amount)
     lse_ref[0, heads:, :] = jnp.zeros((8 - heads, rows), F32)
     context_turned[heads * HEAD_DIM :, :] = jnp.zeros((WIDE - heads * HEAD_DIM, rows), F32)
-    ctx_ref[...] = jnp.transpose(context_turned[...]).astype(BF16)
+    ctx_ref[...] = jnp.transpose(context_turned[...].astype(BF16))
 
     @pl.when(s == 0)
     def _():
@@ -846,8 +856,11 @@
             return carry
 
         lax.fori_loop(0, jnp.where(s == early - 1, rows // 2 // block, rows // block), part_step, 0)
-        for piece in range(PIECES // 2):
-            swap_part(s, piece).start()
+        swap_part(s, 0).start()
+
+    @pl.when(s < early - 1)
+    def _():
+        swap_part(s, 1).start()
 
     @pl.when(s == min(1, seqs - 1))
     def _():
@@ -927,7 +940,7 @@
             pltpu.VMEM((tap_rows, LANES), F32),
             pltpu.VMEM((model, WIDE), F32),
             pltpu.VMEM((WIDE, WIDE), F32),
-            pltpu.VMEM((KERNEL, 64, LANES), F32),
+            pltpu.VMEM((KERNEL, 128, LANES), F32),
             pltpu.VMEM((model // LANES, rows + 2 * EDGE, LANES), F32),
             pltpu.VMEM((2, rows + 2 * EDGE, LANES), F32),
             pltpu.VMEM((rows, LANES), F32),
@@ -959,7 +972,7 @@
 
 def stat_columns(lines):
     rows = lines[0].shape[1]
-    wide = jnp.concatenate(lines + [jnp.zeros((LANES - len(lines), rows), F32)], 0)
+    wide = jnp.concatenate(lines + [jnp.zeros((8 - len(lines), rows), F32)], 0)
     tall = jnp.transpose(wide)
     return [tall[:, k : k + 1] for k in range(len(lines))]
 
@@ -971,7 +984,7 @@
 
 SLOTS = 4
 LAST_LAG = 6
-FFN_STEP = 256
+FFN_STEP = 512
 
 
 def middle_kernel(
@@ -1213,9 +1226,10 @@
             for slot in range(SLOTS):
                 message(kind, *kinds[kind], slot).wait_send()
         cut, cut_ffn = 2 * width // CUTS, hidden_units // CUTS
-        out_grads = jnp.transpose(jnp.concatenate([acc_out0[: width // 2], acc_out1[: width // 2]], 0)).astype(BF16)
-        inner_grads = jnp.transpose(acc_inner[...]).astype(BF16)
-        outer_grads = jnp.transpose(acc_outer[...]).astype(BF16)
+        both = jnp.concatenate([acc_out0[: width // 2], acc_out1[: width // 2]], 0)
+        out_grads = jnp.transpose(both.astype(BF16))
+        inner_grads = jnp.transpose(acc_inner[...].astype(BF16))
+        outer_grads = jnp.transpose(acc_outer[...].astype(BF16))
         for k in range(CUTS):
             part_ffn = slice(k * cut_ffn, (k + 1) * cut_ffn)
             pack_ref[k, pl.ds(0, cut), :] = out_grads[k * cut : (k + 1) * cut]
@@ -1448,9 +1462,9 @@
     every = tap_all[...]
     acc_tap[...] += nn(every.astype(BF16), ca_ref[...])
     acc_tap_bias[...] += sum(every[:, c * LANES : (c + 1) * LANES] for c in range(rows // LANES))
-    weights[...] = jnp.transpose(every).astype(BF16)
-
-    def key_step(i, carry):
+    weights[...] = jnp.transpose(every.astype(BF16))
+
+    def key_step(i, carry, block=512):
         base = pl.multiple_of(i * block, block)
         part = pl.ds(base, block)
         grad_attn = nn(weights[part, :], taps_ref[...]).astype(BF16).astype(F32)
@@ -1470,7 +1484,7 @@
             rows_total[c, part, :] = total[:, lanes]
         return carry
 
-    lax.fori_loop(0, rows // block, key_step, 0)
+    lax.fori_loop(0, rows // 512, key_step, 0)
     acc_point[...] += tn(grads[:, 4 * WIDE : 5 * WIDE], dl_ref[...])
     acc_in[...] += tn(hidden_ref[...], grads[:, : 4 * WIDE])
     step = masks.shape[1]
@@ -1534,7 +1548,7 @@
         group = model // 2
         cut = model // CUTS
         empty = jnp.zeros((cut, width), F32)
-        point_grad = jnp.transpose(acc_point[...])
+        point_grad = jnp.transpose(acc_point[...].astype(BF16)).astype(F32)
         for k in range(CUTS):
             part = pl.ds(k * cut, cut)
             for place in range(2):
@@ -1613,7 +1627,7 @@
         ]
         + hop_scratch(count, pack.shape[1], pack.shape[2])
         + [
-            vmem((KERNEL, 64, LANES), F32),
+            vmem((KERNEL, 128, LANES), F32),
             vmem((model // LANES, padded_rows, LANES), F32),
             vmem((2, padded_rows, LANES), F32),
             vmem((2, padded_rows, LANES), F32),

time: 344 us -> 354 us (1.029); the launches traced: 342 us -> 348 us
  Pallas kernels: 336 us -> 342 us
    pallas_call x1, Pallas kernels: 106 us -> 115 us  [back(): pl.pallas_call(functools.partial(back_kernel, seqs, count), grid=(seqs,),...]
where the time goes in v6:
time: 354 us; the launch traced here: 348 us
  Pallas kernels  342 us (97%)
  local copies, waits for them, and re-layouts  5.37 us (2%)
    pallas_call x1, Pallas kernels, back(): pl.pallas_call(functools.partial(back_kernel, seqs, count), grid=(seqs,),...  115 us
    pallas_call x1, Pallas kernels, middle(): pl.pallas_call(functools.partial(middle_kernel, blocks, early), grid=(blo...  99.7 us
    pallas_call x1, Pallas kernels, front(): pl.pallas_call(functools.partial(front_kernel, seqs, count, early), grid=...  73.2 us
    pallas_call x1, Pallas kernels, tail(): pl.pallas_call(functools.partial(tail_kernel, count, start), out_shape=(j...  30.8 us
    pallas_call x1, Pallas kernels, gather_first(): pl.pallas_call(functools.partial(pack_kernel, count), out_shape=(jax.Shap...  21.3 us

profile of v6, /device:TPU:8, one launch (start us, length us, event | category | flops | bytes accessed | tf_op | source)
XLA Modules:
  0.0 348.2 jit_solution(10248127348896725573)
XLA Ops:
  0.7 21.3 %weight_gather.1 = (bf16[16,144,384]{2,1,0:T(8,128)(2,1)}, bf16[1,240,384]{2,1,0:T(8,128)(2,1)}) custom-call(bf16[48,192]{1,0:T(8,128)(2,1)} %q_ref.1, bf16[48,192]{1,0:T(8,128)(2,1)} %k_ref.1, bf16[48,192]{1,0:T(8,128)(2,1)} %v_ref.1, bf16[48,192]{1,0:T(8,128)(2,1)} %c_ref.1, bf16[48,192]{1,0:T(8,128)(2,1)} %p_ref.1, bf16[9,48]{1,0:T(8,128)(2,1)} %depth_ref.1, ...), custom_call_target="tpu_custom_call" | custom-call | tf_op jit(solution)/shard_map/weight_gather/pallas_call | solution.py:145
  22.0 73.2 %front.1 = (bf16[3072,256]{1,0:T(8,128)(2,1)}, bf16[3072,256]{1,0:T(8,128)(2,1)}, bf16[3072,256]{1,0:T(8,128)(2,1)}, f32[3072,256]{1,0:T(8,128)}, bf16[3072,768]...) custom-call(bf16[3072,768]{1,0:T(8,128)(2,1)} %hidden_any.1, ...), custom_call_target="tpu_custom_call" | custom-call | tf_op jit(solution)/shard_map/front/pallas_call | solution.py:902
  95.2 99.7 %middle.1 = (bf16[3072,384]{1,0:T(8,128)(2,1)}, f32[3072,384]{1,0:T(8,128)}, bf16[3072,256]{1,0:T(8,128)(2,1)}, bf16[3072,256]{1,0:T(8,128)(2,1)}, bf16[16,240,384]{2,1,0:T(8,128)(2,1)}, /*index=5*/f32[8,1536]{1,0:T(8,128)}) custom-call(bf16[3072,384]{1,0:T(8,128)(2,1)} %get-tuple-element.84.early_ref, ...), custom_call_target="tpu_custom_call" | custom-call | tf_op jit(solution)/shard_map/middle/pallas_call | solution.py:1261
  194.9 114.8 %back.1 = (f32[3072,384]{1,0:T(8,128)}, f32[1024,384]{1,0:T(8,128)}, bf16[1024,384]{1,0:T(8,128)(2,1)}, bf16[16,144,384]{2,1,0:T(8,128)(2,1)}, f32[112,256]{1,0:T(8,128)}, /*index=5*/f32[240,384]{1,0:T(8,128)}) custom-call(bf16[3072,256]{1,0:T(8,128)(2,1)} %get-tuple-element.89.grad_context, bf16[3072,256]{1,0:T(8,128)(2,1)} %get-tuple-element.90.grad_conv_ref, ...), custom_call_target="tpu_custom_call" | custom-call | tf_op jit(solution)/shard_map/back/pallas_call | solution.py:1601
  309.7 0.0 copy-start.1
  309.8 30.8 %tail.1 = (f32[144,384]{1,0:T(8,128)}, f32[112,256]{1,0:T(8,128)}, f32[3072,384]{1,0:T(8,128)}) custom-call(bf16[16,144,384]{2,1,0:T(8,128)(2,1)} %get-tuple-element.109.in_ref, f32[112,256]{1,0:T(8,128)} %get-tuple-element.110.table_ref, f32[1024,384]{1,0:T(8,128)} %get-tuple-element.111.own_ref, ...), custom_call_target="tpu_custom_call", output_to_operand_aliasing={{2}: (4, {})} | custom-call | tf_op jit(solution)/shard_map/tail/pallas_call | solution.py:391
  340.6 2.1 final.1
  342.7 0.0 copy-done.1
  342.7 0.0 copy-start
  342.7 1.4 copy.53
  344.1 1.8 copy-done
  345.9 2.2 copy.54
Async XLA Ops:
  309.7 32.9 %copy-start.1 = (bf16[3072,384]{1,0:T(8,128)(2,1)S(1)}, bf16[3072,384]{1,0:T(8,128)(2,1)}, u32[]{:S(2)}) copy-start(bf16[3072,384]{1,0:T(8,128)(2,1)} %get-tuple-element.164) | copy-start | bytes 7077892
  342.7 3.2 copy-start

commit v7 on v6

--- a/solution.py
+++ b/solution.py
@@ -940,7 +940,7 @@
             pltpu.VMEM((tap_rows, LANES), F32),
             pltpu.VMEM((model, WIDE), F32),
             pltpu.VMEM((WIDE, WIDE), F32),
-            pltpu.VMEM((KERNEL, 128, LANES), F32),
+            pltpu.VMEM((KERNEL, 64, LANES), F32),
             pltpu.VMEM((model // LANES, rows + 2 * EDGE, LANES), F32),
             pltpu.VMEM((2, rows + 2 * EDGE, LANES), F32),
             pltpu.VMEM((rows, LANES), F32),
@@ -1464,7 +1464,7 @@
     acc_tap_bias[...] += sum(every[:, c * LANES : (c + 1) * LANES] for c in range(rows // LANES))
     weights[...] = jnp.transpose(every.astype(BF16))
 
-    def key_step(i, carry, block=512):
+    def key_step(i, carry):
         base = pl.multiple_of(i * block, block)
         part = pl.ds(base, block)
         grad_attn = nn(weights[part, :], taps_ref[...]).astype(BF16).astype(F32)
@@ -1484,7 +1484,7 @@
             rows_total[c, part, :] = total[:, lanes]
         return carry
 
-    lax.fori_loop(0, rows // 512, key_step, 0)
+    lax.fori_loop(0, rows // block, key_step, 0)
     acc_point[...] += tn(grads[:, 4 * WIDE : 5 * WIDE], dl_ref[...])
     acc_in[...] += tn(hidden_ref[...], grads[:, : 4 * WIDE])
     step = masks.shape[1]
@@ -1627,7 +1627,7 @@
         ]
         + hop_scratch(count, pack.shape[1], pack.shape[2])
         + [
-            vmem((KERNEL, 128, LANES), F32),
+            vmem((KERNEL, 64, LANES), F32),
             vmem((model // LANES, padded_rows, LANES), F32),
             vmem((2, padded_rows, LANES), F32),
             vmem((2, padded_rows, LANES), F32),

time: 354 us -> 342 us (0.966)
  Pallas kernels: 342 us -> 333 us
    pallas_call x1, Pallas kernels: 115 us -> 105 us  [back(): pl.pallas_call(functools.partial(back_kernel, seqs, count), grid=(seqs,),...]
where the time goes in v7:
time: 342 us; the launch traced here: 339 us
  Pallas kernels  333 us (97%)
  local copies, waits for them, and re-layouts  5.37 us (2%)
    pallas_call x1, Pallas kernels, back(): pl.pallas_call(functools.partial(back_kernel, seqs, count), grid=(seqs,),...  105 us
    pallas_call x1, Pallas kernels, middle(): pl.pallas_call(functools.partial(middle_kernel, blocks, early), grid=(blo...  99.6 us
    pallas_call x1, Pallas kernels, front(): pl.pallas_call(functools.partial(front_kernel, seqs, count, early), grid=...  73.2 us
    pallas_call x1, Pallas kernels, tail(): pl.pallas_call(functools.partial(tail_kernel, count, start), out_shape=(j...  31.7 us
    pallas_call x1, Pallas kernels, gather_first(): pl.pallas_call(functools.partial(pack_kernel, count), out_shape=(jax.Shap...  21.3 us

profile of v7, /device:TPU:8, one launch (start us, length us, event | category | flops | bytes accessed | tf_op | source)
XLA Modules:
  0.0 339.3 jit_solution(4302965736324582847)
XLA Ops:
  0.7 21.3 %weight_gather.1 = (bf16[16,144,384]{2,1,0:T(8,128)(2,1)}, bf16[1,240,384]{2,1,0:T(8,128)(2,1)}) custom-call(bf16[48,192]{1,0:T(8,128)(2,1)} %q_ref.1, bf16[48,192]{1,0:T(8,128)(2,1)} %k_ref.1, bf16[48,192]{1,0:T(8,128)(2,1)} %v_ref.1, bf16[48,192]{1,0:T(8,128)(2,1)} %c_ref.1, bf16[48,192]{1,0:T(8,128)(2,1)} %p_ref.1, bf16[9,48]{1,0:T(8,128)(2,1)} %depth_ref.1, ...), custom_call_target="tpu_custom_call" | custom-call | tf_op jit(solution)/shard_map/weight_gather/pallas_call | solution.py:145
  22.0 73.2 %front.1 = (bf16[3072,256]{1,0:T(8,128)(2,1)}, bf16[3072,256]{1,0:T(8,128)(2,1)}, bf16[3072,256]{1,0:T(8,128)(2,1)}, f32[3072,256]{1,0:T(8,128)}, bf16[3072,768]...) custom-call(bf16[3072,768]{1,0:T(8,128)(2,1)} %hidden_any.1, ...), custom_call_target="tpu_custom_call" | custom-call | tf_op jit(solution)/shard_map/front/pallas_call | solution.py:902
  95.2 99.6 %middle.1 = (bf16[3072,384]{1,0:T(8,128)(2,1)}, f32[3072,384]{1,0:T(8,128)}, bf16[3072,256]{1,0:T(8,128)(2,1)}, bf16[3072,256]{1,0:T(8,128)(2,1)}, bf16[16,240,384]{2,1,0:T(8,128)(2,1)}, /*index=5*/f32[8,1536]{1,0:T(8,128)}) custom-call(bf16[3072,384]{1,0:T(8,128)(2,1)} %get-tuple-element.84.early_ref, ...), custom_call_target="tpu_custom_call" | custom-call | tf_op jit(solution)/shard_map/middle/pallas_call | solution.py:1261
  194.8 105.4 %back.1 = (f32[3072,384]{1,0:T(8,128)}, f32[1024,384]{1,0:T(8,128)}, bf16[1024,384]{1,0:T(8,128)(2,1)}, bf16[16,144,384]{2,1,0:T(8,128)(2,1)}, f32[112,256]{1,0:T(8,128)}, /*index=5*/f32[240,384]{1,0:T(8,128)}) custom-call(bf16[3072,256]{1,0:T(8,128)(2,1)} %get-tuple-element.89.grad_context, bf16[3072,256]{1,0:T(8,128)(2,1)} %get-tuple-element.90.grad_conv_ref, ...), custom_call_target="tpu_custom_call" | custom-call | tf_op jit(solution)/shard_map/back/pallas_call | solution.py:1601
  300.1 0.0 copy-start.1
  300.1 31.7 %tail.1 = (f32[144,384]{1,0:T(8,128)}, f32[112,256]{1,0:T(8,128)}, f32[3072,384]{1,0:T(8,128)}) custom-call(bf16[16,144,384]{2,1,0:T(8,128)(2,1)} %get-tuple-element.109.in_ref, f32[112,256]{1,0:T(8,128)} %get-tuple-element.110.table_ref, f32[1024,384]{1,0:T(8,128)} %get-tuple-element.111.own_ref, ...), custom_call_target="tpu_custom_call", output_to_operand_aliasing={{2}: (4, {})} | custom-call | tf_op jit(solution)/shard_map/tail/pallas_call | solution.py:391
  331.8 2.1 final.1
  333.9 0.0 copy-done.1
  333.9 0.0 copy-start
  333.9 1.4 copy.53
  335.3 1.8 copy-done
  337.1 2.2 copy.54
Async XLA Ops:
  300.1 33.8 %copy-start.1 = (bf16[3072,384]{1,0:T(8,128)(2,1)S(1)}, bf16[3072,384]{1,0:T(8,128)(2,1)}, u32[]{:S(2)}) copy-start(bf16[3072,384]{1,0:T(8,128)(2,1)} %get-tuple-element.164) | copy-start | bytes 7077892
  333.9 3.2 copy-start
